TPU v7x, 512 devices: a whole 4x8x8 slice. The times are simulated.
512 devices in a mesh: dp: 8 (over y), expert: 64 (over x, z, core).
Axes of the slice: x: 4, y: 8, z: 8, core: 2. Of those that a mesh axis runs over, the one named last changes fastest.
Arguments:
- tokens: bfloat16 [65536, 2048], P(('dp', 'expert')), may hold values from -6 to 6
- out_grad: bfloat16 [65536, 2048], P(('dp', 'expert')), may hold values from -6 to 6
- expert_ids: int32 [65536, 6], P(('dp', 'expert')), may hold values from 0 to 63, all different within a row; in each aligned block of 128 rows (0 to 127, 128 to 255, ...) at most 14 rows name the same one
- route_weights: bfloat16 [65536, 6], P(('dp', 'expert')), may hold values from 0.019897461 to 0.5
- blocks: bfloat16 [64, 3, 12, 128, 128], P('expert'), may hold values from -0.5 to 0.5
- layout: int32 [64, 3, 12, 2], P('expert'), may hold values from 0 to 15, as said below
- moments: float32 [64, 3, 12, 128, 128], P('expert', None, None, 'dp'), may hold values from -12 to 12
- partner: int32 [64], replicated, may hold values from 0 to 63, as said below
Outputs:
- token_grad: bfloat16 [65536, 2048], P(('dp', 'expert'))
- route_grad: bfloat16 [65536, 6], P(('dp', 'expert'))
- new_blocks: bfloat16 [64, 3, 12, 128, 128], P('expert')
- new_moments: float32 [64, 3, 12, 128, 128], P('expert', None, None, 'dp')
Inputs may be any that keep to these rules, and one draw needn't show every extreme that they name: `layout`: within one expert and matrix the stored blocks are at distinct places; for gate and up an entry is (block of the 2048 features, block of the 1408 hidden units), for down (block of the hidden units, block of the features). partner pairs the experts: partner[partner[e]] == e and partner[e] != e. `expert_ids`: each row names 6 different experts; among the rows of one device no expert is named more than 14 times, a bound that some block reaches.
All inputs are finite; a program needn't handle non-finite values.
Results may differ from a plain program's by a relative error of at most 0.0064.
Values may be sent and summed in bfloat16 or wider, within the bound.
A program may use at most 128 MiB of HBM per device.

v0:
```python
import jax
import jax.numpy as jnp
from jax import lax
from jax.sharding import PartitionSpec as P

HID = 1408


momentum_decay = 0.9
step_rate = 0.01


def block_product(left, mats, source_idx, target_idx, target_count, flipped):
    row_count = left.shape[0]
    block_size = mats.shape[-1]
    pieces = jnp.take(left.reshape(row_count, -1, block_size), source_idx, axis=1)
    if flipped:
        partial_out = jnp.einsum("rbk,bnk->rbn", pieces, mats, preferred_element_type=jnp.float32)
    else:
        partial_out = jnp.einsum("rbk,bkn->rbn", pieces, mats, preferred_element_type=jnp.float32)
    select = (target_idx[:, None] == jnp.arange(target_count, dtype=jnp.int32)[None, :]).astype(
        jnp.float32
    )
    placed = jnp.einsum("rbn,bc->rcn", partial_out, select, precision=lax.Precision.HIGHEST)
    return placed.reshape(row_count, target_count * block_size)


def block_outer(left, right, left_idx, right_idx, block_size):
    row_count = left.shape[0]
    left_pieces = jnp.take(left.reshape(row_count, -1, block_size), left_idx, axis=1)
    right_pieces = jnp.take(right.reshape(row_count, -1, block_size), right_idx, axis=1)
    return jnp.einsum("rbk,rbn->bkn", left_pieces, right_pieces, preferred_element_type=jnp.float32)


def expert_forward(inputs, matrices, layout_one, hidden_blocks, feat_blocks):
    gate_pre = block_product(
        inputs, matrices[0], layout_one[0, :, 0], layout_one[0, :, 1], hidden_blocks, False
    )
    up_pre = block_product(
        inputs, matrices[1], layout_one[1, :, 0], layout_one[1, :, 1], hidden_blocks, False
    )
    sigmoid_gate = jax.nn.sigmoid(gate_pre)
    activated = gate_pre * sigmoid_gate
    hidden = (activated * up_pre).astype(jnp.bfloat16)
    output = block_product(
        hidden, matrices[2], layout_one[2, :, 0], layout_one[2, :, 1], feat_blocks, False
    )
    return (gate_pre, up_pre, sigmoid_gate, activated, hidden, output)


def expert_backward(
    inputs, upstream, weights_col, matrices, layout_one, hidden_blocks, feat_blocks, saved
):
    gate_pre, up_pre, sigmoid_gate, activated, hidden, output = saved
    score = jnp.sum(output * upstream.astype(jnp.float32), axis=1).astype(jnp.bfloat16)
    scaled = (weights_col.astype(jnp.float32)[:, None] * upstream.astype(jnp.float32)).astype(
        jnp.bfloat16
    )
    hidden_grad = block_product(
        scaled, matrices[2], layout_one[2, :, 1], layout_one[2, :, 0], hidden_blocks, True
    )
    gate_grad = (
        hidden_grad * up_pre * sigmoid_gate * (1.0 + gate_pre * (1.0 - sigmoid_gate))
    ).astype(jnp.bfloat16)
    up_grad = (hidden_grad * activated).astype(jnp.bfloat16)
    input_grad = (
        block_product(
            gate_grad, matrices[0], layout_one[0, :, 1], layout_one[0, :, 0], feat_blocks, True
        )
        + block_product(
            up_grad, matrices[1], layout_one[1, :, 1], layout_one[1, :, 0], feat_blocks, True
        )
    ).astype(jnp.bfloat16)
    block_size = matrices.shape[-1]
    weight_grad = jnp.stack(
        [
            block_outer(inputs, gate_grad, layout_one[0, :, 0], layout_one[0, :, 1], block_size),
            block_outer(inputs, up_grad, layout_one[1, :, 0], layout_one[1, :, 1], block_size),
            block_outer(hidden, scaled, layout_one[2, :, 0], layout_one[2, :, 1], block_size),
        ]
    )
    return (score, input_grad, weight_grad)


def relocate(first_state, second_state, partner, expert_count):
    spread = (
        lax.all_to_all(
            first_state.reshape(expert_count, -1), "expert", split_axis=0, concat_axis=0, tiled=True
        ),
        lax.all_to_all(
            second_state.reshape(expert_count, -1),
            "expert",
            split_axis=0,
            concat_axis=0,
            tiled=True,
        ),
    )
    first_moved = jnp.take(spread[0], partner, axis=0)
    second_moved = jnp.take(spread[1], partner, axis=0)
    collected = (
        lax.all_to_all(first_moved, "expert", split_axis=0, concat_axis=0, tiled=True),
        lax.all_to_all(second_moved, "expert", split_axis=0, concat_axis=0, tiled=True),
    )
    return (collected[0].reshape(first_state.shape), collected[1].reshape(second_state.shape))


def body(tokens, out_grad, expert_ids, route_weights, blocks, layout, moments, partner):
    expert_count = lax.axis_size("expert")
    replica_count = lax.axis_size("dp")
    tok_count, topk_count = expert_ids.shape
    width = tokens.shape[1]
    block_size = blocks.shape[-1]
    capacity = max(2, tok_count * topk_count * 7 // (expert_count * 6))
    pick_count = tok_count * topk_count
    feat_blocks = width // block_size
    hidden_blocks = HID // block_size
    flat_ids = expert_ids.reshape(-1)
    onehot = (flat_ids[:, None] == jnp.arange(expert_count, dtype=jnp.int32)[None, :]).astype(
        jnp.int32
    )
    before = jnp.cumsum(onehot, axis=0) - onehot
    rank_within = jnp.sum(before * onehot, axis=1)
    slot_of = flat_ids * capacity + rank_within
    slot_pick = (
        jnp.full((expert_count * capacity,), pick_count, jnp.int32)
        .at[slot_of]
        .set(jnp.arange(pick_count, dtype=jnp.int32))
    )
    filled = slot_pick < pick_count
    safe_pick = jnp.minimum(slot_pick, pick_count - 1)
    token_of = safe_pick // topk_count
    send_tokens = jnp.where(filled[:, None], tokens[token_of], jnp.zeros((), tokens.dtype))
    send_grads = jnp.where(filled[:, None], out_grad[token_of], jnp.zeros((), out_grad.dtype))
    send_weights = jnp.where(
        filled, route_weights.reshape(-1)[safe_pick], jnp.zeros((), route_weights.dtype)
    )
    matrices = blocks[0]
    layout_one = layout[0]
    recv_tokens = lax.all_to_all(send_tokens, "expert", split_axis=0, concat_axis=0, tiled=True)
    saved = expert_forward(recv_tokens, matrices, layout_one, hidden_blocks, feat_blocks)
    recv_grads, recv_weights = (
        lax.all_to_all(send_grads, "expert", split_axis=0, concat_axis=0, tiled=True),
        lax.all_to_all(send_weights, "expert", split_axis=0, concat_axis=0, tiled=True),
    )
    score, input_grad, weight_grad = expert_backward(
        recv_tokens,
        recv_grads,
        recv_weights,
        matrices,
        layout_one,
        hidden_blocks,
        feat_blocks,
        saved,
    )
    back_grad, back_score = (
        lax.all_to_all(input_grad, "expert", split_axis=0, concat_axis=0, tiled=True),
        lax.all_to_all(score, "expert", split_axis=0, concat_axis=0, tiled=True),
    )
    per_pick = back_grad[slot_of].reshape(tok_count, topk_count, width)
    token_grad = jnp.sum(per_pick.astype(jnp.float32), axis=1).astype(jnp.bfloat16)
    route_grad = back_score[slot_of].reshape(tok_count, topk_count)
    shard_grad = lax.psum_scatter(weight_grad, "dp", scatter_dimension=2, tiled=True)
    row_share = block_size // replica_count
    own_rows = lax.dynamic_slice_in_dim(matrices, lax.axis_index("dp") * row_share, row_share, 2)
    new_moment = momentum_decay * moments[0] + shard_grad
    new_shard = (own_rows.astype(jnp.float32) - step_rate * new_moment).astype(jnp.bfloat16)
    moved_shard, moved_moment = relocate(
        new_shard.astype(jnp.float32), new_moment, partner, expert_count
    )
    outgoing = moved_shard.astype(jnp.bfloat16)
    gathered = lax.all_gather(outgoing, "dp", axis=2, tiled=True)
    return (token_grad, route_grad, gathered[None], moved_moment[None])


def solution(mesh):
    placed = (
        P(("dp", "expert"), None),
        P(("dp", "expert"), None),
        P(("dp", "expert"), None),
        P(("dp", "expert"), None),
        P("expert", None, None, None, None),
        P("expert", None, None, None),
        P("expert", None, None, "dp", None),
        P(),
    )
    return jax.shard_map(
        body,
        mesh=mesh,
        in_specs=placed,
        out_specs=(
            P(("dp", "expert"), None),
            P(("dp", "expert"), None),
            P("expert", None, None, None, None),
            P("expert", None, None, "dp", None),
        ),
        check_vma=False,
    )
```

profile of v0, /device:TPU:1, one launch (start us, length us, event | category | flops | bytes accessed | tf_op | source)
XLA Modules:
  0.0 651.9 jit_solution(4007502249218607038)
XLA Ops:
  11.6 3.4 scatter_custom_fusion
  15.9 5.8 gather_fusion
  22.5 14.8 %all-to-all-start = ((bf16[64,14,1]{1,2,0:T(2,128)(2,1)}), bf16[64,14,1]{1,2,0:T(2,128)(2,1)S(1)}, u32[]{:S(2)}, u32[]{:S(2)}) async-start(bf16[64,14,1]{1,2,0:T(2,128)(2,1)} %all_to_all.76), calls=%async_computation | async-start | bytes 65536 | tf_op jit(solution)/shard_map/all_to_all | solution.py:143
  37.5 5.0 gather_fusion.1
  42.5 6.0 gather.30
  48.6 5.0 gather_fusion.2
  53.6 6.0 gather.32
  59.6 5.8 broadcast_select_fusion
  65.4 106.6 %all_to_all.87 = bf16[64,14,2048]{2,1,0:T(8,128)(2,1)} all-to-all(bf16[64,14,2048]{2,1,0:T(8,128)(2,1)} %get-tuple-element.42), channel_id=1, replica_groups=mesh['dp'=8,'expert'=64] {'expert'}, dimensions={0} | all-to-all | bytes 7340032 | tf_op jit(solution)/shard_map/all_to_all | solution.py:139
  172.0 6.1 all-to-all-start.1
  178.8 7.4 %reshape.188 = bf16[896,16,128]{2,1,0:T(8,128)(2,1)} reshape(bf16[64,14,2048]{2,1,0:T(8,128)(2,1)} %all_to_all.87) | data formatting | bytes 7340032 | tf_op jit(solution)/shard_map/reshape | solution.py:16
  186.2 4.8 copy.94
  191.0 4.6 gather_fusion.7
  195.5 3.1 gather_fusion.6
  198.7 75.4 %all-to-all-done.1 = bf16[64,14,2048]{2,1,0:T(8,128)(2,1)} async-done(((bf16[64,14,2048]{2,1,0:T(8,128)(2,1)}), bf16[64,14,2048]{2,1,0:T(8,128)(2,1)}, u32[]{:S(2)}, u32[]{:S(2)}) %all-to-all-start.1) | async-done | bytes 3670048 | tf_op jit(solution)/shard_map/all_to_all | solution.py:142
  274.1 8.1 %reshape.192 = f32[896,16,128]{2,1,0:T(8,128)} reshape(bf16[64,14,2048]{2,1,0:T(8,128)(2,1)} %all-to-all-done.1) | data formatting | bytes 11010048 | tf_op jit(solution)/shard_map/convert_element_type | solution.py:56
  282.2 7.3 %fusion.13 = bf16[896,16,128]{2,0,1:T(8,128)(2,1)} fusion(f32[896,16,128]{2,1,0:T(8,128)} %reshape.192, f32[896]{0:T(1024)S(1)} %reshape.191), kind=kLoop, calls=%fused_computation.29 | loop fusion | flops 3670016 | bytes 11013632 | tf_op jit(solution)/shard_map/convert_element_type | solution.py:56
  289.5 4.6 gather_fusion.5
  296.8 6.8 %fusion.11 = f32[11,896,128]{2,0,1:T(8,128)S(1)} fusion(f32[896,12,128]{2,0,1:T(8,128)S(1)} %fusion.47, s32[12]{0:T(128)S(1)} %get-tuple-element.50), kind=kOutput, calls=%fused_computation.26 | convolution fusion | flops 181665920 | bytes 10551344 | tf_op jit(solution)/shard_map/rbn,bc->rcn/dot_general | solution.py:24
  304.6 15.5 %fusion.7 = f32[11,896,128]{2,0,1:T(8,128)S(1)} fusion(f32[896,12,128]{2,0,1:T(8,128)S(1)} %fusion.53, s32[12]{0:T(128)S(1)} %get-tuple-element.47), kind=kOutput, calls=%fused_computation.22 | convolution fusion | flops 181665920 | bytes 10551344 | tf_op jit(solution)/shard_map/rbn,bc->rcn/dot_general | solution.py:24
  321.0 7.0 %fusion.9 = f32[11,896,128]{2,0,1:T(8,128)S(1)} fusion(f32[896,12,128]{2,0,1:T(8,128)S(1)} %fusion.50, s32[12]{0:T(128)S(1)} %get-tuple-element.49), kind=kOutput, calls=%fused_computation.24 | convolution fusion | flops 181665920 | bytes 10551344 | tf_op jit(solution)/shard_map/rbn,bc->rcn/dot_general | solution.py:24
  328.0 6.4 fusion.21
  334.5 4.2 gather_fusion.10
  338.7 4.8 fusion.77
  346.0 4.8 fusion.67
  353.4 3.9 fusion.72
  361.9 19.3 %fusion = bf16[896]{0:T(1024)(128)(2,1)S(1)} fusion(f32[896,16,128]{2,1,0:T(8,128)} %reshape.192, f32[896,12,128]{2,0,1:T(8,128)S(1)} %fusion.62, s32[12]{0:T(128)S(1)} %get-tuple-element.46), kind=kOutput, calls=%fused_computation.15 | convolution fusion | flops 267910464 | bytes 12846896 | tf_op jit(solution)/shard_map/rbn,bc->rcn/dot_general | solution.py:24
  382.0 4.4 fusion.59
  386.4 10.7 %reduce-scatter.2.cloned.1.call-done = f32[3,12,16,128]{3,2,1,0:T(8,128)} async-done(((f32[3,12,128,128]{3,2,1,0:T(8,128)}), f32[3,12,16,128]{3,2,1,0:T(8,128)}) %reduce-scatter.2.cloned.1.call-update) | async-done | bytes 294928 | tf_op jit(solution)/shard_map/reduce_scatter | solution.py:162
  402.0 14.9 %all-to-all-start.5 = ((bf16[64,2,576]{2,1,0:T(2,128)(2,1)}), bf16[64,2,576]{2,1,0:T(2,128)(2,1)S(1)}, u32[]{:S(2)}, u32[]{:S(2)}) async-start(bf16[64,2,576]{2,1,0:T(2,128)(2,1)} %reshape.353), calls=%async_computation.6 | async-start | bytes 327680 | tf_op jit(solution)/shard_map/all_to_all | solution.py:87
  417.0 4.3 fusion.56
  421.2 6.3 all-to-all-done.5
  427.5 5.5 all-to-all-start.7
  433.1 12.0 %fusion.3 = f32[16,896,128]{2,0,1:T(8,128)} fusion(f32[896,12,128]{2,0,1:T(8,128)} %fusion.59, s32[12]{0:T(128)S(1)} %get-tuple-element.48), kind=kOutput, calls=%fused_computation.18 | convolution fusion | flops 264241344 | bytes 12845104 | tf_op jit(solution)/shard_map/rbn,bc->rcn/dot_general | solution.py:24
  446.1 10.3 %all-to-all-start.4 = ((bf16[64,14,1]{1,2,0:T(2,128)(2,1)}), bf16[64,14,1]{1,2,0:T(2,128)(2,1)S(1)}, u32[]{:S(2)}, u32[]{:S(2)}) async-start(bf16[64,14,1]{1,2,0:T(2,128)(2,1)} %convert_element_type.112), calls=%async_computation.4 | async-start | bytes 65536 | tf_op jit(solution)/shard_map/all_to_all | solution.py:157
  458.8 6.8 %all-to-all-done.4 = bf16[64,14,1]{1,2,0:T(2,128)(2,1)S(1)} async-done(((bf16[64,14,1]{1,2,0:T(2,128)(2,1)}), bf16[64,14,1]{1,2,0:T(2,128)(2,1)S(1)}, u32[]{:S(2)}, u32[]{:S(2)}) %all-to-all-start.4) | async-done | bytes 1824 | tf_op jit(solution)/shard_map/all_to_all | solution.py:157
  465.6 4.7 all-to-all-start.6
  471.5 9.6 %all-to-all-done.6 = bf16[64,2,576]{2,1,0:T(2,128)(2,1)S(1)} async-done(((bf16[64,2,576]{2,1,0:T(2,128)(2,1)}), bf16[64,2,576]{2,1,0:T(2,128)(2,1)S(1)}, u32[]{:S(2)}, u32[]{:S(2)}) %all-to-all-start.6) | async-done | bytes 147488 | tf_op jit(solution)/shard_map/all_to_all | solution.py:101
  481.0 5.7 all-to-all-start.8
  486.7 13.4 %fusion.23 = bf16[896,16,128]{2,1,0:T(8,128)(2,1)} fusion(f32[16,896,128]{2,0,1:T(8,128)} %fusion.3, f32[896,12,128]{2,0,1:T(8,128)} %fusion.56, s32[12]{0:T(128)S(1)} %get-tuple-element.51), kind=kOutput, calls=%fused_computation.48 | convolution fusion | flops 267911360 | bytes 16515120 | tf_op jit(solution)/shard_map/rbn,bc->rcn/dot_general | solution.py:24
  500.2 7.3 %convert_element_type.100 = bf16[64,14,2048]{2,1,0:T(8,128)(2,1)} reshape(bf16[896,16,128]{2,1,0:T(8,128)(2,1)} %fusion.23) | data formatting | bytes 7340032 | tf_op jit(solution)/shard_map/convert_element_type | solution.py:73
  507.5 10.5 %all-to-all-start.3 = ((bf16[64,14,2048]{2,1,0:T(8,128)(2,1)}), bf16[64,14,2048]{2,1,0:T(8,128)(2,1)}, u32[]{:S(2)}, u32[]{:S(2)}) async-start(bf16[64,14,2048]{2,1,0:T(8,128)(2,1)} %convert_element_type.100), calls=%async_computation.3 | async-start | bytes 8388608 | tf_op jit(solution)/shard_map/all_to_all | solution.py:156
  520.5 5.0 gather_fusion.4
  526.3 87.6 %all-to-all-done.3 = bf16[64,14,2048]{2,1,0:T(8,128)(2,1)} async-done(((bf16[64,14,2048]{2,1,0:T(8,128)(2,1)}), bf16[64,14,2048]{2,1,0:T(8,128)(2,1)}, u32[]{:S(2)}, u32[]{:S(2)}) %all-to-all-start.3) | async-done | bytes 3670048 | tf_op jit(solution)/shard_map/all_to_all | solution.py:156
  613.9 6.0 all_to_all.61
  619.9 9.6 %gather_fusion.3 = bf16[768,2048]{1,0:T(8,128)(2,1)} fusion(bf16[896,2048]{1,0:T(8,128)(2,1)} %all_to_all.61, s32[1024]{0:T(1024)S(1)} %pad_clamp_fusion.2), kind=kCustom, calls=%fused_computation.11 | custom fusion | bytes 6294528 | tf_op jit(solution)/shard_map/gather | solution.py:159
  629.5 6.3 reshape.189
  635.8 5.7 reduce_sum.34
  (103 shorter events, 37.6 us)
Async XLA Ops:
  7.2 30.4 %copy-start = (bf16[128,2048]{1,0:T(8,128)(2,1)S(1)}, bf16[128,2048]{1,0:T(8,128)(2,1)}, u32[]{:S(2)}) copy-start(bf16[128,2048]{1,0:T(8,128)(2,1)} %param.15) | copy-start | bytes 1572868
  22.5 42.9 %all-to-all-start = ((bf16[64,14,1]{1,2,0:T(2,128)(2,1)}), bf16[64,14,1]{1,2,0:T(2,128)(2,1)S(1)}, u32[]{:S(2)}, u32[]{:S(2)}) async-start(bf16[64,14,1]{1,2,0:T(2,128)(2,1)} %all_to_all.76), calls=%async_computation | async-start | bytes 65536 | tf_op jit(solution)/shard_map/all_to_all | solution.py:143
  42.5 6.0 copy-start.2
  172.0 6.5 copy-start.14
  172.0 102.0 %all-to-all-start.1 = ((bf16[64,14,2048]{2,1,0:T(8,128)(2,1)}), bf16[64,14,2048]{2,1,0:T(8,128)(2,1)}, u32[]{:S(2)}, u32[]{:S(2)}) async-start(bf16[64,14,2048]{2,1,0:T(8,128)(2,1)} %get-tuple-element.43), calls=%async_computation.1 | async-start | bytes 8388608 | tf_op jit(solution)/shard_map/all_to_all | solution.py:142
  178.2 219.0 %reduce-scatter.2.cloned.1.call-start = ((), (), s32[]{:S(2)}) async-start(), calls=%async_computation.10 | async-start | bytes 2654208 | tf_op jit(solution)/shard_map/reduce_scatter | solution.py:162
  198.7 121.4 %copy-start.7 = (bf16[12,896,128]{2,1,0:T(8,128)(2,1)}, bf16[12,896,128]{2,1,0:T(8,128)(2,1)S(1)}, u32[]{:S(2)}) copy-start(bf16[12,896,128]{2,1,0:T(8,128)(2,1)S(1)} %gather_fusion.6) | copy-start | bytes 8257540
  296.8 6.8 %copy-start.9 = (bf16[12,896,128]{2,1,0:T(8,128)(2,1)S(1)}, bf16[12,896,128]{2,1,0:T(8,128)(2,1)}, u32[]{:S(2)}) copy-start(bf16[12,896,128]{2,1,0:T(8,128)(2,1)} %gather_fusion.7) | copy-start | bytes 8257540
  296.8 6.8 %copy-start.10 = (bf16[1,3,12,128,128]{4,3,2,1,0:T(8,128)(2,1)S(1)}, bf16[1,3,12,128,128]{4,3,2,1,0:T(8,128)(2,1)}, u32[]{:S(2)}) copy-start(bf16[1,3,12,128,128]{4,3,2,1,0:T(8,128)(2,1)} %param.18) | copy-start | bytes 3538948
  338.7 4.8 copy-start.4
  346.0 4.8 copy-start.3
  353.4 3.9 copy-start.11
  353.4 3.9 copy-start.12
  357.3 1.7 copy-start.15
  357.3 2.6 copy-start.6
  361.9 20.1 %copy-start.8 = (bf16[12,896,128]{2,1,0:T(8,128)(2,1)S(1)}, bf16[12,896,128]{2,1,0:T(8,128)(2,1)}, u32[]{:S(2)}) copy-start(bf16[12,896,128]{2,1,0:T(8,128)(2,1)} %gather_fusion.9) | copy-start | bytes 8257540
  382.0 15.1 %copy-start.13 = (f32[1,3,12,16,128]{4,3,2,1,0:T(8,128)S(1)}, f32[1,3,12,16,128]{4,3,2,1,0:T(8,128)}, u32[]{:S(2)}) copy-start(f32[1,3,12,16,128]{4,3,2,1,0:T(8,128)} %param.20) | copy-start | bytes 884740
  386.4 30.5 %copy-start.5 = (bf16[12,896,128]{2,1,0:T(8,128)(2,1)S(1)}, bf16[12,896,128]{2,1,0:T(8,128)(2,1)}, u32[]{:S(2)}) copy-start(bf16[12,896,128]{2,1,0:T(8,128)(2,1)} %gather_fusion.8) | copy-start | bytes 8257540
  402.0 25.5 %all-to-all-start.5 = ((bf16[64,2,576]{2,1,0:T(2,128)(2,1)}), bf16[64,2,576]{2,1,0:T(2,128)(2,1)S(1)}, u32[]{:S(2)}, u32[]{:S(2)}) async-start(bf16[64,2,576]{2,1,0:T(2,128)(2,1)} %reshape.353), calls=%async_computation.6 | async-start | bytes 327680 | tf_op jit(solution)/shard_map/all_to_all | solution.py:87
  427.5 18.5 %all-to-all-start.7 = ((f32[64,1,1152]{2,1,0:T(1,128)}), f32[64,1,1152]{2,1,0:T(1,128)S(1)}, u32[]{:S(2)}, u32[]{:S(2)}) async-start(f32[64,1,1152]{2,1,0:T(1,128)} %bitcast.42), calls=%async_computation.8 | async-start | bytes 589824 | tf_op jit(solution)/shard_map/all_to_all | solution.py:90
  446.1 19.6 %all-to-all-start.4 = ((bf16[64,14,1]{1,2,0:T(2,128)(2,1)}), bf16[64,14,1]{1,2,0:T(2,128)(2,1)S(1)}, u32[]{:S(2)}, u32[]{:S(2)}) async-start(bf16[64,14,1]{1,2,0:T(2,128)(2,1)} %convert_element_type.112), calls=%async_computation.4 | async-start | bytes 65536 | tf_op jit(solution)/shard_map/all_to_all | solution.py:157
  465.6 15.4 %all-to-all-start.6 = ((bf16[64,2,576]{2,1,0:T(2,128)(2,1)}), bf16[64,2,576]{2,1,0:T(2,128)(2,1)S(1)}, u32[]{:S(2)}, u32[]{:S(2)}) async-start(bf16[64,2,576]{2,1,0:T(2,128)(2,1)} %reshape.355), calls=%async_computation.7 | async-start | bytes 327680 | tf_op jit(solution)/shard_map/all_to_all | solution.py:101
  481.0 26.4 %all-to-all-start.8 = ((f32[64,1,1152]{2,1,0:T(1,128)}), f32[64,1,1152]{2,1,0:T(1,128)S(1)}, u32[]{:S(2)}, u32[]{:S(2)}) async-start(f32[64,1,1152]{2,1,0:T(1,128)} %copy.110), calls=%async_computation.9 | async-start | bytes 589824 | tf_op jit(solution)/shard_map/all_to_all | solution.py:102
  507.5 106.4 %all-to-all-start.3 = ((bf16[64,14,2048]{2,1,0:T(8,128)(2,1)}), bf16[64,14,2048]{2,1,0:T(8,128)(2,1)}, u32[]{:S(2)}, u32[]{:S(2)}) async-start(bf16[64,14,2048]{2,1,0:T(8,128)(2,1)} %convert_element_type.100), calls=%async_computation.3 | async-start | bytes 8388608 | tf_op jit(solution)/shard_map/all_to_all | solution.py:156
  518.0 123.5 %all-gather.2.cloned.1.call-start = ((), (), s32[]{:S(2)}) async-start(), calls=%async_computation.11 | async-start | bytes 1327104 | tf_op jit(solution)/shard_map/all_gather | solution.py:171
  629.5 15.2 %copy-start.1 = (bf16[128,2048]{1,0:T(8,128)(2,1)S(1)}, bf16[128,2048]{1,0:T(8,128)(2,1)}, u32[]{:S(2)}) copy-start(bf16[128,2048]{1,0:T(8,128)(2,1)} %param.15) | copy-start | bytes 1572868
Sparse Core Ops, SparseCore 0:
  359.1 37.9 reduce-scatter.1
  521.4 38.9 all-gather.1
where the time goes:
time: 661 us; the launch traced here: 652 us
  waiting for transfers between devices  196 us (30%)
  local copies, waits for them, and re-layouts  124 us (19%)
  blocking collectives  107 us (16%)
  matrix products  103 us (16%)
  starting transfers between devices  73.2 us (11%)
  other arithmetic  34.2 us (5%)
  between operations  15 us (2%)
    all_to_all x1, blocking collectives, body(): lax.all_to_all(send_tokens, 'expert', split_axis=0, concat_axis=0, tiled=...  107 us
    all_to_all x1, waiting for transfers between devices, body(): lax.all_to_all(input_grad, 'expert', split_axis=0, concat_axis=0, tiled=T...  87.6 us
    all_to_all x1, waiting for transfers between devices, body(): lax.all_to_all(send_grads, 'expert', split_axis=0, concat_axis=0, tiled=T...  75.4 us
    dot_general x6, matrix products, block_product(): jnp.einsum('rbn,bc->rcn', partial_out, select, precision=lax.Precision.HI...  74.1 us
    gather x6, local copies, waits for them, and re-layouts, block_product(): jnp.take(left.reshape(row_count, -1, block_size), source_idx, axis=1)  21.5 us
    all_to_all x1, starting transfers between devices, relocate(): lax.all_to_all(first_state.reshape(expert_count, -1), 'expert', split_axi...  14.9 us
    all_to_all x1, starting transfers between devices, body(): lax.all_to_all(send_weights, 'expert', split_axis=0, concat_axis=0, tiled...  14.8 us
    dot_general x3, matrix products, block_outer(): jnp.einsum('rbk,rbn->bkn', left_pieces, right_pieces, preferred_element_t...  13.5 us
  transfers between devices with their start and end apart: 10, of which 6 were waited for; matrix products, arithmetic and copies ran while one was open for 22% of the time, Pallas kernels for 0%

commit v1 on v0

v1 whole, which is shorter than its diff:
```python
import functools

import jax
import jax.numpy as jnp
from jax import lax
from jax.experimental import pallas as pl
from jax.experimental.pallas import tpu as pltpu
from jax.sharding import PartitionSpec as P

HID = 1408
BLK = 128
CAP = 14
DECAY = 0.9
RATE = 0.01

NT = (((1,), (1,)), ((), ()))
TN = (((0,), (0,)), ((), ()))


def dot(a, b, dims=(((1,), (0,)), ((), ()))):
    return lax.dot_general(a, b, dims, preferred_element_type=jnp.float32)


def lanes(i):
    return pl.ds(pl.multiple_of(i * BLK, BLK), BLK)


def expert_kernel(lay, x_ref, s_ref, w_ref, pg_ref, sc_ref, wg_ref, gate, up, hg, hid, gg, ug, acc):
    nb = w_ref.shape[1]
    rows = x_ref.shape[1]
    per = x_ref.shape[2] // BLK

    def chunk(ref, i):
        return ref[i // per, :, lanes(i % per)]

    @pl.when(pl.program_id(0) == 0)
    def _():
        wg_ref[...] = jnp.zeros_like(wg_ref)

    gate[...] = jnp.zeros_like(gate)
    up[...] = jnp.zeros_like(up)
    hg[...] = jnp.zeros_like(hg)

    def first(b, carry):
        gate[:, lanes(lay[0, b, 1])] += dot(chunk(x_ref, lay[0, b, 0]), w_ref[0, b])
        up[:, lanes(lay[1, b, 1])] += dot(chunk(x_ref, lay[1, b, 0]), w_ref[1, b])
        hg[:, lanes(lay[2, b, 0])] += dot(chunk(s_ref, lay[2, b, 1]), w_ref[2, b], NT)
        return carry

    lax.fori_loop(0, nb, first, 0)

    def middle(j, score):
        g = gate[:, lanes(j)]
        u = up[:, lanes(j)]
        h = hg[:, lanes(j)]
        sig = jax.nn.sigmoid(g)
        act = g * sig
        hb = (act * u).astype(jnp.bfloat16)
        hid[:, lanes(j)] = hb
        gg[:, lanes(j)] = (h * u * sig * (1.0 + g * (1.0 - sig))).astype(jnp.bfloat16)
        ug[:, lanes(j)] = (h * act).astype(jnp.bfloat16)
        return score + hb.astype(jnp.float32) * h

    score = lax.fori_loop(0, HID // BLK, middle, jnp.zeros((rows, BLK), jnp.float32))
    total = jnp.sum(score, axis=1, keepdims=True)
    high = total.astype(jnp.bfloat16).astype(jnp.float32)
    lane = lax.broadcasted_iota(jnp.int32, (rows, BLK), 1)
    place = 0
    sc_ref[...] = jnp.where(
        lane == place, high, jnp.where(lane == place + 8, total - high, 0.0)
    ).astype(jnp.bfloat16)

    acc[...] = jnp.zeros_like(acc)

    def last(b, carry):
        r0, c0, r1, c1 = lay[0, b, 0], lay[0, b, 1], lay[1, b, 0], lay[1, b, 1]
        acc[:, lanes(r0)] += dot(gg[:, lanes(c0)], w_ref[0, b], NT)
        acc[:, lanes(r1)] += dot(ug[:, lanes(c1)], w_ref[1, b], NT)
        wg_ref[0, b] += dot(chunk(x_ref, r0), gg[:, lanes(c0)], TN)
        wg_ref[1, b] += dot(chunk(x_ref, r1), ug[:, lanes(c1)], TN)
        wg_ref[2, b] += dot(hid[:, lanes(lay[2, b, 0])], chunk(s_ref, lay[2, b, 1]), TN)
        return carry

    lax.fori_loop(0, nb, last, 0)
    for q in range(pg_ref.shape[0]):
        width = pg_ref.shape[2]
        pg_ref[q] = acc[:, q * width : (q + 1) * width].astype(jnp.bfloat16)


def expert_compute(layout_one, xs, grads, mats, tile):
    nq, rows, width = xs.shape
    nm, nb = mats.shape[:2]
    row_spec = pl.BlockSpec((nq, tile, width), lambda i, lay: (0, i, 0))
    f32, bf16 = jnp.float32, jnp.bfloat16
    return pl.pallas_call(
        expert_kernel,
        grid_spec=pltpu.PrefetchScalarGridSpec(
            num_scalar_prefetch=1,
            grid=(rows // tile,),
            in_specs=[
                row_spec,
                row_spec,
                pl.BlockSpec((nm, nb, BLK, BLK), lambda i, lay: (0, 0, 0, 0)),
            ],
            out_specs=[
                row_spec,
                pl.BlockSpec((tile, BLK), lambda i, lay: (i, 0)),
                pl.BlockSpec((nm, nb, BLK, BLK), lambda i, lay: (0, 0, 0, 0)),
            ],
            scratch_shapes=[
                pltpu.VMEM((tile, HID), f32),
                pltpu.VMEM((tile, HID), f32),
                pltpu.VMEM((tile, HID), f32),
                pltpu.VMEM((tile, HID), bf16),
                pltpu.VMEM((tile, HID), bf16),
                pltpu.VMEM((tile, HID), bf16),
                pltpu.VMEM((tile, nq * width), f32),
            ],
        ),
        out_shape=[
            jax.ShapeDtypeStruct(xs.shape, bf16),
            jax.ShapeDtypeStruct((rows, BLK), bf16),
            jax.ShapeDtypeStruct(mats.shape, f32),
        ],
        compiler_params=pltpu.CompilerParams(vmem_limit_bytes=56 << 20),
        cost_estimate=pl.CostEstimate(
            flops=8 * nb * rows * BLK * BLK * 2,
            bytes_accessed=3 * xs.size * 2 + mats.size * 6,
            transcendentals=rows * HID,
        ),
    )(layout_one, xs, grads, mats)


def move_state(own_blocks, moments, layout_one, partner, n):
    bf16 = jnp.bfloat16
    tiles = own_blocks.size // (16 * BLK)
    high = moments.astype(bf16)
    low = (moments - high.astype(jnp.float32)).astype(bf16)
    flat_layout = layout_one.reshape(-1)
    lay_tile = jnp.pad(flat_layout, (0, 16 * BLK - flat_layout.size)).astype(bf16)
    count = 3 * tiles + 1
    padded = -(-count // n) * n
    state = jnp.concatenate(
        [
            own_blocks.reshape(tiles, 16, BLK),
            high.reshape(tiles, 16, BLK),
            low.reshape(tiles, 16, BLK),
            lay_tile.reshape(1, 16, BLK),
            jnp.zeros((padded - count, 16, BLK), bf16),
        ]
    ).reshape(n, -1, BLK)
    spread = lax.all_to_all(state, "expert", split_axis=0, concat_axis=0, tiled=True)
    moved = lax.all_to_all(spread[partner], "expert", split_axis=0, concat_axis=0, tiled=True)
    moved = moved.reshape(padded, 16, BLK)
    new_blocks = moved[:tiles].reshape(own_blocks.shape)
    new_moments = (
        moved[tiles : 2 * tiles].astype(jnp.float32)
        + moved[2 * tiles : 3 * tiles].astype(jnp.float32)
    ).reshape(moments.shape)
    new_layout = (
        moved[3 * tiles].reshape(-1)[: flat_layout.size].astype(jnp.int32).reshape(layout_one.shape)
    )
    return new_blocks, new_moments, new_layout


def body(tokens, out_grad, expert_ids, route_weights, blocks, layout, moments, partner):
    f32, bf16 = jnp.float32, jnp.bfloat16
    n = lax.axis_size("expert")
    n_dp = lax.axis_size("dp")
    count, width = tokens.shape
    share = BLK // n_dp
    own = lax.dynamic_slice_in_dim(blocks[0], lax.axis_index("dp") * share, share, 2)
    own, old_moment, layout_one = move_state(own, moments[0], layout[0], partner, n)
    mats = lax.all_gather(own, "dp", axis=2, tiled=True)

    picks = expert_ids[None] == partner[:, None, None]
    named = jnp.any(picks, axis=2)
    before = jnp.tril(jnp.ones((count, count), bf16), -1)
    rank = dot(named.astype(bf16), before, NT)
    rank = jnp.where(named, rank, -1.0)
    weight = jnp.sum(jnp.where(picks, route_weights[None].astype(f32), 0.0), axis=2)
    slots = lax.broadcasted_iota(jnp.int32, (1, CAP, 1), 1).astype(f32)
    choose = rank[:, None, :] == slots
    take = choose.astype(bf16).reshape(n * CAP, count)
    scale = jnp.where(choose, weight[:, None, :], 0.0).astype(bf16).reshape(n * CAP, count)
    send_x = dot(take, tokens).astype(bf16).reshape(n, CAP, width)
    send_s = dot(scale, out_grad).astype(bf16).reshape(n, CAP, width)
    xs = lax.all_to_all(send_x, "expert", split_axis=0, concat_axis=0, tiled=True)
    ss = lax.all_to_all(send_s, "expert", split_axis=0, concat_axis=0, tiled=True)
    pg, sc, wg = expert_compute(
        layout_one, xs.reshape(1, n * CAP, width), ss.reshape(1, n * CAP, width), mats, 448
    )
    back = jnp.concatenate([pg[0], sc], axis=1).reshape(n, CAP, width + BLK)
    back = lax.all_to_all(back, "expert", split_axis=0, concat_axis=0, tiled=True)
    back = back.reshape(n * CAP, width + BLK)
    token_grad = dot(take, back[:, :width], TN).astype(bf16)
    score_rows = back[:, width].astype(f32) + back[:, width + 8].astype(f32)
    score = jnp.sum(jnp.where(choose, score_rows.reshape(n, CAP, 1), 0.0), axis=1)
    score = jnp.sum(jnp.where(picks, score[:, :, None], 0.0), axis=0)
    route_grad = (score / route_weights.astype(f32)).astype(bf16)

    shard = lax.psum_scatter(wg, "dp", scatter_dimension=2, tiled=True)
    moment = DECAY * old_moment + shard
    updated = (own.astype(f32) - RATE * moment).astype(bf16)
    gathered = lax.all_gather(updated, "dp", axis=2, tiled=True)
    return token_grad, route_grad, gathered[None], moment[None]


def solution(mesh):
    rows = P(("dp", "expert"), None)
    state = P("expert", None, None, None, None)
    moment = P("expert", None, None, "dp", None)
    return jax.shard_map(
        body,
        mesh=mesh,
        in_specs=(rows, rows, rows, rows, state, P("expert", None, None, None), moment, P()),
        out_specs=(rows, rows, state, moment),
        check_vma=False,
    )
```

time: 661 us -> 448 us (0.68); the launches traced: 652 us -> 446 us
  blocking collectives: 107 us -> 0 us
  waiting for transfers between devices: 196 us -> 298 us
  matrix products: 103 us -> 9.62 us
  local copies, waits for them, and re-layouts: 124 us -> 44.8 us
  starting transfers between devices: 73.2 us -> 39.9 us
  Pallas kernels: 0 us -> 26.6 us
  other arithmetic: 34.2 us -> 13.4 us
    all_to_all x1 -> x0, blocking collectives: 107 us -> none  [body(): lax.all_to_all(send_tokens, 'expert', split_axis=0, concat_axis=0, tiled=...]
    dot_general x15 -> x4, matrix products: 103 us -> 9.62 us  [dot(): return lax.dot_general(a, b, dims, preferred_element_type=jnp.float32)]
    gather x15 -> x1, local copies, waits for them, and re-layouts: 65.5 us -> 1.41 us  [move_state(): spread[partner]]
    all_gather x1 -> x2, waiting for transfers between devices: 0.01 us -> 43.9 us  [the longest x1 43.9 us: body(): gathered = lax.all_gather(updated, 'dp', axis=2, tiled=True)]
    reduce_scatter x1, waiting for transfers between devices: 10.7 us -> 45.7 us  [body(): shard = lax.psum_scatter(wg, 'dp', scatter_dimension=2, tiled=True)]
    all_to_all x8 -> x5, starting transfers between devices: 72.6 us -> 39.7 us  [the longest x1 14.8 us: move_state(): lax.all_to_all(state, 'expert', split_axis=0, concat_axis=0, tiled=True)]
    pallas_call x0 -> x1, Pallas kernels: none -> 26.6 us  [expert_compute(): pl.pallas_call(expert_kernel, grid_spec=pltpu.PrefetchScalarGridSpec(num_...]
    all_to_all x8 -> x5, waiting for transfers between devices: 186 us -> 208 us  [the longest x1 88.5 us: body(): lax.all_to_all(send_x, 'expert', split_axis=0, concat_axis=0, tiled=True)]
  transfers between devices with their start and end apart: 10 -> 8, of which waited for: 6 -> 7; matrix products, arithmetic and copies ran while one was open for 22% -> 8% of each run, Pallas kernels for 0% -> 0%
where the time goes in v1:
time: 448 us; the launch traced here: 446 us
  waiting for transfers between devices  298 us (67%)
  local copies, waits for them, and re-layouts  44.8 us (10%)
  starting transfers between devices  39.9 us (9%)
  Pallas kernels  26.6 us (6%)
  between operations  14 us (3%)
  other arithmetic  13.4 us (3%)
  matrix products  9.62 us (2%)
    all_to_all x1, waiting for transfers between devices, body(): lax.all_to_all(send_x, 'expert', split_axis=0, concat_axis=0, tiled=True)  88.5 us
    all_to_all x1, waiting for transfers between devices, body(): lax.all_to_all(send_s, 'expert', split_axis=0, concat_axis=0, tiled=True)  87 us
    reduce_scatter x1, waiting for transfers between devices, body(): shard = lax.psum_scatter(wg, 'dp', scatter_dimension=2, tiled=True)  45.7 us
    all_gather x1, waiting for transfers between devices, body(): gathered = lax.all_gather(updated, 'dp', axis=2, tiled=True)  43.9 us
    pallas_call x1, Pallas kernels, expert_compute(): pl.pallas_call(expert_kernel, grid_spec=pltpu.PrefetchScalarGridSpec(num_...  26.6 us
    all_to_all x1, waiting for transfers between devices, move_state(): lax.all_to_all(state, 'expert', split_axis=0, concat_axis=0, tiled=True)  15.2 us
    all_to_all x1, starting transfers between devices, move_state(): lax.all_to_all(state, 'expert', split_axis=0, concat_axis=0, tiled=True)  14.8 us
    dot_general x4, matrix products, dot(): return lax.dot_general(a, b, dims, preferred_element_type=jnp.float32)  9.62 us
  transfers between devices with their start and end apart: 8, of which 7 were waited for; matrix products, arithmetic and copies ran while one was open for 8% of the time, Pallas kernels for 0%

profile of v1, /device:TPU:1, one launch (start us, length us, event | category | flops | bytes accessed | tf_op | source)
XLA Modules:
  0.0 446.2 jit_solution(17949129030241872170)
XLA Ops:
  7.2 0.8 convert.6
  8.1 0.1 reshape_squeeze.7
  8.2 1.0 fusion.5
  9.3 0.7 constant_dynamic-update-slice_fusion.3
  10.0 0.7 constant_dynamic-update-slice_fusion.2
  10.6 0.7 constant_dynamic-update-slice_fusion.1
  11.3 0.6 constant_dynamic-update-slice_fusion
  11.9 0.6 broadcast_dynamic-update-slice_fusion
  12.6 14.8 %all-to-all-start = ((bf16[64,32,128]{2,1,0:T(8,128)(2,1)}), bf16[64,32,128]{2,1,0:T(8,128)(2,1)S(1)}, u32[]{:S(2)}, u32[]{:S(2)}) async-start(bf16[64,32,128]{2,1,0:T(8,128)(2,1)} %bitcast.3), calls=%async_computation | async-start | bytes 1048576 | tf_op jit(solution)/shard_map/all_to_all | solution.py:152
  27.4 0.7 convert_element_type.93
  28.1 0.7 compare_select_fusion.2
  28.7 0.8 fusion.7
  29.5 15.2 %all-to-all-done = bf16[64,32,128]{2,1,0:T(8,128)(2,1)S(1)} async-done(((bf16[64,32,128]{2,1,0:T(8,128)(2,1)}), bf16[64,32,128]{2,1,0:T(8,128)(2,1)S(1)}, u32[]{:S(2)}, u32[]{:S(2)}) %all-to-all-start) | async-done | bytes 524320 | tf_op jit(solution)/shard_map/all_to_all | solution.py:152
  44.7 1.4 gather_fusion
  46.1 6.3 %all-to-all-start.1 = ((bf16[64,32,128]{2,1,0:T(8,128)(2,1)}), bf16[64,32,128]{2,1,0:T(8,128)(2,1)S(1)}, u32[]{:S(2)}, u32[]{:S(2)}) async-start(bf16[64,32,128]{2,1,0:T(8,128)(2,1)} %gather_fusion), calls=%async_computation.1 | async-start | bytes 1048576 | tf_op jit(solution)/shard_map/all_to_all | solution.py:153
  52.4 0.1 eq.44
  52.8 0.2 convolution_select_fusion
  53.1 0.2 broadcast_compare_fusion
  53.3 2.9 convolution_convert_fusion
  56.2 5.8 %reshape.104 = bf16[64,14,2048]{2,1,0:T(8,128)(2,1)} reshape(bf16[896,2048]{1,0:T(8,128)(2,1)} %convolution_convert_fusion) | data formatting | bytes 7340032 | tf_op jit(solution)/shard_map/reshape | solution.py:187
  62.1 7.7 %all-to-all-done.1 = bf16[64,32,128]{2,1,0:T(8,128)(2,1)S(1)} async-done(((bf16[64,32,128]{2,1,0:T(8,128)(2,1)}), bf16[64,32,128]{2,1,0:T(8,128)(2,1)S(1)}, u32[]{:S(2)}, u32[]{:S(2)}) %all-to-all-start.1) | async-done | bytes 524320 | tf_op jit(solution)/shard_map/all_to_all | solution.py:153
  69.7 6.5 %all-to-all-start.3 = ((bf16[64,14,2048]{2,1,0:T(8,128)(2,1)}), bf16[64,14,2048]{2,1,0:T(8,128)(2,1)}, u32[]{:S(2)}, u32[]{:S(2)}) async-start(bf16[64,14,2048]{2,1,0:T(8,128)(2,1)} %reshape.104), calls=%async_computation.3 | async-start | bytes 8388608 | tf_op jit(solution)/shard_map/all_to_all | solution.py:189
  76.2 2.9 convolution_convert_fusion.1
  79.1 6.0 %reshape.102 = bf16[64,14,2048]{2,1,0:T(8,128)(2,1)} reshape(bf16[896,2048]{1,0:T(8,128)(2,1)} %convolution_convert_fusion.1) | data formatting | bytes 7340032 | tf_op jit(solution)/shard_map/reshape | solution.py:186
  85.1 87.0 %all-to-all-done.3 = bf16[64,14,2048]{2,1,0:T(8,128)(2,1)} async-done(((bf16[64,14,2048]{2,1,0:T(8,128)(2,1)}), bf16[64,14,2048]{2,1,0:T(8,128)(2,1)}, u32[]{:S(2)}, u32[]{:S(2)}) %all-to-all-start.3) | async-done | bytes 3670048 | tf_op jit(solution)/shard_map/all_to_all | solution.py:189
  172.1 5.9 %all-to-all-start.2 = ((bf16[64,14,2048]{2,1,0:T(8,128)(2,1)}), bf16[64,14,2048]{2,1,0:T(8,128)(2,1)}, u32[]{:S(2)}, u32[]{:S(2)}) async-start(bf16[64,14,2048]{2,1,0:T(8,128)(2,1)} %reshape.102), calls=%async_computation.2 | async-start | bytes 8388608 | tf_op jit(solution)/shard_map/all_to_all | solution.py:188
  178.1 0.7 slice.39
  178.8 0.7 reshape.108.lay
  179.5 5.9 %reshape.105.s_ref = bf16[1,896,2048]{2,1,0:T(8,128)(2,1)} reshape(bf16[64,14,2048]{2,1,0:T(8,128)(2,1)} %all-to-all-done.3) | data formatting | bytes 7340032 | tf_op jit(solution)/shard_map/reshape | solution.py:191
  185.4 88.5 %all-to-all-done.2 = bf16[64,14,2048]{2,1,0:T(8,128)(2,1)} async-done(((bf16[64,14,2048]{2,1,0:T(8,128)(2,1)}), bf16[64,14,2048]{2,1,0:T(8,128)(2,1)}, u32[]{:S(2)}, u32[]{:S(2)}) %all-to-all-start.2) | async-done | bytes 3670048 | tf_op jit(solution)/shard_map/all_to_all | solution.py:188
  273.9 6.0 %reshape.103.x_ref = bf16[1,896,2048]{2,1,0:T(8,128)(2,1)} reshape(bf16[64,14,2048]{2,1,0:T(8,128)(2,1)} %all-to-all-done.2) | data formatting | bytes 7340032 | tf_op jit(solution)/shard_map/reshape | solution.py:191
  279.9 26.6 %shard_map.111 = (bf16[1,896,2048]{2,1,0:T(8,128)(2,1)}, bf16[896,128]{1,0:T(8,128)(2,1)}, f32[3,12,128,128]{3,2,1,0:T(8,128)}) custom-call(s32[3,12,2]{2,1,0:T(8,128)} %reshape.108.lay, bf16[1,896,2048]{2,1,0:T(8,128)(2,1)} %reshape.103.x_ref, bf16[1,896,2048]{2,1,0:T(8,128)(2,1)} %reshape.105.s_ref, ...), custom_call_target="tpu_custom_call" | custom-call | flops 2818572288 | bytes 14548992 | tf_op jit(solution)/shard_map/pallas_call | solution.py:95
  306.5 1.0 concatenate.13
  307.5 6.0 %concatenate.12 = bf16[64,14,2048]{2,1,0:T(8,128)(2,1)} reshape(bf16[1,896,2048]{2,1,0:T(8,128)(2,1)} %get-tuple-element.7) | data formatting | bytes 7340032 | tf_op jit(solution)/shard_map/concatenate | solution.py:193
  313.5 5.0 %pad_maximum_fusion = bf16[64,14,2176]{2,1,0:T(8,128)(2,1)} fusion(bf16[64,14,128]{2,1,0:T(8,128)(2,1)S(1)} %concatenate.13, bf16[64,14,2048]{2,1,0:T(8,128)(2,1)} %concatenate.12), kind=kLoop, calls=%fused_computation.1 | loop fusion | flops 7798784 | bytes 7798784 | tf_op jit(solution)/shard_map/concatenate | solution.py:193
  318.5 6.2 %all-to-all-start.4 = ((bf16[64,14,2176]{2,1,0:T(8,128)(2,1)}), bf16[64,14,2176]{2,1,0:T(8,128)(2,1)}, u32[]{:S(2)}, u32[]{:S(2)}) async-start(bf16[64,14,2176]{2,1,0:T(8,128)(2,1)} %pad_maximum_fusion), calls=%async_computation.4 | async-start | bytes 8912896 | tf_op jit(solution)/shard_map/all_to_all | solution.py:194
  324.8 0.7 reduce-scatter.2.cloned.1.call-update
  325.6 45.7 %reduce-scatter.2.cloned.1.call-done = f32[3,12,16,128]{3,2,1,0:T(8,128)} async-done(((f32[3,12,128,128]{3,2,1,0:T(8,128)}), f32[3,12,16,128]{3,2,1,0:T(8,128)}) %reduce-scatter.2.cloned.1.call-update) | async-done | bytes 294928 | tf_op jit(solution)/shard_map/reduce_scatter | solution.py:202
  371.3 1.8 add_bitcast_fusion
  373.1 43.9 %all-gather.5.cloned.1.call-done = bf16[3,12,128,128]{3,2,1,0:T(8,128)(2,1)} async-done(((bf16[3,12,16,128]{3,2,1,0:T(8,128)(2,1)}), bf16[3,12,128,128]{3,2,1,0:T(8,128)(2,1)}) %all-gather.5.cloned.1.call-update) | async-done | bytes 1179664 | tf_op jit(solution)/shard_map/all_gather | solution.py:205
  416.9 9.3 %all-to-all-done.4 = bf16[64,14,2176]{2,1,0:T(8,128)(2,1)} async-done(((bf16[64,14,2176]{2,1,0:T(8,128)(2,1)}), bf16[64,14,2176]{2,1,0:T(8,128)(2,1)}, u32[]{:S(2)}, u32[]{:S(2)}) %all-to-all-start.4) | async-done | bytes 3899424 | tf_op jit(solution)/shard_map/all_to_all | solution.py:194
  426.2 6.2 %reshape.107 = bf16[896,2176]{1,0:T(8,128)(2,1)} reshape(bf16[64,14,2176]{2,1,0:T(8,128)(2,1)} %all-to-all-done.4) | data formatting | bytes 7798784 | tf_op jit(solution)/shard_map/reshape | solution.py:195
  432.5 1.5 add_reduce_fusion
  434.0 3.6 fusion.2
  437.6 0.1 add.46
  437.7 0.2 select_reduce_fusion
  438.0 0.6 divide_convert_fusion
  438.6 1.0 copy.28
  (39 shorter events, 0.8 us)
Async XLA Ops:
  7.2 2.1 copy-start
  7.2 45.5 %copy-start.8 = (s32[64]{0:T(128)S(1)}, s32[64]{0:T(128)}, u32[]{:S(2)}) copy-start(s32[64]{0:T(128)} %param.15) | copy-start | bytes 772
  7.2 45.5 %copy-start.6 = (s32[128,6]{0,1:T(8,128)S(1)}, s32[128,6]{0,1:T(8,128)}, u32[]{:S(2)}) copy-start(s32[128,6]{0,1:T(8,128)} %param.10) | copy-start | bytes 9220
  9.2 44.1 %copy-start.4 = (bf16[128,2048]{1,0:T(8,128)(2,1)S(1)}, bf16[128,2048]{1,0:T(8,128)(2,1)}, u32[]{:S(2)}) copy-start(bf16[128,2048]{1,0:T(8,128)(2,1)} %param.9) | copy-start | bytes 1572868
  12.6 32.2 %all-to-all-start = ((bf16[64,32,128]{2,1,0:T(8,128)(2,1)}), bf16[64,32,128]{2,1,0:T(8,128)(2,1)S(1)}, u32[]{:S(2)}, u32[]{:S(2)}) async-start(bf16[64,32,128]{2,1,0:T(8,128)(2,1)} %bitcast.3), calls=%async_computation | async-start | bytes 1048576 | tf_op jit(solution)/shard_map/all_to_all | solution.py:152
  46.1 23.6 %all-to-all-start.1 = ((bf16[64,32,128]{2,1,0:T(8,128)(2,1)}), bf16[64,32,128]{2,1,0:T(8,128)(2,1)S(1)}, u32[]{:S(2)}, u32[]{:S(2)}) async-start(bf16[64,32,128]{2,1,0:T(8,128)(2,1)} %gather_fusion), calls=%async_computation.1 | async-start | bytes 1048576 | tf_op jit(solution)/shard_map/all_to_all | solution.py:153
  62.1 14.1 %copy-start.5 = (bf16[128,2048]{1,0:T(8,128)(2,1)S(1)}, bf16[128,2048]{1,0:T(8,128)(2,1)}, u32[]{:S(2)}) copy-start(bf16[128,2048]{1,0:T(8,128)(2,1)} %param.8) | copy-start | bytes 1572868
  69.7 102.4 %all-to-all-start.3 = ((bf16[64,14,2048]{2,1,0:T(8,128)(2,1)}), bf16[64,14,2048]{2,1,0:T(8,128)(2,1)}, u32[]{:S(2)}, u32[]{:S(2)}) async-start(bf16[64,14,2048]{2,1,0:T(8,128)(2,1)} %reshape.104), calls=%async_computation.3 | async-start | bytes 8388608 | tf_op jit(solution)/shard_map/all_to_all | solution.py:189
  172.1 101.8 %all-to-all-start.2 = ((bf16[64,14,2048]{2,1,0:T(8,128)(2,1)}), bf16[64,14,2048]{2,1,0:T(8,128)(2,1)}, u32[]{:S(2)}, u32[]{:S(2)}) async-start(bf16[64,14,2048]{2,1,0:T(8,128)(2,1)} %reshape.102), calls=%async_computation.2 | async-start | bytes 8388608 | tf_op jit(solution)/shard_map/all_to_all | solution.py:188
  178.1 101.9 %all-gather.3.cloned.1.call-start = ((), (), s32[]{:S(2)}) async-start(), calls=%async_computation.6 | async-start | bytes 1327104 | tf_op jit(solution)/shard_map/all_gather | solution.py:174
  318.5 52.8 %copy-start.2 = (bf16[18,32,128]{2,1,0:T(8,128)(2,1)S(1)}, bf16[18,32,128]{2,1,0:T(8,128)(2,1)}, u32[]{:S(2)}) copy-start(bf16[18,32,128]{2,1,0:T(8,128)(2,1)} %slice.39) | copy-start | bytes 442372
  318.5 107.8 %all-to-all-start.4 = ((bf16[64,14,2176]{2,1,0:T(8,128)(2,1)}), bf16[64,14,2176]{2,1,0:T(8,128)(2,1)}, u32[]{:S(2)}, u32[]{:S(2)}) async-start(bf16[64,14,2176]{2,1,0:T(8,128)(2,1)} %pad_maximum_fusion), calls=%async_computation.4 | async-start | bytes 8912896 | tf_op jit(solution)/shard_map/all_to_all | solution.py:194
  324.7 46.5 %reduce-scatter.2.cloned.1.call-start = ((), (), s32[]{:S(2)}) async-start(), calls=%async_computation.7 | async-start | bytes 2654208 | tf_op jit(solution)/shard_map/reduce_scatter | solution.py:202
  325.5 91.5 %all-gather.5.cloned.1.call-start = ((), (), s32[]{:S(2)}) async-start(), calls=%async_computation.8 | async-start | bytes 1327104 | tf_op jit(solution)/shard_map/all_gather | solution.py:205
  432.5 5.6 %copy-start.7 = (bf16[128,6]{0,1:T(8,128)(2,1)S(1)}, bf16[128,6]{0,1:T(8,128)(2,1)}, u32[]{:S(2)}) copy-start(bf16[128,6]{0,1:T(8,128)(2,1)} %param.11) | copy-start | bytes 4612
  432.5 6.2 %copy-start.3 = (bf16[3,12,128,128]{3,2,1,0:T(8,128)(2,1)S(1)}, bf16[3,12,128,128]{3,2,1,0:T(8,128)(2,1)}, u32[]{:S(2)}) copy-start(bf16[3,12,128,128]{3,2,1,0:T(8,128)(2,1)} %all-gather.5.cloned.1.call-done) | copy-start | bytes 3538948
  432.5 7.2 %copy-start.1 = (bf16[1,3,12,128,128]{4,3,2,1,0:T(8,128)(2,1)S(1)}, bf16[1,3,12,128,128]{4,3,2,1,0:T(8,128)(2,1)}, u32[]{:S(2)}) copy-start(bf16[1,3,12,128,128]{4,3,2,1,0:T(8,128)(2,1)} %param.12) | copy-start | bytes 3538948
Sparse Core Ops, SparseCore 0:
  181.5 40.8 all-gather.2
  328.4 42.7 reduce-scatter.1
  373.8 43.0 all-gather.4

commit v2 on v1

--- a/solution.py
+++ b/solution.py
@@ -25,7 +25,7 @@
     return pl.ds(pl.multiple_of(i * BLK, BLK), BLK)
 
 
-def expert_kernel(lay, x_ref, s_ref, w_ref, pg_ref, sc_ref, wg_ref, gate, up, hg, hid, gg, ug, acc):
+def expert_kernel(lay, place_ref, x_ref, s_ref, w_ref, pg_ref, sc_ref, wg_ref, gate, up, hg, hid, gg, ug, acc):
     nb = w_ref.shape[1]
     rows = x_ref.shape[1]
     per = x_ref.shape[2] // BLK
@@ -65,7 +65,7 @@
     total = jnp.sum(score, axis=1, keepdims=True)
     high = total.astype(jnp.bfloat16).astype(jnp.float32)
     lane = lax.broadcasted_iota(jnp.int32, (rows, BLK), 1)
-    place = 0
+    place = place_ref[0]
     sc_ref[...] = jnp.where(
         lane == place, high, jnp.where(lane == place + 8, total - high, 0.0)
     ).astype(jnp.bfloat16)
@@ -87,25 +87,27 @@
         pg_ref[q] = acc[:, q * width : (q + 1) * width].astype(jnp.bfloat16)
 
 
-def expert_compute(layout_one, xs, grads, mats, tile):
+def expert_compute(layout_one, place, xs, mats, tile):
     nq, rows, width = xs.shape
+    nq = nq // 2
     nm, nb = mats.shape[:2]
-    row_spec = pl.BlockSpec((nq, tile, width), lambda i, lay: (0, i, 0))
+    row_spec = pl.BlockSpec((nq, tile, width), lambda i, lay, place: (0, i, 0))
+    grad_spec = pl.BlockSpec((nq, tile, width), lambda i, lay, place: (1, i, 0))
     f32, bf16 = jnp.float32, jnp.bfloat16
     return pl.pallas_call(
         expert_kernel,
         grid_spec=pltpu.PrefetchScalarGridSpec(
-            num_scalar_prefetch=1,
+            num_scalar_prefetch=2,
             grid=(rows // tile,),
             in_specs=[
                 row_spec,
-                row_spec,
-                pl.BlockSpec((nm, nb, BLK, BLK), lambda i, lay: (0, 0, 0, 0)),
+                grad_spec,
+                pl.BlockSpec((nm, nb, BLK, BLK), lambda i, lay, place: (0, 0, 0, 0)),
             ],
             out_specs=[
                 row_spec,
-                pl.BlockSpec((tile, BLK), lambda i, lay: (i, 0)),
-                pl.BlockSpec((nm, nb, BLK, BLK), lambda i, lay: (0, 0, 0, 0)),
+                pl.BlockSpec((tile, BLK), lambda i, lay, place: (i, 0)),
+                pl.BlockSpec((nm, nb, BLK, BLK), lambda i, lay, place: (0, 0, 0, 0)),
             ],
             scratch_shapes=[
                 pltpu.VMEM((tile, HID), f32),
@@ -118,17 +120,443 @@
             ],
         ),
         out_shape=[
-            jax.ShapeDtypeStruct(xs.shape, bf16),
+            jax.ShapeDtypeStruct((nq, rows, width), bf16),
             jax.ShapeDtypeStruct((rows, BLK), bf16),
             jax.ShapeDtypeStruct(mats.shape, f32),
         ],
         compiler_params=pltpu.CompilerParams(vmem_limit_bytes=56 << 20),
         cost_estimate=pl.CostEstimate(
             flops=8 * nb * rows * BLK * BLK * 2,
-            bytes_accessed=3 * xs.size * 2 + mats.size * 6,
+            bytes_accessed=3 * xs.size + mats.size * 6,
             transcendentals=rows * HID,
         ),
-    )(layout_one, xs, grads, mats)
+    )(layout_one, place, xs, xs, mats)
+
+
+NX, NZ, NCORE = 4, 8, 2
+PLANE = NX * NCORE
+ROWS = NZ * CAP
+MESH = pl.DeviceIdType.MESH
+
+
+def position():
+    me = lax.axis_index("expert")
+    return lax.axis_index("dp"), me // (NZ * NCORE), (me // NCORE) % NZ, me % NCORE
+
+
+def peers():
+    dp, x, z, core = position()
+
+    def along(other):
+        return (dp, x * (NZ * NCORE) + other * NCORE + core)
+
+    def across(other):
+        return (dp, (other // NCORE) * (NZ * NCORE) + z * NCORE + other % NCORE)
+
+    return z, x * NCORE + core, along, across
+
+
+def meet(z, j, along, across):
+    barrier = pltpu.get_barrier_semaphore()
+    for k in range(1, NZ):
+        pl.semaphore_signal(barrier, inc=1, device_id=along((z + k) % NZ), device_id_type=MESH)
+    for k in range(1, PLANE):
+        pl.semaphore_signal(barrier, inc=1, device_id=across((j + k) % PLANE), device_id_type=MESH)
+    pl.semaphore_wait(barrier, NZ + PLANE - 2)
+
+
+def send(src, dst, send_sem, recv_sem, device):
+    return pltpu.make_async_remote_copy(
+        src_ref=src,
+        dst_ref=dst,
+        send_sem=send_sem,
+        recv_sem=recv_sem,
+        device_id=device,
+        device_id_type=MESH,
+    )
+
+
+def span(i, size):
+    return pl.ds(pl.multiple_of(i * size, size), size)
+
+
+def dispatch_kernel(
+    tok, og, meta, xs, chosen, ring, picked, choose, notes,
+    own_sem, notes_send, notes_recv, ring_send, ring_recv, out_send, out_recv, out_own, keep_sem,
+):
+    count = tok.shape[0]
+    chunks, _, width = ring.shape
+    half = chunks // 2
+    z, j, along, across = peers()
+    ahead, behind = along((z + 1) % NZ), along((z + NZ - 1) % NZ)
+
+    def own_copy(q):
+        src = tok if q < half else og
+        return pltpu.make_async_copy(
+            src.at[:, (q % half) * width : (q % half + 1) * width],
+            ring.at[q, span(z, count)],
+            own_sem.at[q],
+        )
+
+    for q in range(chunks):
+        own_copy(q).start()
+    own_notes = pltpu.make_async_copy(meta.at[z], notes.at[z], keep_sem.at[1])
+    own_notes.start()
+    meet(z, j, along, across)
+
+    def note(k, source):
+        return send(
+            meta.at[(z + k) % NZ],
+            notes.at[source],
+            notes_send.at[k],
+            notes_recv.at[k],
+            along((z + k) % NZ),
+        )
+
+    for k in range(1, NZ):
+        note(k, z).start()
+    for q in range(chunks):
+        own_copy(q).wait()
+    own_notes.wait()
+
+    def hop(q, way, step, arriving):
+        rows = count
+        if way == 0:
+            source = (z + 2 * NZ - step - (1 if arriving else 0)) % NZ
+        else:
+            source = (z + step + (1 if arriving else 0)) % NZ
+        start = source * count
+        if step == NZ // 2 - 1:
+            rows = count // 2
+            start = start + way * rows
+        block = ring.at[q, pl.ds(pl.multiple_of(start, rows), rows)]
+        return send(
+            block, block, ring_send.at[q, way, step], ring_recv.at[q, way, step], ahead if way == 0 else behind
+        )
+
+    def out(q, other, landing):
+        step = (other + PLANE - j) % PLANE
+        return send(
+            picked.at[q, span(other, ROWS)],
+            xs.at[q, span(landing, ROWS)],
+            out_send.at[q, step],
+            out_recv.at[q, step],
+            across(other),
+        )
+
+    def own_out(q):
+        return pltpu.make_async_copy(
+            picked.at[q, span(j, ROWS)], xs.at[q, span(j, ROWS)], out_own.at[q]
+        )
+
+    def keep():
+        return pltpu.make_async_copy(choose.at[0], chosen, keep_sem.at[0])
+
+    def build():
+        for k in range(1, NZ):
+            note(k, (z + NZ - k) % NZ).wait_recv()
+        row = lax.broadcasted_iota(jnp.int32, (ROWS, count), 0).astype(jnp.float32)
+
+        def fill(source, carry):
+            both = notes[source].astype(jnp.float32)
+            for other in range(PLANE):
+                hit = row == both[other : other + 1, :]
+                rows = slice(other * ROWS, (other + 1) * ROWS)
+                scale = both[PLANE + other : PLANE + other + 1, :]
+                choose[0, rows, span(source, count)] = jnp.where(hit, 1.0, 0.0).astype(jnp.bfloat16)
+                choose[1, rows, span(source, count)] = jnp.where(hit, scale, 0.0).astype(jnp.bfloat16)
+            return carry
+
+        lax.fori_loop(0, NZ, fill, 0)
+        keep().start()
+
+    def step(i, carry):
+        for s in range(NZ // 2):
+            q = i - s
+
+            @pl.when((q >= 0) & (q < chunks))
+            def _():
+                for way in range(2):
+                    if s:
+                        hop(q, way, s - 1, True).wait_recv()
+                    hop(q, way, s, False).start()
+
+        pl.when(i == 1)(build)
+        q = i - NZ // 2
+
+        @pl.when(q >= 0)
+        def _():
+            for way in range(2):
+                hop(q, way, NZ // 2 - 1, True).wait_recv()
+
+            def part(h, carry):
+                rows = span(h, PLANE // 2 * ROWS)
+                picked[q, rows, :] = dot(choose[q // half, rows, :], ring[q]).astype(jnp.bfloat16)
+                for o in range(PLANE // 2):
+                    other = h * (PLANE // 2) + o
+
+                    @pl.when(other != j)
+                    def _():
+                        out(q, other, j).start()
+
+                return carry
+
+            lax.fori_loop(0, 2, part, 0)
+            own_out(q).start()
+
+        return carry
+
+    lax.fori_loop(0, chunks + NZ // 2, step, 0)
+
+    def finish(q, carry):
+        for way in range(2):
+            for s in range(NZ // 2):
+                hop(q, way, s, False).wait_send()
+        for o in range(1, PLANE):
+            out(q, (j + o) % PLANE, j).wait_send()
+            out(q, (j + o) % PLANE, (j + PLANE - o) % PLANE).wait_recv()
+        own_out(q).wait()
+        return carry
+
+    lax.fori_loop(0, chunks, finish, 0)
+    for k in range(1, NZ):
+        note(k, z).wait_send()
+    keep().wait()
+
+
+def dispatch(tokens, grads, meta, chunks):
+    count, features = tokens.shape
+    width = 2 * features // chunks
+    bf16 = jnp.bfloat16
+    slots = PLANE * ROWS
+    dma = pltpu.SemaphoreType.DMA
+    anywhere = pl.BlockSpec(memory_space=pl.ANY)
+    return pl.pallas_call(
+        dispatch_kernel,
+        in_specs=[anywhere, anywhere, anywhere],
+        out_specs=[anywhere, anywhere],
+        out_shape=[
+            jax.ShapeDtypeStruct((chunks, slots, width), bf16),
+            jax.ShapeDtypeStruct((slots, NZ * count), bf16),
+        ],
+        scratch_shapes=[
+            pltpu.VMEM((chunks, NZ * count, width), bf16),
+            pltpu.VMEM((chunks, slots, width), bf16),
+            pltpu.VMEM((2, slots, NZ * count), bf16),
+            pltpu.VMEM(meta.shape, bf16),
+            dma((chunks,)),
+            dma((NZ,)),
+            dma((NZ,)),
+            dma((chunks, 2, NZ // 2)),
+            dma((chunks, 2, NZ // 2)),
+            dma((chunks, PLANE)),
+            dma((chunks, PLANE)),
+            dma((chunks,)),
+            dma((2,)),
+        ],
+        compiler_params=pltpu.CompilerParams(
+            collective_id=0, has_side_effects=True, vmem_limit_bytes=56 << 20
+        ),
+        cost_estimate=pl.CostEstimate(flops=2 * slots * NZ * count * 2 * features, bytes_accessed=300 << 20, transcendentals=0),
+    )(tokens, grads, meta)
+
+
+def return_kernel(
+    pg, sc, choose, tg, score, back, marks, part, leaving, landed, sums,
+    own_sem, x_send, x_recv, mark_send, mark_recv, z_send, z_recv, sum_send, sum_recv,
+):
+    chunks, slots, width = pg.shape
+    count = tg.shape[0]
+    last = NZ // 2 - 1
+    z, j, along, across = peers()
+    ahead, behind = along((z + 1) % NZ), along((z + NZ - 1) % NZ)
+
+    def own_copy(q):
+        return pltpu.make_async_copy(
+            pg.at[q, span(j, ROWS)], back.at[q, span(j, ROWS)], own_sem.at[q]
+        )
+
+    own_marks = pltpu.make_async_copy(sc.at[span(j, ROWS)], marks.at[span(j, ROWS)], own_sem.at[chunks])
+    for q in range(chunks):
+        own_copy(q).start()
+    own_marks.start()
+    meet(z, j, along, across)
+
+    def cross(q, o, landing):
+        other = (j + o) % PLANE
+        return send(
+            pg.at[q, span(other, ROWS)],
+            back.at[q, span(landing, ROWS)],
+            x_send.at[q, o],
+            x_recv.at[q, o],
+            across(other),
+        )
+
+    def mark(o, landing):
+        other = (j + o) % PLANE
+        return send(
+            sc.at[span(other, ROWS)],
+            marks.at[span(landing, ROWS)],
+            mark_send.at[o],
+            mark_recv.at[o],
+            across(other),
+        )
+
+    def start_cross(q, carry):
+        for o in range(1, PLANE):
+            cross(q, o, j).start()
+        return carry
+
+    lax.fori_loop(0, chunks, start_cross, 0)
+    for o in range(1, PLANE):
+        mark(o, j).start()
+    for q in range(chunks):
+        own_copy(q).wait()
+    own_marks.wait()
+
+    def hop(q, way, step):
+        rows = slice(0, count)
+        if step == 0:
+            rows = slice(way * (count // 2), (way + 1) * (count // 2))
+        return send(
+            leaving.at[q, way, step, rows],
+            landed.at[q, way, step, rows],
+            z_send.at[q, way, step],
+            z_recv.at[q, way, step],
+            ahead if way == 0 else behind,
+        )
+
+    def target(way, step):
+        if way == 0:
+            return (z + NZ // 2 - step) % NZ
+        return (z + NZ // 2 + step) % NZ
+
+    def step(i, carry):
+        @pl.when(i < chunks)
+        def _():
+            q = i
+            for o in range(1, PLANE):
+                cross(q, o, (j + PLANE - o) % PLANE).wait_recv()
+
+            def add(t, carry):
+                cols = span(t, 2 * count)
+                part[q, cols, :] = dot(choose[:, cols], back[q], TN)
+                return carry
+
+            lax.fori_loop(0, NZ // 2, add, 0)
+            for way in range(2):
+                size = count // 2
+                start = target(way, 0) * count + way * size
+                rows = pl.ds(pl.multiple_of(start, size), size)
+                leaving[q, way, 0, way * size : (way + 1) * size, :] = part[q, rows, :].astype(jnp.bfloat16)
+                hop(q, way, 0).start()
+
+        for s in range(1, NZ // 2):
+            q = i - s
+
+            @pl.when((q >= 0) & (q < chunks))
+            def _():
+                for way in range(2):
+                    hop(q, way, s - 1).wait_recv()
+                    mine = part[q, span(target(way, s), count), :]
+                    if s == 1:
+                        size = count // 2
+                        near = slice(way * size, (way + 1) * size)
+                        far = slice((1 - way) * size, (2 - way) * size)
+                        more = landed[q, way, 0, near, :].astype(jnp.float32)
+                        leaving[q, way, 1, near, :] = (mine[near] + more).astype(jnp.bfloat16)
+                        leaving[q, way, 1, far, :] = mine[far].astype(jnp.bfloat16)
+                    else:
+                        more = landed[q, way, s - 1].astype(jnp.float32)
+                        leaving[q, way, s] = (mine + more).astype(jnp.bfloat16)
+                    hop(q, way, s).start()
+
+        q = i - NZ // 2
+
+        @pl.when(q >= 0)
+        def _():
+            total = part[q, span(z, count), :]
+            for way in range(2):
+                hop(q, way, last).wait_recv()
+                total = total + landed[q, way, last].astype(jnp.float32)
+            tg[:, pl.ds(pl.multiple_of(q * width, width), width)] = total.astype(jnp.bfloat16)
+
+        @pl.when(i == chunks - 1)
+        def _():
+            for o in range(1, PLANE):
+                mark(o, (j + PLANE - o) % PLANE).wait_recv()
+            spread = dot(marks[...], choose[...], TN)
+            both = spread[:PLANE] + spread[PLANE : 2 * PLANE]
+            for source in range(NZ):
+                sums[source] = both[:, source * count : (source + 1) * count]
+            own_sum().start()
+            for k in range(1, NZ):
+                summed(k, z).start()
+
+        return carry
+
+    def own_sum():
+        return pltpu.make_async_copy(sums.at[z], score.at[z], sum_send.at[0])
+
+    def summed(k, landing):
+        other = (z + k) % NZ
+        return send(sums.at[other], score.at[landing], sum_send.at[k], sum_recv.at[k], along(other))
+
+    lax.fori_loop(0, chunks + NZ // 2, step, 0)
+
+    def finish(q, carry):
+        for o in range(1, PLANE):
+            cross(q, o, j).wait_send()
+        for way in range(2):
+            for s in range(NZ // 2):
+                hop(q, way, s).wait_send()
+        return carry
+
+    lax.fori_loop(0, chunks, finish, 0)
+    own_sum().wait()
+    for o in range(1, PLANE):
+        mark(o, j).wait_send()
+    for k in range(1, NZ):
+        summed(k, z).wait_send()
+        summed(k, (z + NZ - k) % NZ).wait_recv()
+
+
+def give_back(pg, sc, choose, count):
+    chunks, slots, width = pg.shape
+    f32, bf16 = jnp.float32, jnp.bfloat16
+    dma = pltpu.SemaphoreType.DMA
+    anywhere = pl.BlockSpec(memory_space=pl.ANY)
+    vmem = pl.BlockSpec(memory_space=pltpu.VMEM)
+    return pl.pallas_call(
+        return_kernel,
+        in_specs=[anywhere, anywhere, vmem],
+        out_specs=[vmem, anywhere],
+        out_shape=[
+            jax.ShapeDtypeStruct((count, chunks * width), bf16),
+            jax.ShapeDtypeStruct((NZ, PLANE, count), f32),
+        ],
+        scratch_shapes=[
+            pltpu.VMEM((chunks, slots, width), bf16),
+            pltpu.VMEM(sc.shape, bf16),
+            pltpu.VMEM((chunks, NZ * count, width), f32),
+            pltpu.VMEM((chunks, 2, NZ // 2, count, width), bf16),
+            pltpu.VMEM((chunks, 2, NZ // 2, count, width), bf16),
+            pltpu.VMEM((NZ, PLANE, count), f32),
+            dma((chunks + 1,)),
+            dma((chunks, PLANE)),
+            dma((chunks, PLANE)),
+            dma((PLANE,)),
+            dma((PLANE,)),
+            dma((chunks, 2, NZ // 2)),
+            dma((chunks, 2, NZ // 2)),
+            dma((NZ,)),
+            dma((NZ,)),
+        ],
+        compiler_params=pltpu.CompilerParams(
+            collective_id=1, has_side_effects=True, vmem_limit_bytes=56 << 20
+        ),
+        cost_estimate=pl.CostEstimate(flops=2 * slots * NZ * count * chunks * width, bytes_accessed=150 << 20, transcendentals=0),
+    )(pg, sc, choose)
 
 
 def move_state(own_blocks, moments, layout_one, partner, n):
@@ -177,25 +605,18 @@
     named = jnp.any(picks, axis=2)
     before = jnp.tril(jnp.ones((count, count), bf16), -1)
     rank = dot(named.astype(bf16), before, NT)
-    rank = jnp.where(named, rank, -1.0)
     weight = jnp.sum(jnp.where(picks, route_weights[None].astype(f32), 0.0), axis=2)
-    slots = lax.broadcasted_iota(jnp.int32, (1, CAP, 1), 1).astype(f32)
-    choose = rank[:, None, :] == slots
-    take = choose.astype(bf16).reshape(n * CAP, count)
-    scale = jnp.where(choose, weight[:, None, :], 0.0).astype(bf16).reshape(n * CAP, count)
-    send_x = dot(take, tokens).astype(bf16).reshape(n, CAP, width)
-    send_s = dot(scale, out_grad).astype(bf16).reshape(n, CAP, width)
-    xs = lax.all_to_all(send_x, "expert", split_axis=0, concat_axis=0, tiled=True)
-    ss = lax.all_to_all(send_s, "expert", split_axis=0, concat_axis=0, tiled=True)
-    pg, sc, wg = expert_compute(
-        layout_one, xs.reshape(1, n * CAP, width), ss.reshape(1, n * CAP, width), mats, 448
-    )
-    back = jnp.concatenate([pg[0], sc], axis=1).reshape(n, CAP, width + BLK)
-    back = lax.all_to_all(back, "expert", split_axis=0, concat_axis=0, tiled=True)
-    back = back.reshape(n * CAP, width + BLK)
-    token_grad = dot(take, back[:, :width], TN).astype(bf16)
-    score_rows = back[:, width].astype(f32) + back[:, width + 8].astype(f32)
-    score = jnp.sum(jnp.where(choose, score_rows.reshape(n, CAP, 1), 0.0), axis=1)
+    z, j, _, _ = peers()
+    slot = jnp.where(named, rank + (z * CAP).astype(f32), -1.0)
+
+    def by_plane(a):
+        return a.reshape(NX, NZ, NCORE, count).transpose(1, 0, 2, 3).reshape(NZ, PLANE, count)
+
+    meta = jnp.concatenate([by_plane(slot), by_plane(weight)], axis=1).astype(bf16)
+    xs, choose = dispatch(tokens, out_grad, meta, 8)
+    pg, sc, wg = expert_compute(layout_one, j.reshape(1), xs, mats, 448)
+    token_grad, score = give_back(pg, sc, choose, count)
+    score = score.reshape(NZ, NX, NCORE, count).transpose(1, 0, 2, 3).reshape(n, count)
     score = jnp.sum(jnp.where(picks, score[:, :, None], 0.0), axis=0)
     route_grad = (score / route_weights.astype(f32)).astype(bf16)
 

time: 448 us -> 357 us (0.80)
  waiting for transfers between devices: 298 us -> 56.3 us
  Pallas kernels: 26.6 us -> 232 us
  local copies, waits for them, and re-layouts: 44.8 us -> 10.7 us
  starting transfers between devices: 39.9 us -> 15 us
  blocking collectives: 0 us -> 23.4 us
  matrix products: 9.62 us -> 0.2 us
  other arithmetic: 13.4 us -> 5.12 us
    pallas_call x0 -> x2, Pallas kernels: none -> 205 us  [the longest x1 117 us: dispatch(): pl.pallas_call(dispatch_kernel, in_specs=[anywhere, anywhere, anywhere],...]
    all_to_all x4 -> x0, waiting for transfers between devices: 192 us -> none  [the longest x1 88.5 us: body(): lax.all_to_all(send_x, 'expert', split_axis=0, concat_axis=0, tiled=True)]
    all_gather x1, waiting for transfers between devices: 43.9 us -> 0.01 us  [body(): gathered = lax.all_gather(updated, 'dp', axis=2, tiled=True)]
    reshape x5 -> x2, local copies, waits for them, and re-layouts: 30 us -> 0.8 us  [the longest x1 0.77 us: body(): score.reshape(NZ, NX, NCORE, count).transpose(1, 0, 2, 3).reshape(n, count)]
    all_to_all x4 -> x0, starting transfers between devices: 24.9 us -> none  [the longest x1 6.47 us: body(): lax.all_to_all(send_s, 'expert', split_axis=0, concat_axis=0, tiled=True)]
    all_to_all x0 -> x1, blocking collectives: none -> 23.4 us  [move_state(): lax.all_to_all(spread[partner], 'expert', split_axis=0, concat_axis=0, ti...]
    dot_general x4 -> x1, matrix products: 9.62 us -> 0.2 us  [dot(): return lax.dot_general(a, b, dims, preferred_element_type=jnp.float32)]
    concatenate x2 -> x0, local copies, waits for them, and re-layouts: 6.99 us -> none  [body(): back = jnp.concatenate([pg[0], sc], axis=1).reshape(n, CAP, width + BLK)]
  transfers between devices with their start and end apart: 8 -> 4, of which waited for: 7 -> 2; matrix products, arithmetic and copies ran while one was open for 8% -> 1% of each run, Pallas kernels for 0% -> 58%
where the time goes in v2:
time: 357 us
  Pallas kernels  232 us (65%)
  waiting for transfers between devices  56.3 us (16%)
  blocking collectives  23.4 us (7%)
  starting transfers between devices  15 us (4%)
  between operations  14 us (4%)
  local copies, waits for them, and re-layouts  10.7 us (3%)
  other arithmetic  5.12 us (1%)
    pallas_call x1, Pallas kernels, dispatch(): pl.pallas_call(dispatch_kernel, in_specs=[anywhere, anywhere, anywhere],...  117 us
    pallas_call x1, Pallas kernels, give_back(): pl.pallas_call(return_kernel, in_specs=[anywhere, anywhere, vmem], out_sp...  88 us
    reduce_scatter x1, waiting for transfers between devices, body(): shard = lax.psum_scatter(wg, 'dp', scatter_dimension=2, tiled=True)  39 us
    pallas_call x1, Pallas kernels, expert_compute(): pl.pallas_call(expert_kernel, grid_spec=pltpu.PrefetchScalarGridSpec(num_...  26.6 us
    all_to_all x1, blocking collectives, move_state(): lax.all_to_all(spread[partner], 'expert', split_axis=0, concat_axis=0, ti...  23.4 us
    all_to_all x1, waiting for transfers between devices, move_state(): lax.all_to_all(state, 'expert', split_axis=0, concat_axis=0, tiled=True)  17.2 us
    all_to_all x1, starting transfers between devices, move_state(): lax.all_to_all(state, 'expert', split_axis=0, concat_axis=0, tiled=True)  14.8 us
  transfers between devices with their start and end apart: 4, of which 2 were waited for; matrix products, arithmetic and copies ran while one was open for 1% of the time, Pallas kernels for 58%

profile of v2, /device:TPU:1, one launch (start us, length us, event | category | flops | bytes accessed | tf_op | source)
XLA Modules:
  0.0 356.6 jit_solution(15764932987564165623)
XLA Ops:
  7.2 0.0 copy-start
  7.2 0.8 convert.18
  8.0 0.1 copy.22
  8.1 0.1 reshape_squeeze.7
  8.2 1.0 fusion.2
  9.2 0.0 copy-start.4
  9.2 0.0 copy-done
  9.3 0.7 constant_dynamic-update-slice_fusion.3
  10.0 0.7 constant_dynamic-update-slice_fusion.2
  10.6 0.7 constant_dynamic-update-slice_fusion.1
  11.3 0.6 constant_dynamic-update-slice_fusion
  11.9 0.6 broadcast_dynamic-update-slice_fusion
  12.5 14.8 %all-to-all-start = ((bf16[64,32,128]{2,1,0:T(8,128)(2,1)}), bf16[64,32,128]{2,1,0:T(8,128)(2,1)S(1)}, u32[]{:S(2)}, u32[]{:S(2)}) async-start(bf16[64,32,128]{2,1,0:T(8,128)(2,1)} %bitcast.3), calls=%async_computation | async-start | bytes 1048576 | tf_op jit(solution)/shard_map/all_to_all | solution.py:580
  27.4 0.0 all-gather.3.cloned.1.call-start
  27.4 0.0 copy-done.4
  27.5 0.0 copy-start.3
  27.5 0.0 copy-start.2
  27.5 17.2 %all-to-all-done = bf16[64,32,128]{2,1,0:T(8,128)(2,1)S(1)} async-done(((bf16[64,32,128]{2,1,0:T(8,128)(2,1)}), bf16[64,32,128]{2,1,0:T(8,128)(2,1)S(1)}, u32[]{:S(2)}, u32[]{:S(2)}) %all-to-all-start) | async-done | bytes 524320 | tf_op jit(solution)/shard_map/all_to_all | solution.py:580
  44.7 0.7 gather_fusion
  45.4 23.4 %all_to_all.10 = bf16[64,32,128]{2,1,0:T(8,128)(2,1)S(1)} all-to-all(bf16[64,32,128]{2,1,0:T(8,128)(2,1)S(1)} %gather_fusion), channel_id=1, replica_groups=mesh['dp'=8,'expert'=64] {'expert'}, dimensions={0} | all-to-all | bytes 1048576 | tf_op jit(solution)/shard_map/all_to_all | solution.py:581
  68.8 0.7 slice.27
  69.4 0.0 all-gather.3.cloned.1.call-update
  69.5 0.0 reduce-scatter.2.cloned.1.call-start
  69.5 0.0 copy-done.3
  69.6 0.0 copy-done.2
  69.6 0.1 compare_reduce_fusion
  69.7 0.2 fusion.1
  69.9 0.1 fusion.3
  70.1 0.6 pad_maximum_fusion.meta
  70.7 117.3 %shard_map.111 = (bf16[8,896,512]{2,1,0:T(8,128)(2,1)}, bf16[896,1024]{1,0:T(8,128)(2,1)}) custom-call(bf16[128,2048]{1,0:T(8,128)(2,1)} %tok.1, bf16[128,2048]{1,0:T(8,128)(2,1)} %og.1, bf16[8,16,128]{2,1,0:T(8,128)(2,1)} %pad_maximum_fusion.meta), custom_call_target="tpu_custom_call" | custom-call | flops 7516192768 | bytes 314572800 | tf_op jit(solution)/shard_map/pallas_call | solution.py:334
  188.0 0.7 reshape.83.lay
  188.7 0.0 all-gather.3.cloned.1.call-done.w_ref
  188.7 26.6 %shard_map.112 = (bf16[4,896,512]{2,1,0:T(8,128)(2,1)}, bf16[896,128]{1,0:T(8,128)(2,1)}, f32[3,12,128,128]{3,2,1,0:T(8,128)}) custom-call(s32[3,12,2]{2,1,0:T(8,128)} %reshape.83.lay, s32[1]{0:T(128)} %bitcast.6.place_ref, bf16[8,896,512]{2,1,0:T(8,128)(2,1)} %get-tuple-element.11.x_ref.s_ref, bf16[8,896,512]{2,1,0:T(8,128)(2,1)} %get-tuple-element.11.x_ref.s_ref, ...), custom_call_target="tpu_custom_call" | custom-call | flops 2818572288 | bytes 14548992 | tf_op jit(solution)/shard_map/pallas_call | solution.py:97
  215.3 0.0 copy-start.1
  215.3 0.0 reduce-scatter.2.cloned.1.call-update
  215.3 0.0 all-gather.5.cloned.1.call-start
  215.4 39.0 %reduce-scatter.2.cloned.1.call-done = f32[3,12,16,128]{3,2,1,0:T(8,128)} async-done(((f32[3,12,128,128]{3,2,1,0:T(8,128)}), f32[3,12,16,128]{3,2,1,0:T(8,128)}) %reduce-scatter.2.cloned.1.call-update) | async-done | bytes 294928 | tf_op jit(solution)/shard_map/reduce_scatter | solution.py:623
  254.5 0.0 copy-done.1
  254.5 1.8 add_bitcast_fusion
  256.2 0.0 all-gather.5.cloned.1.call-update
  256.3 88.0 %shard_map.113 = (bf16[128,2048]{1,0:T(8,128)(2,1)}, f32[8,8,128]{2,1,0:T(8,128)}) custom-call(bf16[4,896,512]{2,1,0:T(8,128)(2,1)} %get-tuple-element.12.pg, bf16[896,128]{1,0:T(8,128)(2,1)} %get-tuple-element.13.sc, bf16[896,1024]{1,0:T(8,128)(2,1)} %get-tuple-element.14.choose), custom_call_target="tpu_custom_call" | custom-call | flops 3758096384 | bytes 157286400 | tf_op jit(solution)/shard_map/pallas_call | solution.py:530
  344.3 0.8 copy.25
  345.0 0.1 fusion.4
  345.1 0.6 divide_convert_fusion
  345.7 0.0 all-gather.5.cloned.1.call-done
  345.7 1.9 copy.32
  347.6 2.4 copy.33
  (10 shorter events, 0.1 us)
Async XLA Ops:
  7.2 2.1 copy-start
  9.2 18.2 %copy-start.4 = (s32[64]{0:T(128)S(1)}, s32[64]{0:T(128)}, u32[]{:S(2)}) copy-start(s32[64]{0:T(128)} %param.15) | copy-start | bytes 772
  12.5 32.2 %all-to-all-start = ((bf16[64,32,128]{2,1,0:T(8,128)(2,1)}), bf16[64,32,128]{2,1,0:T(8,128)(2,1)S(1)}, u32[]{:S(2)}, u32[]{:S(2)}) async-start(bf16[64,32,128]{2,1,0:T(8,128)(2,1)} %bitcast.3), calls=%async_computation | async-start | bytes 1048576 | tf_op jit(solution)/shard_map/all_to_all | solution.py:580
  27.4 161.3 %all-gather.3.cloned.1.call-start = ((), (), s32[]{:S(2)}) async-start(), calls=%async_computation.3 | async-start | bytes 1327104 | tf_op jit(solution)/shard_map/all_gather | solution.py:602
  27.5 42.1 %copy-start.3 = (bf16[128,6]{0,1:T(8,128)(2,1)S(1)}, bf16[128,6]{0,1:T(8,128)(2,1)}, u32[]{:S(2)}) copy-start(bf16[128,6]{0,1:T(8,128)(2,1)} %param.11) | copy-start | bytes 4612
  27.5 42.1 %copy-start.2 = (s32[128,6]{0,1:T(8,128)S(1)}, s32[128,6]{0,1:T(8,128)}, u32[]{:S(2)}) copy-start(s32[128,6]{0,1:T(8,128)} %param.10) | copy-start | bytes 9220
  69.5 185.0 %reduce-scatter.2.cloned.1.call-start = ((), (), s32[]{:S(2)}) async-start(), calls=%async_computation.4 | async-start | bytes 2654208 | tf_op jit(solution)/shard_map/reduce_scatter | solution.py:623
  215.3 39.2 %copy-start.1 = (bf16[18,32,128]{2,1,0:T(8,128)(2,1)S(1)}, bf16[18,32,128]{2,1,0:T(8,128)(2,1)}, u32[]{:S(2)}) copy-start(bf16[18,32,128]{2,1,0:T(8,128)(2,1)} %slice.27) | copy-start | bytes 442372
  215.3 130.4 %all-gather.5.cloned.1.call-start = ((), (), s32[]{:S(2)}) async-start(), calls=%async_computation.5 | async-start | bytes 1327104 | tf_op jit(solution)/shard_map/all_gather | solution.py:626
Sparse Core Ops, SparseCore 0:
  69.6 36.6 all-gather.2
  215.4 38.9 reduce-scatter.1
  257.0 43.3 all-gather.4

commit v3 on v2

--- a/solution.py
+++ b/solution.py
@@ -25,7 +25,7 @@
     return pl.ds(pl.multiple_of(i * BLK, BLK), BLK)
 
 
-def expert_kernel(lay, place_ref, x_ref, s_ref, w_ref, pg_ref, sc_ref, wg_ref, gate, up, hg, hid, gg, ug, acc):
+def expert_kernel(lay, place_ref, x_ref, s_ref, w_ref, pg_ref, sc_ref, out_ref, wg_ref, gate, up, hg, hid, gg, ug, acc):
     nb = w_ref.shape[1]
     rows = x_ref.shape[1]
     per = x_ref.shape[2] // BLK
@@ -65,7 +65,10 @@
     total = jnp.sum(score, axis=1, keepdims=True)
     high = total.astype(jnp.bfloat16).astype(jnp.float32)
     lane = lax.broadcasted_iota(jnp.int32, (rows, BLK), 1)
-    place = place_ref[0]
+    group = pl.program_id(0) * (rows // (NCORE * ROWS))
+    for k in range(1, rows // (NCORE * ROWS)):
+        group = group + (lax.broadcasted_iota(jnp.int32, (rows, BLK), 0) >= k * NCORE * ROWS).astype(jnp.int32)
+    place = jnp.where(group == 0, 0, NX - group) * NCORE + place_ref[0]
     sc_ref[...] = jnp.where(
         lane == place, high, jnp.where(lane == place + 8, total - high, 0.0)
     ).astype(jnp.bfloat16)
@@ -85,6 +88,13 @@
     for q in range(pg_ref.shape[0]):
         width = pg_ref.shape[2]
         pg_ref[q] = acc[:, q * width : (q + 1) * width].astype(jnp.bfloat16)
+
+    @pl.when(pl.program_id(0) == pl.num_programs(0) - 1)
+    def _():
+        share = out_ref.shape[2]
+        for y in range(out_ref.shape[0]):
+            for m in range(w_ref.shape[0]):
+                out_ref[y, m * nb : (m + 1) * nb] = wg_ref[m, :, y * share : (y + 1) * share, :].astype(jnp.bfloat16)
 
 
 def expert_compute(layout_one, place, xs, mats, tile):
@@ -107,9 +117,10 @@
             out_specs=[
                 row_spec,
                 pl.BlockSpec((tile, BLK), lambda i, lay, place: (i, 0)),
-                pl.BlockSpec((nm, nb, BLK, BLK), lambda i, lay, place: (0, 0, 0, 0)),
+                pl.BlockSpec((NY, nm * nb, BLK // NY, BLK), lambda i, lay, place: (0, 0, 0, 0)),
             ],
             scratch_shapes=[
+                pltpu.VMEM(mats.shape, f32),
                 pltpu.VMEM((tile, HID), f32),
                 pltpu.VMEM((tile, HID), f32),
                 pltpu.VMEM((tile, HID), f32),
@@ -122,7 +133,7 @@
         out_shape=[
             jax.ShapeDtypeStruct((nq, rows, width), bf16),
             jax.ShapeDtypeStruct((rows, BLK), bf16),
-            jax.ShapeDtypeStruct(mats.shape, f32),
+            jax.ShapeDtypeStruct((NY, nm * nb, BLK // NY, BLK), bf16),
         ],
         compiler_params=pltpu.CompilerParams(vmem_limit_bytes=56 << 20),
         cost_estimate=pl.CostEstimate(
@@ -133,36 +144,40 @@
     )(layout_one, place, xs, xs, mats)
 
 
-NX, NZ, NCORE = 4, 8, 2
+NX, NZ, NCORE, NY = 4, 8, 2, 8
 PLANE = NX * NCORE
 ROWS = NZ * CAP
 MESH = pl.DeviceIdType.MESH
 
 
-def position():
-    me = lax.axis_index("expert")
-    return lax.axis_index("dp"), me // (NZ * NCORE), (me // NCORE) % NZ, me % NCORE
-
-
-def peers():
-    dp, x, z, core = position()
-
-    def along(other):
-        return (dp, x * (NZ * NCORE) + other * NCORE + core)
-
-    def across(other):
-        return (dp, (other // NCORE) * (NZ * NCORE) + z * NCORE + other % NCORE)
-
-    return z, x * NCORE + core, along, across
-
-
-def meet(z, j, along, across):
-    barrier = pltpu.get_barrier_semaphore()
-    for k in range(1, NZ):
-        pl.semaphore_signal(barrier, inc=1, device_id=along((z + k) % NZ), device_id_type=MESH)
-    for k in range(1, PLANE):
-        pl.semaphore_signal(barrier, inc=1, device_id=across((j + k) % PLANE), device_id_type=MESH)
-    pl.semaphore_wait(barrier, NZ + PLANE - 2)
+class Place:
+    def __init__(self):
+        me = lax.axis_index("expert")
+        self.y = lax.axis_index("dp")
+        self.me = me
+        self.x = me // (NZ * NCORE)
+        self.z = (me // NCORE) % NZ
+        self.core = me % NCORE
+
+    def along(self, dz):
+        return (self.y, self.x * (NZ * NCORE) + (self.z + dz) % NZ * NCORE + self.core)
+
+    def across(self, dx, core):
+        return (self.y, (self.x + dx) % NX * (NZ * NCORE) + self.z * NCORE + core)
+
+    def over(self, dy):
+        return ((self.y + dy) % NY, self.me)
+
+    def meet(self, with_y):
+        others = [self.along(k) for k in range(1, NZ)]
+        others += [self.across(dx, c) for dx in range(1, NX) for c in range(NCORE)]
+        others.append(self.across(0, 1 - self.core))
+        if with_y:
+            others += [self.over(k) for k in range(1, NY)]
+        barrier = pltpu.get_barrier_semaphore()
+        for other in others:
+            pl.semaphore_signal(barrier, inc=1, device_id=other, device_id_type=MESH)
+        pl.semaphore_wait(barrier, len(others))
 
 
 def send(src, dst, send_sem, recv_sem, device):
@@ -180,15 +195,98 @@
     return pl.ds(pl.multiple_of(i * size, size), size)
 
 
+class Exchange:
+    far = NX // 2
+
+    def __init__(self, place, src, dst, relay, own_sem, send_sem, recv_sem, relay_send, relay_recv):
+        self.place, self.src, self.dst, self.relay = place, src, dst, relay
+        self.own_sem, self.send_sem, self.recv_sem = own_sem, send_sem, recv_sem
+        self.relay_send, self.relay_recv = relay_send, relay_recv
+
+    def direct(self, q, dx, core):
+        number = dx * NCORE + core
+        landing = (NX - dx) % NX * NCORE + self.place.core
+        return send(
+            self.src.at[q, span(number, ROWS)],
+            self.dst.at[q, span(landing, ROWS)],
+            self.send_sem.at[q, number],
+            self.recv_sem.at[q, landing],
+            self.place.across(dx, core),
+        )
+
+    def first_leg(self, q, way):
+        number = self.far * NCORE + way
+        return send(
+            self.src.at[q, span(number, ROWS)],
+            self.relay.at[q, way],
+            self.send_sem.at[q, number],
+            self.relay_recv.at[q, way],
+            self.place.across(1 if way == 0 else NX - 1, self.place.core),
+        )
+
+    def second_leg(self, q, way):
+        landing = self.far * NCORE + self.place.core
+        return send(
+            self.relay.at[q, way],
+            self.dst.at[q, span(landing, ROWS)],
+            self.relay_send.at[q, way],
+            self.recv_sem.at[q, landing],
+            self.place.across(1 if way == 0 else NX - 1, way),
+        )
+
+    def own(self, q):
+        rows = span(self.place.core, ROWS)
+        return pltpu.make_async_copy(self.src.at[q, rows], self.dst.at[q, rows], self.own_sem.at[q])
+
+    def start(self, q, steps=(2, 1, 3, 0)):
+        for dx in steps:
+            if dx == 0:
+                self.direct(q, 0, 1 - self.place.core).start()
+                self.own(q).start()
+            elif dx == self.far and self.relay is not None:
+                for way in range(2):
+                    self.first_leg(q, way).start()
+            else:
+                for core in range(NCORE):
+                    self.direct(q, dx, core).start()
+
+    def forward(self, q):
+        for way in range(2):
+            self.first_leg(q, way).wait_recv()
+            self.second_leg(q, way).start()
+
+    def arrive(self, q):
+        def one(landing):
+            part = self.dst.at[q, span(landing, ROWS)]
+            send(part, part, self.send_sem.at[q, landing], self.recv_sem.at[q, landing], self.place.across(1, 0)).wait_recv()
+
+        for dx in range(1, NX):
+            for core in range(NCORE):
+                one(dx * NCORE + core)
+        one(1 - self.place.core)
+        self.own(q).wait()
+
+    def leave(self, q):
+        for dx in range(1, NX):
+            for core in range(NCORE):
+                if dx == self.far and self.relay is not None:
+                    self.first_leg(q, core).wait_send()
+                    self.second_leg(q, core).wait_send()
+                else:
+                    self.direct(q, dx, core).wait_send()
+        self.direct(q, 0, 1 - self.place.core).wait_send()
+
+
 def dispatch_kernel(
-    tok, og, meta, xs, chosen, ring, picked, choose, notes,
-    own_sem, notes_send, notes_recv, ring_send, ring_recv, out_send, out_recv, out_own, keep_sem,
+    tok, og, meta, xs, chosen, ring, picked, choose, notes, relay,
+    own_sem, notes_send, notes_recv, ring_send, ring_recv, out_own, out_send, out_recv, relay_send, relay_recv, keep_sem,
 ):
     count = tok.shape[0]
     chunks, _, width = ring.shape
     half = chunks // 2
-    z, j, along, across = peers()
-    ahead, behind = along((z + 1) % NZ), along((z + NZ - 1) % NZ)
+    place = Place()
+    z = place.z
+    out = Exchange(place, picked, xs, relay, out_own, out_send, out_recv, relay_send, relay_recv)
 
     def own_copy(q):
         src = tok if q < half else og
@@ -202,15 +300,11 @@
         own_copy(q).start()
     own_notes = pltpu.make_async_copy(meta.at[z], notes.at[z], keep_sem.at[1])
     own_notes.start()
-    meet(z, j, along, across)
+    place.meet(False)
 
     def note(k, source):
         return send(
-            meta.at[(z + k) % NZ],
-            notes.at[source],
-            notes_send.at[k],
-            notes_recv.at[k],
-            along((z + k) % NZ),
+            meta.at[(z + k) % NZ], notes.at[source], notes_send.at[k], notes_recv.at[k], place.along(k)
         )
 
     for k in range(1, NZ):
@@ -231,22 +325,11 @@
             start = start + way * rows
         block = ring.at[q, pl.ds(pl.multiple_of(start, rows), rows)]
         return send(
-            block, block, ring_send.at[q, way, step], ring_recv.at[q, way, step], ahead if way == 0 else behind
-        )
-
-    def out(q, other, landing):
-        step = (other + PLANE - j) % PLANE
-        return send(
-            picked.at[q, span(other, ROWS)],
-            xs.at[q, span(landing, ROWS)],
-            out_send.at[q, step],
-            out_recv.at[q, step],
-            across(other),
-        )
-
-    def own_out(q):
-        return pltpu.make_async_copy(
-            picked.at[q, span(j, ROWS)], xs.at[q, span(j, ROWS)], out_own.at[q]
+            block,
+            block,
+            ring_send.at[q, way, step],
+            ring_recv.at[q, way, step],
+            place.along(1 if way == 0 else NZ - 1),
         )
 
     def keep():
@@ -282,40 +365,32 @@
                     hop(q, way, s, False).start()
 
         pl.when(i == 1)(build)
+
+        @pl.when((i > NZ // 2) & (i <= NZ // 2 + chunks))
+        def _():
+            out.forward(i - NZ // 2 - 1)
+
         q = i - NZ // 2
 
-        @pl.when(q >= 0)
+        @pl.when((q >= 0) & (q < chunks))
         def _():
             for way in range(2):
                 hop(q, way, NZ // 2 - 1, True).wait_recv()
-
-            def part(h, carry):
-                rows = span(h, PLANE // 2 * ROWS)
+            for h in (1, 0):
+                rows = slice(h * (PLANE // 2) * ROWS, (h + 1) * (PLANE // 2) * ROWS)
                 picked[q, rows, :] = dot(choose[q // half, rows, :], ring[q]).astype(jnp.bfloat16)
-                for o in range(PLANE // 2):
-                    other = h * (PLANE // 2) + o
-
-                    @pl.when(other != j)
-                    def _():
-                        out(q, other, j).start()
-
-                return carry
-
-            lax.fori_loop(0, 2, part, 0)
-            own_out(q).start()
+                out.start(q, (2, 3) if h else (1, 0))
 
         return carry
 
-    lax.fori_loop(0, chunks + NZ // 2, step, 0)
+    lax.fori_loop(0, chunks + NZ // 2 + 1, step, 0)
 
     def finish(q, carry):
         for way in range(2):
             for s in range(NZ // 2):
                 hop(q, way, s, False).wait_send()
-        for o in range(1, PLANE):
-            out(q, (j + o) % PLANE, j).wait_send()
-            out(q, (j + o) % PLANE, (j + PLANE - o) % PLANE).wait_recv()
-        own_out(q).wait()
+        out.leave(q)
+        out.arrive(q)
         return carry
 
     lax.fori_loop(0, chunks, finish, 0)
@@ -344,75 +419,87 @@
             pltpu.VMEM((chunks, slots, width), bf16),
             pltpu.VMEM((2, slots, NZ * count), bf16),
             pltpu.VMEM(meta.shape, bf16),
+            pltpu.VMEM((chunks, 2, ROWS, width), bf16),
             dma((chunks,)),
             dma((NZ,)),
             dma((NZ,)),
             dma((chunks, 2, NZ // 2)),
             dma((chunks, 2, NZ // 2)),
+            dma((chunks,)),
             dma((chunks, PLANE)),
             dma((chunks, PLANE)),
-            dma((chunks,)),
+            dma((chunks, 2)),
+            dma((chunks, 2)),
             dma((2,)),
         ],
         compiler_params=pltpu.CompilerParams(
             collective_id=0, has_side_effects=True, vmem_limit_bytes=56 << 20
         ),
-        cost_estimate=pl.CostEstimate(flops=2 * slots * NZ * count * 2 * features, bytes_accessed=300 << 20, transcendentals=0),
+        cost_estimate=pl.CostEstimate(
+            flops=2 * slots * NZ * count * 2 * features, bytes_accessed=300 << 20, transcendentals=0
+        ),
     )(tokens, grads, meta)
 
 
 def return_kernel(
-    pg, sc, choose, tg, score, back, marks, part, leaving, landed, sums,
-    own_sem, x_send, x_recv, mark_send, mark_recv, z_send, z_recv, sum_send, sum_recv,
+    pg, sc, choose, wg, own_blocks, old_moment, tg, score, moment, blocks,
+    back, marks, relay, part, leaving, landed, sums, grads,
+    x_own, x_send, x_recv, relay_send, relay_recv, mark_own, mark_send, mark_recv,
+    z_send, z_recv, sum_send, sum_recv, y_send, y_recv, share_send, share_recv,
 ):
     chunks, slots, width = pg.shape
     count = tg.shape[0]
     last = NZ // 2 - 1
-    z, j, along, across = peers()
-    ahead, behind = along((z + 1) % NZ), along((z + NZ - 1) % NZ)
-
-    def own_copy(q):
-        return pltpu.make_async_copy(
-            pg.at[q, span(j, ROWS)], back.at[q, span(j, ROWS)], own_sem.at[q]
+    place = Place()
+    z, y = place.z, place.y
+    cross = Exchange(place, pg, back, relay, x_own, x_send, x_recv, relay_send, relay_recv)
+    mark = Exchange(place, sc, marks, None, mark_own, mark_send, mark_recv, None, None)
+
+    own_grads = pltpu.make_async_copy(wg.at[y], grads.at[y], y_send.at[0])
+    own_grads.start()
+    place.meet(True)
+    cross.start(0)
+
+    def grad(k, landing):
+        return send(wg.at[(y + k) % NY], grads.at[landing], y_send.at[k], y_recv.at[k], place.over(k))
+
+    for k in range(1, NY):
+        grad(k, y).start()
+    mark.start(0)
+    cross.start(1)
+    cross.forward(0)
+
+    def share(way, step, arriving):
+        if way == 0:
+            source = (y + 2 * NY - step - (1 if arriving else 0)) % NY
+        else:
+            source = (y + step + (1 if arriving else 0)) % NY
+        n = blocks.shape[0]
+        which = slice(0, n)
+        if step == NY // 2 - 1:
+            which = slice(way * (n // 2), (way + 1) * (n // 2))
+        rows = blocks.at[which, span(source, BLK // NY)]
+        return send(
+            rows, rows, share_send.at[way, step], share_recv.at[way, step], place.over(1 if way == 0 else NY - 1)
         )
 
-    own_marks = pltpu.make_async_copy(sc.at[span(j, ROWS)], marks.at[span(j, ROWS)], own_sem.at[chunks])
-    for q in range(chunks):
-        own_copy(q).start()
-    own_marks.start()
-    meet(z, j, along, across)
-
-    def cross(q, o, landing):
-        other = (j + o) % PLANE
-        return send(
-            pg.at[q, span(other, ROWS)],
-            back.at[q, span(landing, ROWS)],
-            x_send.at[q, o],
-            x_recv.at[q, o],
-            across(other),
-        )
-
-    def mark(o, landing):
-        other = (j + o) % PLANE
-        return send(
-            sc.at[span(other, ROWS)],
-            marks.at[span(landing, ROWS)],
-            mark_send.at[o],
-            mark_recv.at[o],
-            across(other),
-        )
-
-    def start_cross(q, carry):
-        for o in range(1, PLANE):
-            cross(q, o, j).start()
-        return carry
-
-    lax.fori_loop(0, chunks, start_cross, 0)
-    for o in range(1, PLANE):
-        mark(o, j).start()
-    for q in range(chunks):
-        own_copy(q).wait()
-    own_marks.wait()
+    def update():
+        for k in range(1, NY):
+            grad(k, (y + NY - k) % NY).wait_recv()
+        own_grads.wait()
+
+        def one(b, carry):
+            total = DECAY * old_moment[b]
+            for source in range(NY):
+                total = total + grads[source, b].astype(jnp.float32)
+            moment[b] = total
+            fresh = own_blocks[b].astype(jnp.float32) - RATE * total
+            blocks[b, span(y, BLK // NY), :] = fresh.astype(jnp.bfloat16)
+            return carry
+
+        lax.fori_loop(0, blocks.shape[0], one, 0)
+        for way in range(2):
+            share(way, 0, False).start()
 
     def hop(q, way, step):
         rows = slice(0, count)
@@ -423,7 +510,7 @@
             landed.at[q, way, step, rows],
             z_send.at[q, way, step],
             z_recv.at[q, way, step],
-            ahead if way == 0 else behind,
+            place.along(1 if way == 0 else NZ - 1),
         )
 
     def target(way, step):
@@ -431,12 +518,17 @@
             return (z + NZ // 2 - step) % NZ
         return (z + NZ // 2 + step) % NZ
 
+    def own_sum():
+        return pltpu.make_async_copy(sums.at[z], score.at[z], sum_send.at[0])
+
+    def summed(k, landing):
+        return send(sums.at[(z + k) % NZ], score.at[landing], sum_send.at[k], sum_recv.at[k], place.along(k))
+
     def step(i, carry):
         @pl.when(i < chunks)
         def _():
             q = i
-            for o in range(1, PLANE):
-                cross(q, o, (j + PLANE - o) % PLANE).wait_recv()
+            cross.arrive(q)
 
             def add(t, carry):
                 cols = span(t, 2 * count)
@@ -481,11 +573,27 @@
                 total = total + landed[q, way, last].astype(jnp.float32)
             tg[:, pl.ds(pl.multiple_of(q * width, width), width)] = total.astype(jnp.bfloat16)
 
+        @pl.when(i + 2 < chunks)
+        def _():
+            cross.start(i + 2)
+
+        @pl.when(i + 1 < chunks)
+        def _():
+            cross.forward(i + 1)
+
+        pl.when(i == 2)(update)
+        for s in range(1, NY // 2):
+
+            @pl.when(i == 2 + s)
+            def _():
+                for way in range(2):
+                    share(way, s - 1, True).wait_recv()
+                    share(way, s, False).start()
+
         @pl.when(i == chunks - 1)
         def _():
-            for o in range(1, PLANE):
-                mark(o, (j + PLANE - o) % PLANE).wait_recv()
-            spread = dot(marks[...], choose[...], TN)
+            mark.arrive(0)
+            spread = dot(marks[0], choose[...], TN)
             both = spread[:PLANE] + spread[PLANE : 2 * PLANE]
             for source in range(NZ):
                 sums[source] = both[:, source * count : (source + 1) * count]
@@ -495,33 +603,30 @@
 
         return carry
 
-    def own_sum():
-        return pltpu.make_async_copy(sums.at[z], score.at[z], sum_send.at[0])
-
-    def summed(k, landing):
-        other = (z + k) % NZ
-        return send(sums.at[other], score.at[landing], sum_send.at[k], sum_recv.at[k], along(other))
-
     lax.fori_loop(0, chunks + NZ // 2, step, 0)
 
     def finish(q, carry):
-        for o in range(1, PLANE):
-            cross(q, o, j).wait_send()
+        cross.leave(q)
         for way in range(2):
             for s in range(NZ // 2):
                 hop(q, way, s).wait_send()
         return carry
 
     lax.fori_loop(0, chunks, finish, 0)
+    mark.leave(0)
     own_sum().wait()
-    for o in range(1, PLANE):
-        mark(o, j).wait_send()
     for k in range(1, NZ):
         summed(k, z).wait_send()
         summed(k, (z + NZ - k) % NZ).wait_recv()
-
-
-def give_back(pg, sc, choose, count):
+    for k in range(1, NY):
+        grad(k, y).wait_send()
+    for way in range(2):
+        share(way, NY // 2 - 1, True).wait_recv()
+        for s in range(NY // 2):
+            share(way, s, False).wait_send()
+
+
+def give_back(pg, sc, choose, wg, own_blocks, old_moment, count):
     chunks, slots, width = pg.shape
     f32, bf16 = jnp.float32, jnp.bfloat16
     dma = pltpu.SemaphoreType.DMA
@@ -529,34 +634,47 @@
     vmem = pl.BlockSpec(memory_space=pltpu.VMEM)
     return pl.pallas_call(
         return_kernel,
-        in_specs=[anywhere, anywhere, vmem],
-        out_specs=[vmem, anywhere],
+        in_specs=[anywhere, anywhere, vmem, anywhere, vmem, vmem],
+        out_specs=[vmem, anywhere, vmem, vmem],
         out_shape=[
             jax.ShapeDtypeStruct((count, chunks * width), bf16),
             jax.ShapeDtypeStruct((NZ, PLANE, count), f32),
+            jax.ShapeDtypeStruct(old_moment.shape, f32),
+            jax.ShapeDtypeStruct((wg.shape[1], BLK, BLK), bf16),
         ],
         scratch_shapes=[
             pltpu.VMEM((chunks, slots, width), bf16),
             pltpu.VMEM(sc.shape, bf16),
+            pltpu.VMEM((chunks, 2, ROWS, width), bf16),
             pltpu.VMEM((chunks, NZ * count, width), f32),
             pltpu.VMEM((chunks, 2, NZ // 2, count, width), bf16),
             pltpu.VMEM((chunks, 2, NZ // 2, count, width), bf16),
             pltpu.VMEM((NZ, PLANE, count), f32),
-            dma((chunks + 1,)),
+            pltpu.VMEM(wg.shape, bf16),
+            dma((chunks,)),
             dma((chunks, PLANE)),
             dma((chunks, PLANE)),
-            dma((PLANE,)),
-            dma((PLANE,)),
+            dma((chunks, 2)),
+            dma((chunks, 2)),
+            dma((1,)),
+            dma((1, PLANE)),
+            dma((1, PLANE)),
             dma((chunks, 2, NZ // 2)),
             dma((chunks, 2, NZ // 2)),
             dma((NZ,)),
             dma((NZ,)),
+            dma((NY,)),
+            dma((NY,)),
+            dma((2, NY // 2)),
+            dma((2, NY // 2)),
         ],
         compiler_params=pltpu.CompilerParams(
             collective_id=1, has_side_effects=True, vmem_limit_bytes=56 << 20
         ),
-        cost_estimate=pl.CostEstimate(flops=2 * slots * NZ * count * chunks * width, bytes_accessed=150 << 20, transcendentals=0),
-    )(pg, sc, choose)
+        cost_estimate=pl.CostEstimate(
+            flops=2 * slots * NZ * count * chunks * width, bytes_accessed=150 << 20, transcendentals=0
+        ),
+    )(pg, sc, choose, wg, own_blocks, old_moment)
 
 
 def move_state(own_blocks, moments, layout_one, partner, n):
@@ -601,30 +719,33 @@
     own, old_moment, layout_one = move_state(own, moments[0], layout[0], partner, n)
     mats = lax.all_gather(own, "dp", axis=2, tiled=True)
 
-    picks = expert_ids[None] == partner[:, None, None]
+    place = Place()
+    number = jnp.arange(n, dtype=jnp.int32)
+    where = (place.x + number // NCORE % NX) % NX * (NZ * NCORE) + number // PLANE * NCORE + number % NCORE
+    holds = partner[where]
+    picks = expert_ids[None] == holds[:, None, None]
     named = jnp.any(picks, axis=2)
     before = jnp.tril(jnp.ones((count, count), bf16), -1)
     rank = dot(named.astype(bf16), before, NT)
     weight = jnp.sum(jnp.where(picks, route_weights[None].astype(f32), 0.0), axis=2)
-    z, j, _, _ = peers()
-    slot = jnp.where(named, rank + (z * CAP).astype(f32), -1.0)
-
-    def by_plane(a):
-        return a.reshape(NX, NZ, NCORE, count).transpose(1, 0, 2, 3).reshape(NZ, PLANE, count)
-
-    meta = jnp.concatenate([by_plane(slot), by_plane(weight)], axis=1).astype(bf16)
+    slot = jnp.where(named, rank + (place.z * CAP).astype(f32), -1.0)
+    meta = jnp.concatenate(
+        [slot.reshape(NZ, PLANE, count), weight.reshape(NZ, PLANE, count)], axis=1
+    ).astype(bf16)
     xs, choose = dispatch(tokens, out_grad, meta, 8)
-    pg, sc, wg = expert_compute(layout_one, j.reshape(1), xs, mats, 448)
-    token_grad, score = give_back(pg, sc, choose, count)
-    score = score.reshape(NZ, NX, NCORE, count).transpose(1, 0, 2, 3).reshape(n, count)
-    score = jnp.sum(jnp.where(picks, score[:, :, None], 0.0), axis=0)
+    pg, sc, wg = expert_compute(layout_one, place.core.reshape(1), xs, mats, 448)
+    tiles = own.shape[0] * own.shape[1]
+    token_grad, score, moment, updated = give_back(
+        pg, sc[None], choose, wg, own.reshape(tiles, share, BLK), old_moment.reshape(tiles, share, BLK), count
+    )
+    score = jnp.sum(jnp.where(picks, score.reshape(n, count)[:, :, None], 0.0), axis=0)
     route_grad = (score / route_weights.astype(f32)).astype(bf16)
-
-    shard = lax.psum_scatter(wg, "dp", scatter_dimension=2, tiled=True)
-    moment = DECAY * old_moment + shard
-    updated = (own.astype(f32) - RATE * moment).astype(bf16)
-    gathered = lax.all_gather(updated, "dp", axis=2, tiled=True)
-    return token_grad, route_grad, gathered[None], moment[None]
+    return (
+        token_grad,
+        route_grad,
+        updated.reshape(blocks.shape),
+        moment.reshape(moments.shape),
+    )
 
 
 def solution(mesh):

time: 357 us -> 331 us (0.927)
  blocking collectives: 23.4 us -> 0 us
  waiting for transfers between devices: 56.3 us -> 34.5 us
  Pallas kernels: 232 us -> 243 us
  starting transfers between devices: 15 us -> 21.3 us
    reduce_scatter x1 -> x0, waiting for transfers between devices: 39 us -> none  [body(): shard = lax.psum_scatter(wg, 'dp', scatter_dimension=2, tiled=True)]
    all_to_all x1 -> x0, blocking collectives: 23.4 us -> none  [move_state(): lax.all_to_all(spread[partner], 'expert', split_axis=0, concat_axis=0, ti...]
    all_to_all x0 -> x1, waiting for transfers between devices: none -> 17.2 us  [move_state(): lax.all_to_all(spread[partner], 'expert', split_axis=0, concat_axis=0, ti...]
    pallas_call x1, Pallas kernels: 88 us -> 98.1 us  [give_back(): pl.pallas_call(return_kernel, in_specs=[anywhere, anywhere, vmem, anywher...]
    all_to_all x0 -> x1, starting transfers between devices: none -> 6.41 us  [move_state(): lax.all_to_all(spread[partner], 'expert', split_axis=0, concat_axis=0, ti...]
    unnamed x16 -> x17, local copies, waits for them, and re-layouts: 6.93 us -> 7.68 us
  transfers between devices with their start and end apart: 4 -> 3, of which waited for: 2 -> 2; matrix products, arithmetic and copies ran while one was open for 1% -> 1% of each run, Pallas kernels for 58% -> 36%
where the time goes in v3:
time: 331 us
  Pallas kernels  243 us (73%)
  waiting for transfers between devices  34.5 us (10%)
  starting transfers between devices  21.3 us (6%)
  between operations  14.2 us (4%)
  local copies, waits for them, and re-layouts  12.2 us (4%)
  other arithmetic  4.86 us (1%)
    pallas_call x1, Pallas kernels, dispatch(): pl.pallas_call(dispatch_kernel, in_specs=[anywhere, anywhere, anywhere],...  119 us
    pallas_call x1, Pallas kernels, give_back(): pl.pallas_call(return_kernel, in_specs=[anywhere, anywhere, vmem, anywher...  98.1 us
    pallas_call x1, Pallas kernels, expert_compute(): pl.pallas_call(expert_kernel, grid_spec=pltpu.PrefetchScalarGridSpec(num_...  26.2 us
    all_to_all x1, waiting for transfers between devices, move_state(): lax.all_to_all(state, 'expert', split_axis=0, concat_axis=0, tiled=True)  17.3 us
    all_to_all x1, waiting for transfers between devices, move_state(): lax.all_to_all(spread[partner], 'expert', split_axis=0, concat_axis=0, ti...  17.2 us
    all_to_all x1, starting transfers between devices, move_state(): lax.all_to_all(state, 'expert', split_axis=0, concat_axis=0, tiled=True)  14.8 us
    unnamed x17, local copies, waits for them, and re-layouts  7.68 us
  transfers between devices with their start and end apart: 3, of which 2 were waited for; matrix products, arithmetic and copies ran while one was open for 1% of the time, Pallas kernels for 36%

profile of v3, /device:TPU:1, one launch (start us, length us, event | category | flops | bytes accessed | tf_op | source)
XLA Modules:
  0.0 330.5 jit_solution(3221548013962245118)
XLA Ops:
  7.2 0.0 copy-start
  7.2 0.8 convert.14
  8.0 0.1 copy.18
  8.1 0.1 reshape_squeeze.7
  8.2 1.0 fusion.3
  9.2 0.0 copy-start.1
  9.2 0.0 copy-done
  9.3 0.7 constant_dynamic-update-slice_fusion.3
  10.0 0.7 constant_dynamic-update-slice_fusion.2
  10.6 0.7 constant_dynamic-update-slice_fusion.1
  11.3 0.6 constant_dynamic-update-slice_fusion
  11.9 0.6 broadcast_dynamic-update-slice_fusion
  12.5 14.8 %all-to-all-start = ((bf16[64,32,128]{2,1,0:T(8,128)(2,1)}), bf16[64,32,128]{2,1,0:T(8,128)(2,1)S(1)}, u32[]{:S(2)}, u32[]{:S(2)}) async-start(bf16[64,32,128]{2,1,0:T(8,128)(2,1)} %bitcast.3), calls=%async_computation | async-start | bytes 1048576 | tf_op jit(solution)/shard_map/all_to_all | solution.py:698
  27.4 0.0 copy-done.1
  27.4 17.3 %all-to-all-done = bf16[64,32,128]{2,1,0:T(8,128)(2,1)S(1)} async-done(((bf16[64,32,128]{2,1,0:T(8,128)(2,1)}), bf16[64,32,128]{2,1,0:T(8,128)(2,1)S(1)}, u32[]{:S(2)}, u32[]{:S(2)}) %all-to-all-start) | async-done | bytes 524320 | tf_op jit(solution)/shard_map/all_to_all | solution.py:698
  44.7 1.4 gather_fusion
  46.1 0.0 copy-start.4
  46.1 0.0 copy-start.3
  46.1 6.4 %all-to-all-start.1 = ((bf16[64,32,128]{2,1,0:T(8,128)(2,1)}), bf16[64,32,128]{2,1,0:T(8,128)(2,1)S(1)}, u32[]{:S(2)}, u32[]{:S(2)}) async-start(bf16[64,32,128]{2,1,0:T(8,128)(2,1)} %gather_fusion), calls=%async_computation.1 | async-start | bytes 1048576 | tf_op jit(solution)/shard_map/all_to_all | solution.py:699
  52.5 0.0 all-gather.2.cloned.1.call-start
  52.7 17.2 %all-to-all-done.1 = bf16[64,32,128]{2,1,0:T(8,128)(2,1)S(1)} async-done(((bf16[64,32,128]{2,1,0:T(8,128)(2,1)}), bf16[64,32,128]{2,1,0:T(8,128)(2,1)S(1)}, u32[]{:S(2)}, u32[]{:S(2)}) %all-to-all-start.1) | async-done | bytes 524320 | tf_op jit(solution)/shard_map/all_to_all | solution.py:699
  69.9 0.7 slice.32
  70.5 0.0 all-gather.2.cloned.1.call-update
  70.6 0.8 gather_fusion.1
  71.3 0.0 copy-done.4
  71.4 0.0 copy-done.3
  71.4 0.1 compare_reduce_fusion
  71.5 0.2 fusion.2
  71.7 0.1 fusion.4
  71.8 0.6 pad_maximum_fusion.meta
  72.4 119.0 %shard_map.111 = (bf16[8,896,512]{2,1,0:T(8,128)(2,1)}, bf16[896,1024]{1,0:T(8,128)(2,1)}) custom-call(bf16[128,2048]{1,0:T(8,128)(2,1)} %tok.1, bf16[128,2048]{1,0:T(8,128)(2,1)} %og.1, bf16[8,16,128]{2,1,0:T(8,128)(2,1)} %pad_maximum_fusion.meta), custom_call_target="tpu_custom_call" | custom-call | flops 7516192768 | bytes 314572800 | tf_op jit(solution)/shard_map/pallas_call | solution.py:409
  191.4 0.7 reshape.235.lay
  192.2 0.8 convert_add_fusion
  192.9 0.0 all-gather.2.cloned.1.call-done.w_ref
  192.9 26.2 %shard_map.112 = (bf16[4,896,512]{2,1,0:T(8,128)(2,1)}, bf16[896,128]{1,0:T(8,128)(2,1)}, bf16[8,36,16,128]{3,2,1,0:T(8,128)(2,1)}) custom-call(s32[3,12,2]{2,1,0:T(8,128)} %reshape.235.lay, s32[1]{0:T(128)} %bitcast.6.place_ref, bf16[8,896,512]{2,1,0:T(8,128)(2,1)} %get-tuple-element.13.x_ref.s_ref, bf16[8,896,512]{2,1,0:T(8,128)(2,1)} %get-tuple-element.13.x_ref.s_ref, ...), custom_call_target="tpu_custom_call" | custom-call | flops 2818572288 | bytes 14548992 | tf_op jit(solution)/shard_map/pallas_call | solution.py:107
  219.1 98.1 %shard_map.113 = (bf16[128,2048]{1,0:T(8,128)(2,1)}, f32[8,8,128]{2,1,0:T(8,128)}, f32[36,16,128]{2,1,0:T(8,128)}, bf16[36,128,128]{2,1,0:T(8,128)(2,1)}) custom-call(bf16[4,896,512]{2,1,0:T(8,128)(2,1)} %get-tuple-element.14.pg, bf16[1,896,128]{2,1,0:T(8,128)(2,1)} %bitcast.38, bf16[896,1024]{1,0:T(8,128)(2,1)} %get-tuple-element.16.choose, ...), custom_call_target="tpu_custom_call" | custom-call | flops 3758096384 | bytes 157286400 | tf_op jit(solution)/shard_map/pallas_call | solution.py:635
  317.2 0.9 fusion.5
  318.1 0.6 divide_convert_fusion
  318.6 1.9 copy.26
  320.5 0.0 copy-start.2
  320.5 2.5 copy.27
  323.0 0.0 copy-done.2
  323.0 0.7 copy.28
  (9 shorter events, 0.1 us)
Async XLA Ops:
  7.2 2.1 copy-start
  9.2 18.2 %copy-start.1 = (s32[64]{0:T(128)S(1)}, s32[64]{0:T(128)}, u32[]{:S(2)}) copy-start(s32[64]{0:T(128)} %param.15) | copy-start | bytes 772
  12.5 32.2 %all-to-all-start = ((bf16[64,32,128]{2,1,0:T(8,128)(2,1)}), bf16[64,32,128]{2,1,0:T(8,128)(2,1)S(1)}, u32[]{:S(2)}, u32[]{:S(2)}) async-start(bf16[64,32,128]{2,1,0:T(8,128)(2,1)} %bitcast.3), calls=%async_computation | async-start | bytes 1048576 | tf_op jit(solution)/shard_map/all_to_all | solution.py:698
  46.1 25.2 %copy-start.4 = (bf16[128,6]{0,1:T(8,128)(2,1)S(1)}, bf16[128,6]{0,1:T(8,128)(2,1)}, u32[]{:S(2)}) copy-start(bf16[128,6]{0,1:T(8,128)(2,1)} %param.11) | copy-start | bytes 4612
  46.1 25.3 %copy-start.3 = (s32[128,6]{0,1:T(8,128)S(1)}, s32[128,6]{0,1:T(8,128)}, u32[]{:S(2)}) copy-start(s32[128,6]{0,1:T(8,128)} %param.10) | copy-start | bytes 9220
  46.1 23.7 %all-to-all-start.1 = ((bf16[64,32,128]{2,1,0:T(8,128)(2,1)}), bf16[64,32,128]{2,1,0:T(8,128)(2,1)S(1)}, u32[]{:S(2)}, u32[]{:S(2)}) async-start(bf16[64,32,128]{2,1,0:T(8,128)(2,1)} %gather_fusion), calls=%async_computation.1 | async-start | bytes 1048576 | tf_op jit(solution)/shard_map/all_to_all | solution.py:699
  52.5 140.4 %all-gather.2.cloned.1.call-start = ((), (), s32[]{:S(2)}) async-start(), calls=%async_computation.2 | async-start | bytes 1327104 | tf_op jit(solution)/shard_map/all_gather | solution.py:720
  320.5 2.5 copy-start.2
Sparse Core Ops, SparseCore 0:
  70.7 36.6 all-gather.1

commit v4 on v3

--- a/solution.py
+++ b/solution.py
@@ -115,7 +115,7 @@
                 pl.BlockSpec((nm, nb, BLK, BLK), lambda i, lay, place: (0, 0, 0, 0)),
             ],
             out_specs=[
-                row_spec,
+                pl.BlockSpec((2 * nq, tile, width // 2), lambda i, lay, place: (0, i, 0)),
                 pl.BlockSpec((tile, BLK), lambda i, lay, place: (i, 0)),
                 pl.BlockSpec((NY, nm * nb, BLK // NY, BLK), lambda i, lay, place: (0, 0, 0, 0)),
             ],
@@ -131,7 +131,7 @@
             ],
         ),
         out_shape=[
-            jax.ShapeDtypeStruct((nq, rows, width), bf16),
+            jax.ShapeDtypeStruct((2 * nq, rows, width // 2), bf16),
             jax.ShapeDtypeStruct((rows, BLK), bf16),
             jax.ShapeDtypeStruct((NY, nm * nb, BLK // NY, BLK), bf16),
         ],
@@ -277,9 +277,120 @@
         self.direct(q, 0, 1 - self.place.core).wait_send()
 
 
+class Share:
+    def __init__(self, place, blocks, send_sem, recv_sem):
+        self.place, self.blocks, self.send_sem, self.recv_sem = place, blocks, send_sem, recv_sem
+
+    def hop(self, way, step, arriving):
+        past = step + (1 if arriving else 0)
+        source = (self.place.y + (2 * NY - past if way == 0 else past)) % NY
+        n = self.blocks.shape[0]
+        which = slice(0, n)
+        if step == NY // 2 - 1:
+            which = slice(way * (n // 2), (way + 1) * (n // 2))
+        rows = self.blocks.at[which, span(source, BLK // NY)]
+        device = self.place.over(1 if way == 0 else NY - 1)
+        return send(rows, rows, self.send_sem.at[way, step], self.recv_sem.at[way, step], device)
+
+    def advance(self, step):
+        for way in range(2):
+            if step:
+                self.hop(way, step - 1, True).wait_recv()
+            if step < NY // 2:
+                self.hop(way, step, False).start()
+
+    def leave(self):
+        for way in range(2):
+            for step in range(NY // 2):
+                self.hop(way, step, False).wait_send()
+
+
+class Move:
+    def __init__(self, place, state, partner, held, own_sem, send_sem, recv_sem):
+        self.place, self.partner, self.held = place, partner, held
+        self.buffers = [state] + list(held)
+        self.own_sem, self.send_sem, self.recv_sem = own_sem, send_sem, recv_sem
+
+    def ends(self, stage):
+        return self.buffers[(0, 1, 3, 4)[stage]], self.buffers[(1, 2, 4, 5)[stage]]
+
+    def own(self, stage):
+        src, dst = self.ends(stage)
+        if stage % 2 == 0:
+            here = self.place.z
+            return pltpu.make_async_copy(src.at[here], dst.at[here], self.own_sem.at[stage])
+        here = self.place.x * NCORE + self.place.core
+        return pltpu.make_async_copy(src.at[:, here], dst.at[here], self.own_sem.at[stage])
+
+    def piece(self, stage, k, core, arriving):
+        place = self.place
+        src, dst = self.ends(stage)
+        if stage % 2 == 0:
+            landing = (place.z + NZ - k) % NZ if arriving else place.z
+            return send(
+                src.at[(place.z + k) % NZ],
+                dst.at[landing],
+                self.send_sem.at[stage, k],
+                self.recv_sem.at[stage, k],
+                place.along(k),
+            )
+        other = (place.x + k) % NX * NCORE + core
+        if arriving:
+            return send(
+                src.at[:, other],
+                dst.at[other],
+                self.send_sem.at[stage, k * NCORE + core],
+                self.recv_sem.at[stage, k * NCORE + core],
+                place.across(k, core),
+            )
+        return send(
+            src.at[:, other],
+            dst.at[place.x * NCORE + place.core],
+            self.send_sem.at[stage, k * NCORE + core],
+            self.recv_sem.at[stage, (NX - k) % NX * NCORE + place.core],
+            place.across(k, core),
+        )
+
+    def pieces(self, stage, arriving):
+        if stage % 2 == 0:
+            return [self.piece(stage, k, 0, arriving) for k in range(1, NZ)]
+        rest = [self.piece(stage, k, c, arriving) for k in range(1, NX) for c in range(NCORE)]
+        return rest + [self.piece(stage, 0, 1 - self.place.core, arriving)]
+
+    def start(self, stage):
+        for copy in self.pieces(stage, False):
+            copy.start()
+        self.own(stage).start()
+
+    def arrive(self, stage):
+        for copy in self.pieces(stage, True):
+            copy.wait_recv()
+        self.own(stage).wait()
+
+    def leave(self):
+        for stage in range(4):
+            for copy in self.pieces(stage, False):
+                copy.wait_send()
+
+    def order(self):
+        def one(slot, carry):
+            z, j = slot // PLANE, slot % PLANE
+            expert = self.partner[j // NCORE * (NZ * NCORE) + z * NCORE + j % NCORE]
+            j_from = expert // (NZ * NCORE) * NCORE + expert % NCORE
+            self.held[2][z, j] = self.held[1][j_from, expert // NCORE % NZ]
+            return carry
+
+        lax.fori_loop(0, NZ * PLANE, one, 0)
+
+    def tile(self, t):
+        return self.held[4][t // 2 % PLANE, t // (2 * PLANE), span(t % 2, 16), :]
+
+
 def dispatch_kernel(
-    tok, og, meta, xs, chosen, ring, picked, choose, notes, relay,
+    tok, og, meta, state, partner, xs, chosen, blocks, own_rows, moment, lay, ring, picked, choose, notes, relay,
+    held_0, held_1, held_2, held_3, held_4,
     own_sem, notes_send, notes_recv, ring_send, ring_recv, out_own, out_send, out_recv, relay_send, relay_recv, keep_sem,
+    move_own, move_send, move_recv, share_send, share_recv,
 ):
     count = tok.shape[0]
     chunks, _, width = ring.shape
@@ -287,6 +398,8 @@
     place = Place()
     z = place.z
     out = Exchange(place, picked, xs, relay, out_own, out_send, out_recv, relay_send, relay_recv)
+    move = Move(place, state, partner, (held_0, held_1, held_2, held_3, held_4), move_own, move_send, move_recv)
+    share = Share(place, blocks, share_send, share_recv)
 
     def own_copy(q):
         src = tok if q < half else og
@@ -300,7 +413,7 @@
         own_copy(q).start()
     own_notes = pltpu.make_async_copy(meta.at[z], notes.at[z], keep_sem.at[1])
     own_notes.start()
-    place.meet(False)
+    place.meet(True)
 
     def note(k, source):
         return send(
@@ -312,6 +425,20 @@
     for q in range(chunks):
         own_copy(q).wait()
     own_notes.wait()
+    move.start(0)
+
+    def unpack():
+        n = blocks.shape[0]
+
+        def one(b, carry):
+            rows = move.tile(b)
+            own_rows[b] = rows
+            blocks[b, span(place.y, BLK // NY), :] = rows
+            moment[b] = move.tile(n + b).astype(jnp.float32) + move.tile(2 * n + b).astype(jnp.float32)
+            return carry
+
+        lax.fori_loop(0, n, one, 0)
+        lay[...] = move.tile(3 * n)
 
     def hop(q, way, step, arriving):
         rows = count
@@ -381,6 +508,34 @@
                 picked[q, rows, :] = dot(choose[q // half, rows, :], ring[q]).astype(jnp.bfloat16)
                 out.start(q, (2, 3) if h else (1, 0))
 
+        @pl.when(i == 1)
+        def _():
+            move.arrive(0)
+            move.start(1)
+
+        @pl.when(i == 2)
+        def _():
+            move.arrive(1)
+            move.order()
+            move.start(2)
+
+        @pl.when(i == 4)
+        def _():
+            move.arrive(2)
+            move.start(3)
+
+        @pl.when(i == 5)
+        def _():
+            move.arrive(3)
+            unpack()
+            share.advance(0)
+
+        for s in range(1, NY // 2 + 1):
+
+            @pl.when(i == 5 + s)
+            def _():
+                share.advance(s)
+
         return carry
 
     lax.fori_loop(0, chunks + NZ // 2 + 1, step, 0)
@@ -397,9 +552,11 @@
     for k in range(1, NZ):
         note(k, z).wait_send()
     keep().wait()
-
-
-def dispatch(tokens, grads, meta, chunks):
+    move.leave()
+    share.leave()
+
+
+def dispatch(tokens, grads, meta, state, partner, tiles, chunks):
     count, features = tokens.shape
     width = 2 * features // chunks
     bf16 = jnp.bfloat16
@@ -408,11 +565,15 @@
     anywhere = pl.BlockSpec(memory_space=pl.ANY)
     return pl.pallas_call(
         dispatch_kernel,
-        in_specs=[anywhere, anywhere, anywhere],
-        out_specs=[anywhere, anywhere],
+        in_specs=[anywhere] * 4 + [pl.BlockSpec(memory_space=pltpu.SMEM)],
+        out_specs=[anywhere, anywhere] + [pl.BlockSpec(memory_space=pltpu.VMEM)] * 4,
         out_shape=[
             jax.ShapeDtypeStruct((chunks, slots, width), bf16),
             jax.ShapeDtypeStruct((slots, NZ * count), bf16),
+            jax.ShapeDtypeStruct((tiles, BLK, BLK), bf16),
+            jax.ShapeDtypeStruct((tiles, BLK // NY, BLK), bf16),
+            jax.ShapeDtypeStruct((tiles, BLK // NY, BLK), jnp.float32),
+            jax.ShapeDtypeStruct((BLK // NY, BLK), bf16),
         ],
         scratch_shapes=[
             pltpu.VMEM((chunks, NZ * count, width), bf16),
@@ -420,6 +581,7 @@
             pltpu.VMEM((2, slots, NZ * count), bf16),
             pltpu.VMEM(meta.shape, bf16),
             pltpu.VMEM((chunks, 2, ROWS, width), bf16),
+            *[pltpu.VMEM(state.shape, bf16)] * 5,
             dma((chunks,)),
             dma((NZ,)),
             dma((NZ,)),
@@ -431,6 +593,11 @@
             dma((chunks, 2)),
             dma((chunks, 2)),
             dma((2,)),
+            dma((4,)),
+            dma((4, NZ)),
+            dma((4, NZ)),
+            dma((2, NY // 2)),
+            dma((2, NY // 2)),
         ],
         compiler_params=pltpu.CompilerParams(
             collective_id=0, has_side_effects=True, vmem_limit_bytes=56 << 20
@@ -438,7 +605,7 @@
         cost_estimate=pl.CostEstimate(
             flops=2 * slots * NZ * count * 2 * features, bytes_accessed=300 << 20, transcendentals=0
         ),
-    )(tokens, grads, meta)
+    )(tokens, grads, meta, state, partner)
 
 
 def return_kernel(
@@ -469,19 +636,7 @@
     cross.start(1)
     cross.forward(0)
 
-    def share(way, step, arriving):
-        if way == 0:
-            source = (y + 2 * NY - step - (1 if arriving else 0)) % NY
-        else:
-            source = (y + step + (1 if arriving else 0)) % NY
-        n = blocks.shape[0]
-        which = slice(0, n)
-        if step == NY // 2 - 1:
-            which = slice(way * (n // 2), (way + 1) * (n // 2))
-        rows = blocks.at[which, span(source, BLK // NY)]
-        return send(
-            rows, rows, share_send.at[way, step], share_recv.at[way, step], place.over(1 if way == 0 else NY - 1)
-        )
+    share = Share(place, blocks, share_send, share_recv)
 
     def update():
         for k in range(1, NY):
@@ -498,8 +653,7 @@
             return carry
 
         lax.fori_loop(0, blocks.shape[0], one, 0)
-        for way in range(2):
-            share(way, 0, False).start()
+        share.advance(0)
 
     def hop(q, way, step):
         rows = slice(0, count)
@@ -581,14 +735,12 @@
         def _():
             cross.forward(i + 1)
 
-        pl.when(i == 2)(update)
-        for s in range(1, NY // 2):
-
-            @pl.when(i == 2 + s)
+        pl.when(i == 5)(update)
+        for s in range(1, NY // 2 + 1):
+
+            @pl.when(i == 5 + s)
             def _():
-                for way in range(2):
-                    share(way, s - 1, True).wait_recv()
-                    share(way, s, False).start()
+                share.advance(s)
 
         @pl.when(i == chunks - 1)
         def _():
@@ -620,10 +772,7 @@
         summed(k, (z + NZ - k) % NZ).wait_recv()
     for k in range(1, NY):
         grad(k, y).wait_send()
-    for way in range(2):
-        share(way, NY // 2 - 1, True).wait_recv()
-        for s in range(NY // 2):
-            share(way, s, False).wait_send()
+    share.leave()
 
 
 def give_back(pg, sc, choose, wg, own_blocks, old_moment, count):
@@ -677,36 +826,16 @@
     )(pg, sc, choose, wg, own_blocks, old_moment)
 
 
-def move_state(own_blocks, moments, layout_one, partner, n):
+def pack_state(own_blocks, moments, layout_one):
     bf16 = jnp.bfloat16
-    tiles = own_blocks.size // (16 * BLK)
     high = moments.astype(bf16)
     low = (moments - high.astype(jnp.float32)).astype(bf16)
     flat_layout = layout_one.reshape(-1)
     lay_tile = jnp.pad(flat_layout, (0, 16 * BLK - flat_layout.size)).astype(bf16)
-    count = 3 * tiles + 1
-    padded = -(-count // n) * n
-    state = jnp.concatenate(
-        [
-            own_blocks.reshape(tiles, 16, BLK),
-            high.reshape(tiles, 16, BLK),
-            low.reshape(tiles, 16, BLK),
-            lay_tile.reshape(1, 16, BLK),
-            jnp.zeros((padded - count, 16, BLK), bf16),
-        ]
-    ).reshape(n, -1, BLK)
-    spread = lax.all_to_all(state, "expert", split_axis=0, concat_axis=0, tiled=True)
-    moved = lax.all_to_all(spread[partner], "expert", split_axis=0, concat_axis=0, tiled=True)
-    moved = moved.reshape(padded, 16, BLK)
-    new_blocks = moved[:tiles].reshape(own_blocks.shape)
-    new_moments = (
-        moved[tiles : 2 * tiles].astype(jnp.float32)
-        + moved[2 * tiles : 3 * tiles].astype(jnp.float32)
-    ).reshape(moments.shape)
-    new_layout = (
-        moved[3 * tiles].reshape(-1)[: flat_layout.size].astype(jnp.int32).reshape(layout_one.shape)
-    )
-    return new_blocks, new_moments, new_layout
+    parts = [a.reshape(-1, 16, BLK) for a in (own_blocks, high, low, lay_tile)]
+    count = sum(a.shape[0] for a in parts)
+    parts.append(jnp.zeros((2 * NZ * PLANE - count, 16, BLK), bf16))
+    return jnp.concatenate(parts).reshape(NZ, PLANE, 32, BLK)
 
 
 def body(tokens, out_grad, expert_ids, route_weights, blocks, layout, moments, partner):
@@ -716,8 +845,8 @@
     count, width = tokens.shape
     share = BLK // n_dp
     own = lax.dynamic_slice_in_dim(blocks[0], lax.axis_index("dp") * share, share, 2)
-    own, old_moment, layout_one = move_state(own, moments[0], layout[0], partner, n)
-    mats = lax.all_gather(own, "dp", axis=2, tiled=True)
+    state = pack_state(own, moments[0], layout[0])
+    tiles = own.shape[0] * own.shape[1]
 
     place = Place()
     number = jnp.arange(n, dtype=jnp.int32)
@@ -732,11 +861,15 @@
     meta = jnp.concatenate(
         [slot.reshape(NZ, PLANE, count), weight.reshape(NZ, PLANE, count)], axis=1
     ).astype(bf16)
-    xs, choose = dispatch(tokens, out_grad, meta, 8)
-    pg, sc, wg = expert_compute(layout_one, place.core.reshape(1), xs, mats, 448)
-    tiles = own.shape[0] * own.shape[1]
+    xs, choose, mats, own, old_moment, lay = dispatch(
+        tokens, out_grad, meta, state, partner, tiles, 8
+    )
+    layout_one = lay.reshape(-1)[: layout[0].size].astype(jnp.int32).reshape(layout[0].shape)
+    pg, sc, wg = expert_compute(
+        layout_one, place.core.reshape(1), xs, mats.reshape(blocks[0].shape), 448
+    )
     token_grad, score, moment, updated = give_back(
-        pg, sc[None], choose, wg, own.reshape(tiles, share, BLK), old_moment.reshape(tiles, share, BLK), count
+        pg, sc[None], choose, wg, own, old_moment, count
     )
     score = jnp.sum(jnp.where(picks, score.reshape(n, count)[:, :, None], 0.0), axis=0)
     route_grad = (score / route_weights.astype(f32)).astype(bf16)

time: 331 us -> 300 us (0.906)
  Pallas kernels: 243 us -> 284 us
  waiting for transfers between devices: 34.5 us -> 0 us
  starting transfers between devices: 21.3 us -> 0 us
  between operations: 14.2 us -> 0.85 us
  local copies, waits for them, and re-layouts: 12.2 us -> 8.37 us
    pallas_call x1, Pallas kernels: 119 us -> 159 us  [dispatch(): pl.pallas_call(dispatch_kernel, in_specs=[anywhere] * 4 + [pl.BlockSpec(m...]
    all_to_all x2 -> x0, waiting for transfers between devices: 34.5 us -> none  [the longest x1 17.3 us: move_state(): lax.all_to_all(state, 'expert', split_axis=0, concat_axis=0, tiled=True)]
    all_to_all x2 -> x0, starting transfers between devices: 21.2 us -> none  [the longest x1 14.8 us: move_state(): lax.all_to_all(state, 'expert', split_axis=0, concat_axis=0, tiled=True)]
    unnamed x17 -> x19, local copies, waits for them, and re-layouts: 7.68 us -> 5.93 us
  transfers between devices with their start and end apart: 3 -> 0, of which waited for: 2 -> 0; matrix products, arithmetic and copies ran while one was open for 1% -> 0% of each run, Pallas kernels for 36% -> 0%
where the time goes in v4:
time: 300 us; the launch traced here: 299 us
  Pallas kernels  284 us (95%)
  local copies, waits for them, and re-layouts  8.37 us (3%)
  other arithmetic  5.84 us (2%)
    pallas_call x1, Pallas kernels, dispatch(): pl.pallas_call(dispatch_kernel, in_specs=[anywhere] * 4 + [pl.BlockSpec(m...  159 us
    pallas_call x1, Pallas kernels, give_back(): pl.pallas_call(return_kernel, in_specs=[anywhere, anywhere, vmem, anywher...  98.2 us
    pallas_call x1, Pallas kernels, expert_compute(): pl.pallas_call(expert_kernel, grid_spec=pltpu.PrefetchScalarGridSpec(num_...  26.3 us

profile of v4, /device:TPU:1, one launch (start us, length us, event | category | flops | bytes accessed | tf_op | source)
XLA Modules:
  0.0 299.0 jit_solution(12034679546824274310)
XLA Ops:
  0.6 0.0 copy-start
  0.6 0.0 copy-start.1
  0.7 0.8 convert.16
  1.5 1.4 gather_fusion
  3.0 0.7 convert_element_type.35
  3.7 0.8 compare_reduce_fusion
  4.4 0.2 fusion.2
  4.6 0.1 copy.18
  4.8 0.1 reshape_squeeze.4
  4.9 0.8 fusion.4
  5.7 0.6 pad_maximum_fusion.meta
  6.3 0.0 copy-done
  6.3 0.0 copy-done.1
  6.5 0.0 copy-start.3
  6.5 0.8 copy-done.3
  7.3 159.2 %shard_map.111 = (bf16[8,896,512]{2,1,0:T(8,128)(2,1)}, bf16[896,1024]{1,0:T(8,128)(2,1)}, bf16[36,128,128]{2,1,0:T(8,128)(2,1)}, bf16[36,16,128]{2,1,0:T(8,128)...) custom-call(bf16[128,2048]{1,0:T(8,128)(2,1)} %tok.1, bf16[128,2048]{1,0:T(8,128)(2,1)} %og.1, ...), custom_call_target="tpu_custom_call" | custom-call | flops 7516192768 | bytes 314572800 | tf_op jit(solution)/shard_map/pallas_call | solution.py:566
  166.6 0.7 slice_convert_fusion
  167.2 0.7 reshape.228.lay
  168.0 26.3 %shard_map.112 = (bf16[8,896,256]{2,1,0:T(8,128)(2,1)}, bf16[896,128]{1,0:T(8,128)(2,1)}, bf16[8,36,16,128]{3,2,1,0:T(8,128)(2,1)}) custom-call(s32[3,12,2]{2,1,0:T(8,128)} %reshape.228.lay, s32[1]{0:T(128)} %bitcast.8.place_ref, bf16[8,896,512]{2,1,0:T(8,128)(2,1)} %get-tuple-element.18.x_ref.s_ref, bf16[8,896,512]{2,1,0:T(8,128)(2,1)} %get-tuple-element.18.x_ref.s_ref, ...), custom_call_target="tpu_custom_call" | custom-call | flops 2818572288 | bytes 14548992 | tf_op jit(solution)/shard_map/pallas_call | solution.py:107
  194.3 0.0 copy-start.4
  194.3 0.0 copy-start.5
  194.3 98.2 %shard_map.113 = (bf16[128,2048]{1,0:T(8,128)(2,1)}, f32[8,8,128]{2,1,0:T(8,128)}, f32[36,16,128]{2,1,0:T(8,128)}, bf16[36,128,128]{2,1,0:T(8,128)(2,1)}) custom-call(bf16[8,896,256]{2,1,0:T(8,128)(2,1)} %get-tuple-element.20.pg, bf16[1,896,128]{2,1,0:T(8,128)(2,1)} %bitcast.32, bf16[896,1024]{1,0:T(8,128)(2,1)} %get-tuple-element.22.choose, ...), custom_call_target="tpu_custom_call" | custom-call | flops 3758096384 | bytes 157286400 | tf_op jit(solution)/shard_map/pallas_call | solution.py:784
  292.5 0.0 copy-done.4
  292.5 0.9 fusion.5
  293.4 0.0 copy-done.5
  293.4 0.6 divide_convert_fusion
  294.0 1.9 copy.26
  295.9 0.0 copy-start.2
  295.9 2.5 copy.27
  298.3 0.0 copy-done.2
  298.3 0.7 copy.28
  (10 shorter events, 0.2 us)
Async XLA Ops:
  0.6 5.7 %copy-start = (bf16[1,3,12,128,128]{4,3,2,1,0:T(8,128)(2,1)S(1)}, bf16[1,3,12,128,128]{4,3,2,1,0:T(8,128)(2,1)}, u32[]{:S(2)}) copy-start(bf16[1,3,12,128,128]{4,3,2,1,0:T(8,128)(2,1)} %param.12) | copy-start | bytes 3538948
  0.6 5.7 %copy-start.1 = (f32[1,3,12,16,128]{4,3,2,1,0:T(8,128)S(1)}, f32[1,3,12,16,128]{4,3,2,1,0:T(8,128)}, u32[]{:S(2)}) copy-start(f32[1,3,12,16,128]{4,3,2,1,0:T(8,128)} %param.14) | copy-start | bytes 884740
  6.5 0.8 copy-start.3
  194.3 98.3 %copy-start.4 = (s32[128,6]{0,1:T(8,128)S(1)}, s32[128,6]{0,1:T(8,128)}, u32[]{:S(2)}) copy-start(s32[128,6]{0,1:T(8,128)} %param.10) | copy-start | bytes 9220
  194.3 99.1 %copy-start.5 = (bf16[128,6]{0,1:T(8,128)(2,1)S(1)}, bf16[128,6]{0,1:T(8,128)(2,1)}, u32[]{:S(2)}) copy-start(bf16[128,6]{0,1:T(8,128)(2,1)} %param.11) | copy-start | bytes 4612
  295.9 2.5 copy-start.2

commit v5 on v4

--- a/solution.py
+++ b/solution.py
@@ -383,14 +383,14 @@
         lax.fori_loop(0, NZ * PLANE, one, 0)
 
     def tile(self, t):
-        return self.held[4][t // 2 % PLANE, t // (2 * PLANE), span(t % 2, 16), :]
+        return self.held[4][t % PLANE, t // PLANE]
 
 
 def dispatch_kernel(
-    tok, og, meta, state, partner, xs, chosen, blocks, own_rows, moment, lay, ring, picked, choose, notes, relay,
-    held_0, held_1, held_2, held_3, held_4,
+    tok, og, meta, state, late_state, partner, xs, chosen, blocks, own_rows, moment, lay, ring, picked, choose, turned, notes, relay,
+    held_0, held_1, held_2, held_3, held_4, late_0, late_1, late_2, late_3, late_4,
     own_sem, notes_send, notes_recv, ring_send, ring_recv, out_own, out_send, out_recv, relay_send, relay_recv, keep_sem,
-    move_own, move_send, move_recv, share_send, share_recv,
+    move_own, move_send, move_recv, share_send, share_recv, late_own, late_send, late_recv,
 ):
     count = tok.shape[0]
     chunks, _, width = ring.shape
@@ -399,6 +399,7 @@
     z = place.z
     out = Exchange(place, picked, xs, relay, out_own, out_send, out_recv, relay_send, relay_recv)
     move = Move(place, state, partner, (held_0, held_1, held_2, held_3, held_4), move_own, move_send, move_recv)
+    late = Move(place, late_state, partner, (late_0, late_1, late_2, late_3, late_4), late_own, late_send, late_recv)
     share = Share(place, blocks, share_send, share_recv)
 
     def own_copy(q):
@@ -434,11 +435,17 @@
             rows = move.tile(b)
             own_rows[b] = rows
             blocks[b, span(place.y, BLK // NY), :] = rows
-            moment[b] = move.tile(n + b).astype(jnp.float32) + move.tile(2 * n + b).astype(jnp.float32)
             return carry
 
         lax.fori_loop(0, n, one, 0)
-        lay[...] = move.tile(3 * n)
+        lay[...] = move.tile(n)
+
+    def unpack_late():
+        def one(b, carry):
+            moment[b] = late.tile(b)
+            return carry
+
+        lax.fori_loop(0, moment.shape[0], one, 0)
 
     def hop(q, way, step, arriving):
         rows = count
@@ -460,7 +467,7 @@
         )
 
     def keep():
-        return pltpu.make_async_copy(choose.at[0], chosen, keep_sem.at[0])
+        return pltpu.make_async_copy(turned, chosen, keep_sem.at[0])
 
     def build():
         for k in range(1, NZ):
@@ -478,6 +485,14 @@
             return carry
 
         lax.fori_loop(0, NZ, fill, 0)
+
+    def turn():
+        def one(source, carry):
+            block = choose[0, :, span(source, count)].astype(jnp.float32)
+            turned[span(source, count), :] = block.T.astype(jnp.bfloat16)
+            return carry
+
+        lax.fori_loop(0, NZ, one, 0)
         keep().start()
 
     def step(i, carry):
@@ -492,10 +507,7 @@
                     hop(q, way, s, False).start()
 
         pl.when(i == 1)(build)
-
-        @pl.when((i > NZ // 2) & (i <= NZ // 2 + chunks))
-        def _():
-            out.forward(i - NZ // 2 - 1)
+        pl.when(i == NZ // 2 + 3)(turn)
 
         q = i - NZ // 2
 
@@ -508,6 +520,10 @@
                 picked[q, rows, :] = dot(choose[q // half, rows, :], ring[q]).astype(jnp.bfloat16)
                 out.start(q, (2, 3) if h else (1, 0))
 
+        @pl.when((i > NZ // 2) & (i <= NZ // 2 + chunks))
+        def _():
+            out.forward(i - NZ // 2 - 1)
+
         @pl.when(i == 1)
         def _():
             move.arrive(0)
@@ -535,6 +551,31 @@
             @pl.when(i == 5 + s)
             def _():
                 share.advance(s)
+
+        @pl.when(i == chunks)
+        def _():
+            late.start(0)
+
+        @pl.when(i == chunks + 1)
+        def _():
+            late.arrive(0)
+            late.start(1)
+
+        @pl.when(i == chunks + 2)
+        def _():
+            late.arrive(1)
+            late.order()
+            late.start(2)
+
+        @pl.when(i == chunks + 3)
+        def _():
+            late.arrive(2)
+            late.start(3)
+
+        @pl.when(i == chunks + 4)
+        def _():
+            late.arrive(3)
+            unpack_late()
 
         return carry
 
@@ -553,10 +594,11 @@
         note(k, z).wait_send()
     keep().wait()
     move.leave()
+    late.leave()
     share.leave()
 
 
-def dispatch(tokens, grads, meta, state, partner, tiles, chunks):
+def dispatch(tokens, grads, meta, state, late_state, partner, tiles, chunks):
     count, features = tokens.shape
     width = 2 * features // chunks
     bf16 = jnp.bfloat16
@@ -565,23 +607,24 @@
     anywhere = pl.BlockSpec(memory_space=pl.ANY)
     return pl.pallas_call(
         dispatch_kernel,
-        in_specs=[anywhere] * 4 + [pl.BlockSpec(memory_space=pltpu.SMEM)],
+        in_specs=[anywhere] * 5 + [pl.BlockSpec(memory_space=pltpu.SMEM)],
         out_specs=[anywhere, anywhere] + [pl.BlockSpec(memory_space=pltpu.VMEM)] * 4,
         out_shape=[
             jax.ShapeDtypeStruct((chunks, slots, width), bf16),
-            jax.ShapeDtypeStruct((slots, NZ * count), bf16),
+            jax.ShapeDtypeStruct((NZ * count, slots), bf16),
             jax.ShapeDtypeStruct((tiles, BLK, BLK), bf16),
             jax.ShapeDtypeStruct((tiles, BLK // NY, BLK), bf16),
-            jax.ShapeDtypeStruct((tiles, BLK // NY, BLK), jnp.float32),
+            jax.ShapeDtypeStruct((tiles, BLK // NY, BLK), bf16),
             jax.ShapeDtypeStruct((BLK // NY, BLK), bf16),
         ],
         scratch_shapes=[
             pltpu.VMEM((chunks, NZ * count, width), bf16),
             pltpu.VMEM((chunks, slots, width), bf16),
             pltpu.VMEM((2, slots, NZ * count), bf16),
+            pltpu.VMEM((NZ * count, slots), bf16),
             pltpu.VMEM(meta.shape, bf16),
             pltpu.VMEM((chunks, 2, ROWS, width), bf16),
-            *[pltpu.VMEM(state.shape, bf16)] * 5,
+            *[pltpu.VMEM(state.shape, bf16)] * 10,
             dma((chunks,)),
             dma((NZ,)),
             dma((NZ,)),
@@ -598,6 +641,9 @@
             dma((4, NZ)),
             dma((2, NY // 2)),
             dma((2, NY // 2)),
+            dma((4,)),
+            dma((4, NZ)),
+            dma((4, NZ)),
         ],
         compiler_params=pltpu.CompilerParams(
             collective_id=0, has_side_effects=True, vmem_limit_bytes=56 << 20
@@ -605,7 +651,7 @@
         cost_estimate=pl.CostEstimate(
             flops=2 * slots * NZ * count * 2 * features, bytes_accessed=300 << 20, transcendentals=0
         ),
-    )(tokens, grads, meta, state, partner)
+    )(tokens, grads, meta, state, late_state, partner)
 
 
 def return_kernel(
@@ -632,9 +678,11 @@
 
     for k in range(1, NY):
         grad(k, y).start()
-    mark.start(0)
     cross.start(1)
     cross.forward(0)
+    cross.start(2)
+    mark.start(0)
+    cross.forward(1)
 
     share = Share(place, blocks, share_send, share_recv)
 
@@ -644,7 +692,7 @@
         own_grads.wait()
 
         def one(b, carry):
-            total = DECAY * old_moment[b]
+            total = DECAY * old_moment[b].astype(jnp.float32)
             for source in range(NY):
                 total = total + grads[source, b].astype(jnp.float32)
             moment[b] = total
@@ -686,7 +734,7 @@
 
             def add(t, carry):
                 cols = span(t, 2 * count)
-                part[q, cols, :] = dot(choose[:, cols], back[q], TN)
+                part[q, cols, :] = dot(choose[cols, :], back[q])
                 return carry
 
             lax.fori_loop(0, NZ // 2, add, 0)
@@ -727,13 +775,13 @@
                 total = total + landed[q, way, last].astype(jnp.float32)
             tg[:, pl.ds(pl.multiple_of(q * width, width), width)] = total.astype(jnp.bfloat16)
 
+        @pl.when(i + 3 < chunks)
+        def _():
+            cross.start(i + 3)
+
         @pl.when(i + 2 < chunks)
         def _():
-            cross.start(i + 2)
-
-        @pl.when(i + 1 < chunks)
-        def _():
-            cross.forward(i + 1)
+            cross.forward(i + 2)
 
         pl.when(i == 5)(update)
         for s in range(1, NY // 2 + 1):
@@ -745,7 +793,7 @@
         @pl.when(i == chunks - 1)
         def _():
             mark.arrive(0)
-            spread = dot(marks[0], choose[...], TN)
+            spread = dot(marks[0], choose[...], (((0,), (1,)), ((), ())))
             both = spread[:PLANE] + spread[PLANE : 2 * PLANE]
             for source in range(NZ):
                 sums[source] = both[:, source * count : (source + 1) * count]
@@ -826,16 +874,11 @@
     )(pg, sc, choose, wg, own_blocks, old_moment)
 
 
-def pack_state(own_blocks, moments, layout_one):
-    bf16 = jnp.bfloat16
-    high = moments.astype(bf16)
-    low = (moments - high.astype(jnp.float32)).astype(bf16)
-    flat_layout = layout_one.reshape(-1)
-    lay_tile = jnp.pad(flat_layout, (0, 16 * BLK - flat_layout.size)).astype(bf16)
-    parts = [a.reshape(-1, 16, BLK) for a in (own_blocks, high, low, lay_tile)]
-    count = sum(a.shape[0] for a in parts)
-    parts.append(jnp.zeros((2 * NZ * PLANE - count, 16, BLK), bf16))
-    return jnp.concatenate(parts).reshape(NZ, PLANE, 32, BLK)
+def pieces(*parts):
+    tiles = [a.reshape(-1, 16, BLK).astype(jnp.bfloat16) for a in parts]
+    count = sum(a.shape[0] for a in tiles)
+    tiles.append(jnp.zeros((NZ * PLANE - count, 16, BLK), jnp.bfloat16))
+    return jnp.concatenate(tiles).reshape(NZ, PLANE, 16, BLK)
 
 
 def body(tokens, out_grad, expert_ids, route_weights, blocks, layout, moments, partner):
@@ -845,7 +888,9 @@
     count, width = tokens.shape
     share = BLK // n_dp
     own = lax.dynamic_slice_in_dim(blocks[0], lax.axis_index("dp") * share, share, 2)
-    state = pack_state(own, moments[0], layout[0])
+    flat_layout = layout[0].reshape(-1)
+    state = pieces(own, jnp.pad(flat_layout, (0, 16 * BLK - flat_layout.size)))
+    late_state = pieces(moments[0])
     tiles = own.shape[0] * own.shape[1]
 
     place = Place()
@@ -862,7 +907,7 @@
         [slot.reshape(NZ, PLANE, count), weight.reshape(NZ, PLANE, count)], axis=1
     ).astype(bf16)
     xs, choose, mats, own, old_moment, lay = dispatch(
-        tokens, out_grad, meta, state, partner, tiles, 8
+        tokens, out_grad, meta, state, late_state, partner, tiles, 8
     )
     layout_one = lay.reshape(-1)[: layout[0].size].astype(jnp.int32).reshape(layout[0].shape)
     pg, sc, wg = expert_compute(

time: 300 us -> 272 us (0.907)
  Pallas kernels: 284 us -> 254 us
    pallas_call x1, Pallas kernels: 98.2 us -> 75.3 us  [give_back(): pl.pallas_call(return_kernel, in_specs=[anywhere, anywhere, vmem, anywher...]
    pallas_call x1, Pallas kernels: 159 us -> 153 us  [dispatch(): pl.pallas_call(dispatch_kernel, in_specs=[anywhere] * 5 + [pl.BlockSpec(m...]
where the time goes in v5:
time: 272 us; the launch traced here: 270 us
  Pallas kernels  254 us (93%)
  local copies, waits for them, and re-layouts  8.31 us (3%)
  other arithmetic  6.67 us (2%)
    pallas_call x1, Pallas kernels, dispatch(): pl.pallas_call(dispatch_kernel, in_specs=[anywhere] * 5 + [pl.BlockSpec(m...  153 us
    pallas_call x1, Pallas kernels, give_back(): pl.pallas_call(return_kernel, in_specs=[anywhere, anywhere, vmem, anywher...  75.3 us
    pallas_call x1, Pallas kernels, expert_compute(): pl.pallas_call(expert_kernel, grid_spec=pltpu.PrefetchScalarGridSpec(num_...  26.3 us

profile of v5, /device:TPU:1, one launch (start us, length us, event | category | flops | bytes accessed | tf_op | source)
XLA Modules:
  0.0 270.1 jit_solution(12044617002591747587)
XLA Ops:
  0.6 0.0 copy-start
  0.6 0.0 copy-start.1
  0.7 0.1 pad.9.clone
  0.8 0.8 convert.16
  1.6 1.4 gather_fusion
  3.0 0.7 convert_element_type.39
  3.7 0.8 compare_reduce_fusion
  4.5 0.2 fusion.2
  4.7 0.1 copy.18
  4.8 0.1 reshape_squeeze.5
  5.0 0.8 fusion.3
  5.8 0.6 pad_maximum_fusion.meta
  6.4 0.0 copy-done
  6.4 0.8 maximum_maximum_fusion
  7.3 0.0 copy-done.1
  7.3 0.7 concatenate.12
  8.0 152.6 %shard_map.111 = (bf16[8,896,512]{2,1,0:T(8,128)(2,1)}, bf16[1024,896]{1,0:T(8,128)(2,1)}, bf16[36,128,128]{2,1,0:T(8,128)(2,1)}, bf16[36,16,128]{2,1,0:T(8,128)...) custom-call(bf16[128,2048]{1,0:T(8,128)(2,1)} %tok.1, bf16[128,2048]{1,0:T(8,128)(2,1)} %og.1, ...), custom_call_target="tpu_custom_call" | custom-call | flops 7516192768 | bytes 314572800 | tf_op jit(solution)/shard_map/pallas_call | solution.py:608
  160.6 0.7 slice_convert_fusion
  161.3 0.7 reshape.239.lay
  162.0 26.3 %shard_map.112 = (bf16[8,896,256]{2,1,0:T(8,128)(2,1)}, bf16[896,128]{1,0:T(8,128)(2,1)}, bf16[8,36,16,128]{3,2,1,0:T(8,128)(2,1)}) custom-call(s32[3,12,2]{2,1,0:T(8,128)} %reshape.239.lay, s32[1]{0:T(128)} %bitcast.9.place_ref, bf16[8,896,512]{2,1,0:T(8,128)(2,1)} %get-tuple-element.18.x_ref.s_ref, bf16[8,896,512]{2,1,0:T(8,128)(2,1)} %get-tuple-element.18.x_ref.s_ref, ...), custom_call_target="tpu_custom_call" | custom-call | flops 2818572288 | bytes 14548992 | tf_op jit(solution)/shard_map/pallas_call | solution.py:107
  188.3 0.0 copy-start.3
  188.3 0.0 copy-start.4
  188.3 75.3 %shard_map.113 = (bf16[128,2048]{1,0:T(8,128)(2,1)}, f32[8,8,128]{2,1,0:T(8,128)}, f32[36,16,128]{2,1,0:T(8,128)}, bf16[36,128,128]{2,1,0:T(8,128)(2,1)}) custom-call(bf16[8,896,256]{2,1,0:T(8,128)(2,1)} %get-tuple-element.20.pg, bf16[1,896,128]{2,1,0:T(8,128)(2,1)} %bitcast.30, bf16[1024,896]{1,0:T(8,128)(2,1)} %get-tuple-element.22.choose, ...), custom_call_target="tpu_custom_call" | custom-call | flops 3758096384 | bytes 157286400 | tf_op jit(solution)/shard_map/pallas_call | solution.py:832
  263.6 0.0 copy-done.3
  263.6 0.9 fusion.4
  264.5 0.0 copy-done.4
  264.5 0.6 divide_convert_fusion
  265.1 1.9 copy.22
  266.9 0.0 copy-start.2
  266.9 2.5 copy.23
  269.4 0.0 copy-done.2
  269.4 0.7 copy.24
  (7 shorter events, 0.1 us)
Async XLA Ops:
  0.6 5.8 %copy-start = (bf16[1,3,12,128,128]{4,3,2,1,0:T(8,128)(2,1)S(1)}, bf16[1,3,12,128,128]{4,3,2,1,0:T(8,128)(2,1)}, u32[]{:S(2)}) copy-start(bf16[1,3,12,128,128]{4,3,2,1,0:T(8,128)(2,1)} %param.12) | copy-start | bytes 3538948
  0.6 6.6 %copy-start.1 = (f32[1,3,12,16,128]{4,3,2,1,0:T(8,128)S(1)}, f32[1,3,12,16,128]{4,3,2,1,0:T(8,128)}, u32[]{:S(2)}) copy-start(f32[1,3,12,16,128]{4,3,2,1,0:T(8,128)} %param.14) | copy-start | bytes 884740
  188.3 75.3 %copy-start.3 = (s32[128,6]{0,1:T(8,128)S(1)}, s32[128,6]{0,1:T(8,128)}, u32[]{:S(2)}) copy-start(s32[128,6]{0,1:T(8,128)} %param.10) | copy-start | bytes 9220
  188.3 76.2 %copy-start.4 = (bf16[128,6]{0,1:T(8,128)(2,1)S(1)}, bf16[128,6]{0,1:T(8,128)(2,1)}, u32[]{:S(2)}) copy-start(bf16[128,6]{0,1:T(8,128)(2,1)} %param.11) | copy-start | bytes 4612
  266.9 2.5 copy-start.2

commit v6 on v5

--- a/solution.py
+++ b/solution.py
@@ -115,7 +115,7 @@
                 pl.BlockSpec((nm, nb, BLK, BLK), lambda i, lay, place: (0, 0, 0, 0)),
             ],
             out_specs=[
-                pl.BlockSpec((2 * nq, tile, width // 2), lambda i, lay, place: (0, i, 0)),
+                pl.BlockSpec((nq * width // 256, tile, 256), lambda i, lay, place: (0, i, 0)),
                 pl.BlockSpec((tile, BLK), lambda i, lay, place: (i, 0)),
                 pl.BlockSpec((NY, nm * nb, BLK // NY, BLK), lambda i, lay, place: (0, 0, 0, 0)),
             ],
@@ -131,7 +131,7 @@
             ],
         ),
         out_shape=[
-            jax.ShapeDtypeStruct((2 * nq, rows, width // 2), bf16),
+            jax.ShapeDtypeStruct((nq * width // 256, rows, 256), bf16),
             jax.ShapeDtypeStruct((rows, BLK), bf16),
             jax.ShapeDtypeStruct((NY, nm * nb, BLK // NY, BLK), bf16),
         ],
@@ -196,12 +196,9 @@
 
 
 class Exchange:
-    far = NX // 2
-
-    def __init__(self, place, src, dst, relay, own_sem, send_sem, recv_sem, relay_send, relay_recv):
-        self.place, self.src, self.dst, self.relay = place, src, dst, relay
+    def __init__(self, place, src, dst, own_sem, send_sem, recv_sem):
+        self.place, self.src, self.dst = place, src, dst
         self.own_sem, self.send_sem, self.recv_sem = own_sem, send_sem, recv_sem
-        self.relay_send, self.relay_recv = relay_send, relay_recv
 
     def direct(self, q, dx, core):
         number = dx * NCORE + core
@@ -214,26 +211,6 @@
             self.place.across(dx, core),
         )
 
-    def first_leg(self, q, way):
-        number = self.far * NCORE + way
-        return send(
-            self.src.at[q, span(number, ROWS)],
-            self.relay.at[q, way],
-            self.send_sem.at[q, number],
-            self.relay_recv.at[q, way],
-            self.place.across(1 if way == 0 else NX - 1, self.place.core),
-        )
-
-    def second_leg(self, q, way):
-        landing = self.far * NCORE + self.place.core
-        return send(
-            self.relay.at[q, way],
-            self.dst.at[q, span(landing, ROWS)],
-            self.relay_send.at[q, way],
-            self.recv_sem.at[q, landing],
-            self.place.across(1 if way == 0 else NX - 1, way),
-        )
-
     def own(self, q):
         rows = span(self.place.core, ROWS)
         return pltpu.make_async_copy(self.src.at[q, rows], self.dst.at[q, rows], self.own_sem.at[q])
@@ -243,17 +220,9 @@
             if dx == 0:
                 self.direct(q, 0, 1 - self.place.core).start()
                 self.own(q).start()
-            elif dx == self.far and self.relay is not None:
-                for way in range(2):
-                    self.first_leg(q, way).start()
             else:
                 for core in range(NCORE):
                     self.direct(q, dx, core).start()
-
-    def forward(self, q):
-        for way in range(2):
-            self.first_leg(q, way).wait_recv()
-            self.second_leg(q, way).start()
 
     def arrive(self, q):
         def one(landing):
@@ -269,11 +238,7 @@
     def leave(self, q):
         for dx in range(1, NX):
             for core in range(NCORE):
-                if dx == self.far and self.relay is not None:
-                    self.first_leg(q, core).wait_send()
-                    self.second_leg(q, core).wait_send()
-                else:
-                    self.direct(q, dx, core).wait_send()
+                self.direct(q, dx, core).wait_send()
         self.direct(q, 0, 1 - self.place.core).wait_send()
 
 
@@ -387,19 +352,18 @@
 
 
 def dispatch_kernel(
-    tok, og, meta, state, late_state, partner, xs, chosen, blocks, own_rows, moment, lay, ring, picked, choose, turned, notes, relay,
-    held_0, held_1, held_2, held_3, held_4, late_0, late_1, late_2, late_3, late_4,
-    own_sem, notes_send, notes_recv, ring_send, ring_recv, out_own, out_send, out_recv, relay_send, relay_recv, keep_sem,
-    move_own, move_send, move_recv, share_send, share_recv, late_own, late_send, late_recv,
+    tok, og, meta, state, partner, xs, chosen, blocks, own_rows, lay, ring, picked, choose, turned, notes,
+    held_0, held_1, held_2, held_3, held_4,
+    own_sem, notes_send, notes_recv, ring_send, ring_recv, out_own, out_send, out_recv, keep_sem,
+    move_own, move_send, move_recv, share_send, share_recv,
 ):
     count = tok.shape[0]
     chunks, _, width = ring.shape
     half = chunks // 2
     place = Place()
     z = place.z
-    out = Exchange(place, picked, xs, relay, out_own, out_send, out_recv, relay_send, relay_recv)
+    out = Exchange(place, picked, xs, out_own, out_send, out_recv)
     move = Move(place, state, partner, (held_0, held_1, held_2, held_3, held_4), move_own, move_send, move_recv)
-    late = Move(place, late_state, partner, (late_0, late_1, late_2, late_3, late_4), late_own, late_send, late_recv)
     share = Share(place, blocks, share_send, share_recv)
 
     def own_copy(q):
@@ -420,32 +384,6 @@
         return send(
             meta.at[(z + k) % NZ], notes.at[source], notes_send.at[k], notes_recv.at[k], place.along(k)
         )
-
-    for k in range(1, NZ):
-        note(k, z).start()
-    for q in range(chunks):
-        own_copy(q).wait()
-    own_notes.wait()
-    move.start(0)
-
-    def unpack():
-        n = blocks.shape[0]
-
-        def one(b, carry):
-            rows = move.tile(b)
-            own_rows[b] = rows
-            blocks[b, span(place.y, BLK // NY), :] = rows
-            return carry
-
-        lax.fori_loop(0, n, one, 0)
-        lay[...] = move.tile(n)
-
-    def unpack_late():
-        def one(b, carry):
-            moment[b] = late.tile(b)
-            return carry
-
-        lax.fori_loop(0, moment.shape[0], one, 0)
 
     def hop(q, way, step, arriving):
         rows = count
@@ -466,6 +404,29 @@
             place.along(1 if way == 0 else NZ - 1),
         )
 
+    for k in range(1, NZ):
+        note(k, z).start()
+    for q in range(chunks):
+        own_copy(q).wait()
+    own_notes.wait()
+    for way in range(2):
+        hop(0, way, 0, False).start()
+    move.start(0)
+    for way in range(2):
+        hop(1, way, 0, False).start()
+
+    def unpack():
+        n = blocks.shape[0]
+
+        def one(b, carry):
+            rows = move.tile(b)
+            own_rows[b] = rows
+            blocks[b, span(place.y, BLK // NY), :] = rows
+            return carry
+
+        lax.fori_loop(0, n, one, 0)
+        lay[...] = move.tile(n)
+
     def keep():
         return pltpu.make_async_copy(turned, chosen, keep_sem.at[0])
 
@@ -497,7 +458,7 @@
 
     def step(i, carry):
         for s in range(NZ // 2):
-            q = i - s
+            q = i - s if s else i + 2
 
             @pl.when((q >= 0) & (q < chunks))
             def _():
@@ -520,27 +481,23 @@
                 picked[q, rows, :] = dot(choose[q // half, rows, :], ring[q]).astype(jnp.bfloat16)
                 out.start(q, (2, 3) if h else (1, 0))
 
-        @pl.when((i > NZ // 2) & (i <= NZ // 2 + chunks))
-        def _():
-            out.forward(i - NZ // 2 - 1)
-
-        @pl.when(i == 1)
+        @pl.when(i == 3)
         def _():
             move.arrive(0)
             move.start(1)
 
-        @pl.when(i == 2)
+        @pl.when(i == 5)
         def _():
             move.arrive(1)
             move.order()
             move.start(2)
 
-        @pl.when(i == 4)
+        @pl.when(i == 8)
         def _():
             move.arrive(2)
             move.start(3)
 
-        @pl.when(i == 5)
+        @pl.when(i == 10)
         def _():
             move.arrive(3)
             unpack()
@@ -548,38 +505,13 @@
 
         for s in range(1, NY // 2 + 1):
 
-            @pl.when(i == 5 + s)
+            @pl.when(i == 10 + s)
             def _():
                 share.advance(s)
 
-        @pl.when(i == chunks)
-        def _():
-            late.start(0)
-
-        @pl.when(i == chunks + 1)
-        def _():
-            late.arrive(0)
-            late.start(1)
-
-        @pl.when(i == chunks + 2)
-        def _():
-            late.arrive(1)
-            late.order()
-            late.start(2)
-
-        @pl.when(i == chunks + 3)
-        def _():
-            late.arrive(2)
-            late.start(3)
-
-        @pl.when(i == chunks + 4)
-        def _():
-            late.arrive(3)
-            unpack_late()
-
         return carry
 
-    lax.fori_loop(0, chunks + NZ // 2 + 1, step, 0)
+    lax.fori_loop(0, chunks + NZ // 2, step, 0)
 
     def finish(q, carry):
         for way in range(2):
@@ -594,11 +526,10 @@
         note(k, z).wait_send()
     keep().wait()
     move.leave()
-    late.leave()
     share.leave()
 
 
-def dispatch(tokens, grads, meta, state, late_state, partner, tiles, chunks):
+def dispatch(tokens, grads, meta, state, partner, tiles, chunks):
     count, features = tokens.shape
     width = 2 * features // chunks
     bf16 = jnp.bfloat16
@@ -607,13 +538,12 @@
     anywhere = pl.BlockSpec(memory_space=pl.ANY)
     return pl.pallas_call(
         dispatch_kernel,
-        in_specs=[anywhere] * 5 + [pl.BlockSpec(memory_space=pltpu.SMEM)],
-        out_specs=[anywhere, anywhere] + [pl.BlockSpec(memory_space=pltpu.VMEM)] * 4,
+        in_specs=[anywhere] * 4 + [pl.BlockSpec(memory_space=pltpu.SMEM)],
+        out_specs=[anywhere, anywhere] + [pl.BlockSpec(memory_space=pltpu.VMEM)] * 3,
         out_shape=[
             jax.ShapeDtypeStruct((chunks, slots, width), bf16),
             jax.ShapeDtypeStruct((NZ * count, slots), bf16),
             jax.ShapeDtypeStruct((tiles, BLK, BLK), bf16),
-            jax.ShapeDtypeStruct((tiles, BLK // NY, BLK), bf16),
             jax.ShapeDtypeStruct((tiles, BLK // NY, BLK), bf16),
             jax.ShapeDtypeStruct((BLK // NY, BLK), bf16),
         ],
@@ -623,8 +553,7 @@
             pltpu.VMEM((2, slots, NZ * count), bf16),
             pltpu.VMEM((NZ * count, slots), bf16),
             pltpu.VMEM(meta.shape, bf16),
-            pltpu.VMEM((chunks, 2, ROWS, width), bf16),
-            *[pltpu.VMEM(state.shape, bf16)] * 10,
+            *[pltpu.VMEM(state.shape, bf16)] * 5,
             dma((chunks,)),
             dma((NZ,)),
             dma((NZ,)),
@@ -633,17 +562,12 @@
             dma((chunks,)),
             dma((chunks, PLANE)),
             dma((chunks, PLANE)),
-            dma((chunks, 2)),
-            dma((chunks, 2)),
             dma((2,)),
             dma((4,)),
             dma((4, NZ)),
             dma((4, NZ)),
             dma((2, NY // 2)),
             dma((2, NY // 2)),
-            dma((4,)),
-            dma((4, NZ)),
-            dma((4, NZ)),
         ],
         compiler_params=pltpu.CompilerParams(
             collective_id=0, has_side_effects=True, vmem_limit_bytes=56 << 20
@@ -651,27 +575,31 @@
         cost_estimate=pl.CostEstimate(
             flops=2 * slots * NZ * count * 2 * features, bytes_accessed=300 << 20, transcendentals=0
         ),
-    )(tokens, grads, meta, state, late_state, partner)
+    )(tokens, grads, meta, state, partner)
 
 
 def return_kernel(
-    pg, sc, choose, wg, own_blocks, old_moment, tg, score, moment, blocks,
-    back, marks, relay, part, leaving, landed, sums, grads,
-    x_own, x_send, x_recv, relay_send, relay_recv, mark_own, mark_send, mark_recv,
+    pg, sc, choose, wg, own_blocks, late_state, partner, tg, score, moment, blocks,
+    back, marks, part, leaving, landed, sums, grads, held_0, held_1, held_2, held_3, held_4,
+    x_own, x_send, x_recv, mark_own, mark_send, mark_recv,
     z_send, z_recv, sum_send, sum_recv, y_send, y_recv, share_send, share_recv,
+    move_own, move_send, move_recv,
 ):
     chunks, slots, width = pg.shape
     count = tg.shape[0]
     last = NZ // 2 - 1
     place = Place()
     z, y = place.z, place.y
-    cross = Exchange(place, pg, back, relay, x_own, x_send, x_recv, relay_send, relay_recv)
-    mark = Exchange(place, sc, marks, None, mark_own, mark_send, mark_recv, None, None)
+    cross = Exchange(place, pg, back, x_own, x_send, x_recv)
+    mark = Exchange(place, sc, marks, mark_own, mark_send, mark_recv)
+
+    move = Move(place, late_state, partner, (held_0, held_1, held_2, held_3, held_4), move_own, move_send, move_recv)
 
     own_grads = pltpu.make_async_copy(wg.at[y], grads.at[y], y_send.at[0])
     own_grads.start()
     place.meet(True)
     cross.start(0)
+    move.start(0)
 
     def grad(k, landing):
         return send(wg.at[(y + k) % NY], grads.at[landing], y_send.at[k], y_recv.at[k], place.over(k))
@@ -679,20 +607,19 @@
     for k in range(1, NY):
         grad(k, y).start()
     cross.start(1)
-    cross.forward(0)
     cross.start(2)
     mark.start(0)
-    cross.forward(1)
 
     share = Share(place, blocks, share_send, share_recv)
 
     def update():
+        move.arrive(3)
         for k in range(1, NY):
             grad(k, (y + NY - k) % NY).wait_recv()
         own_grads.wait()
 
         def one(b, carry):
-            total = DECAY * old_moment[b].astype(jnp.float32)
+            total = DECAY * move.tile(b).astype(jnp.float32)
             for source in range(NY):
                 total = total + grads[source, b].astype(jnp.float32)
             moment[b] = total
@@ -779,14 +706,26 @@
         def _():
             cross.start(i + 3)
 
-        @pl.when(i + 2 < chunks)
-        def _():
-            cross.forward(i + 2)
-
-        pl.when(i == 5)(update)
+        @pl.when(i == 1)
+        def _():
+            move.arrive(0)
+            move.start(1)
+
+        @pl.when(i == 3)
+        def _():
+            move.arrive(1)
+            move.order()
+            move.start(2)
+
+        @pl.when(i == 5)
+        def _():
+            move.arrive(2)
+            move.start(3)
+
+        pl.when(i == 7)(update)
         for s in range(1, NY // 2 + 1):
 
-            @pl.when(i == 5 + s)
+            @pl.when(i == 7 + s)
             def _():
                 share.advance(s)
 
@@ -821,9 +760,10 @@
     for k in range(1, NY):
         grad(k, y).wait_send()
     share.leave()
-
-
-def give_back(pg, sc, choose, wg, own_blocks, old_moment, count):
+    move.leave()
+
+
+def give_back(pg, sc, choose, wg, own_blocks, late_state, partner, count):
     chunks, slots, width = pg.shape
     f32, bf16 = jnp.float32, jnp.bfloat16
     dma = pltpu.SemaphoreType.DMA
@@ -831,28 +771,26 @@
     vmem = pl.BlockSpec(memory_space=pltpu.VMEM)
     return pl.pallas_call(
         return_kernel,
-        in_specs=[anywhere, anywhere, vmem, anywhere, vmem, vmem],
+        in_specs=[anywhere, anywhere, vmem, anywhere, vmem, anywhere, pl.BlockSpec(memory_space=pltpu.SMEM)],
         out_specs=[vmem, anywhere, vmem, vmem],
         out_shape=[
             jax.ShapeDtypeStruct((count, chunks * width), bf16),
             jax.ShapeDtypeStruct((NZ, PLANE, count), f32),
-            jax.ShapeDtypeStruct(old_moment.shape, f32),
+            jax.ShapeDtypeStruct(own_blocks.shape, f32),
             jax.ShapeDtypeStruct((wg.shape[1], BLK, BLK), bf16),
         ],
         scratch_shapes=[
             pltpu.VMEM((chunks, slots, width), bf16),
             pltpu.VMEM(sc.shape, bf16),
-            pltpu.VMEM((chunks, 2, ROWS, width), bf16),
             pltpu.VMEM((chunks, NZ * count, width), f32),
             pltpu.VMEM((chunks, 2, NZ // 2, count, width), bf16),
             pltpu.VMEM((chunks, 2, NZ // 2, count, width), bf16),
             pltpu.VMEM((NZ, PLANE, count), f32),
             pltpu.VMEM(wg.shape, bf16),
+            *[pltpu.VMEM(late_state.shape, bf16)] * 5,
             dma((chunks,)),
             dma((chunks, PLANE)),
             dma((chunks, PLANE)),
-            dma((chunks, 2)),
-            dma((chunks, 2)),
             dma((1,)),
             dma((1, PLANE)),
             dma((1, PLANE)),
@@ -864,6 +802,9 @@
             dma((NY,)),
             dma((2, NY // 2)),
             dma((2, NY // 2)),
+            dma((4,)),
+            dma((4, NZ)),
+            dma((4, NZ)),
         ],
         compiler_params=pltpu.CompilerParams(
             collective_id=1, has_side_effects=True, vmem_limit_bytes=56 << 20
@@ -871,7 +812,7 @@
         cost_estimate=pl.CostEstimate(
             flops=2 * slots * NZ * count * chunks * width, bytes_accessed=150 << 20, transcendentals=0
         ),
-    )(pg, sc, choose, wg, own_blocks, old_moment)
+    )(pg, sc, choose, wg, own_blocks, late_state, partner)
 
 
 def pieces(*parts):
@@ -906,15 +847,15 @@
     meta = jnp.concatenate(
         [slot.reshape(NZ, PLANE, count), weight.reshape(NZ, PLANE, count)], axis=1
     ).astype(bf16)
-    xs, choose, mats, own, old_moment, lay = dispatch(
-        tokens, out_grad, meta, state, late_state, partner, tiles, 8
+    xs, choose, mats, own, lay = dispatch(
+        tokens, out_grad, meta, state, partner, tiles, 16
     )
     layout_one = lay.reshape(-1)[: layout[0].size].astype(jnp.int32).reshape(layout[0].shape)
     pg, sc, wg = expert_compute(
         layout_one, place.core.reshape(1), xs, mats.reshape(blocks[0].shape), 448
     )
     token_grad, score, moment, updated = give_back(
-        pg, sc[None], choose, wg, own, old_moment, count
+        pg, sc[None], choose, wg, own, late_state, partner, count
     )
     score = jnp.sum(jnp.where(picks, score.reshape(n, count)[:, :, None], 0.0), axis=0)
     route_grad = (score / route_weights.astype(f32)).astype(bf16)

time: 272 us -> 267 us (0.982)
  Pallas kernels: 254 us -> 250 us
    pallas_call x1, Pallas kernels: 153 us -> 139 us  [dispatch(): pl.pallas_call(dispatch_kernel, in_specs=[anywhere] * 4 + [pl.BlockSpec(m...]
    pallas_call x1, Pallas kernels: 75.3 us -> 85.4 us  [give_back(): pl.pallas_call(return_kernel, in_specs=[anywhere, anywhere, vmem, anywher...]
where the time goes in v6:
time: 267 us; the launch traced here: 266 us
  Pallas kernels  250 us (94%)
  local copies, waits for them, and re-layouts  8.37 us (3%)
  other arithmetic  6.61 us (2%)
    pallas_call x1, Pallas kernels, dispatch(): pl.pallas_call(dispatch_kernel, in_specs=[anywhere] * 4 + [pl.BlockSpec(m...  139 us
    pallas_call x1, Pallas kernels, give_back(): pl.pallas_call(return_kernel, in_specs=[anywhere, anywhere, vmem, anywher...  85.4 us
    pallas_call x1, Pallas kernels, expert_compute(): pl.pallas_call(expert_kernel, grid_spec=pltpu.PrefetchScalarGridSpec(num_...  26.2 us

profile of v6, /device:TPU:1, one launch (start us, length us, event | category | flops | bytes accessed | tf_op | source)
XLA Modules:
  0.0 266.3 jit_solution(7299345934433457445)
XLA Ops:
  0.6 0.0 copy-start
  0.7 1.5 gather_fusion
  2.2 0.8 compare_reduce_fusion
  3.0 0.2 fusion.2
  3.2 0.7 convert_element_type.39
  3.9 0.8 fusion.3
  4.7 0.6 pad_maximum_fusion.meta
  5.3 0.0 copy-done
  5.4 0.7 convert.16
  6.1 0.1 copy.18
  6.2 0.1 reshape_squeeze.5
  6.3 0.1 pad.9.clone
  6.4 0.8 maximum_maximum_fusion
  7.2 138.7 %shard_map.111 = (bf16[16,896,256]{2,1,0:T(8,128)(2,1)}, bf16[1024,896]{1,0:T(8,128)(2,1)}, bf16[36,128,128]{2,1,0:T(8,128)(2,1)}, bf16[36,16,128]{2,1,0:T(8,128)(2,1)}, bf16[16,128]{1,0:T(8,128)(2,1)}) custom-call(bf16[128,2048]{1,0:T(8,128)(2,1)} %tok.1, bf16[128,2048]{1,0:T(8,128)(2,1)} %og.1, bf16[8,16,128]{2,1,0:T(8,128)(2,1)} %pad_maximum_fusion.meta, ...), custom_call_target="tpu_custom_call" | custom-call | flops 7516192768 | bytes 314572800 | tf_op jit(solution)/shard_map/pallas_call | solution.py:539
  145.9 0.7 slice_convert_fusion
  146.6 0.7 reshape.239.lay
  147.3 0.0 copy-start.1
  147.3 26.2 %shard_map.112 = (bf16[8,896,256]{2,1,0:T(8,128)(2,1)}, bf16[896,128]{1,0:T(8,128)(2,1)}, bf16[8,36,16,128]{3,2,1,0:T(8,128)(2,1)}) custom-call(s32[3,12,2]{2,1,0:T(8,128)} %reshape.239.lay, s32[1]{0:T(128)} %bitcast.7.place_ref, bf16[16,896,256]{2,1,0:T(8,128)(2,1)} %get-tuple-element.17.x_ref.s_ref, bf16[16,896,256]{2,1,0:T(8,128)(2,1)} %get-tuple-element.17.x_ref.s_ref, ...), custom_call_target="tpu_custom_call" | custom-call | flops 2818572288 | bytes 14548992 | tf_op jit(solution)/shard_map/pallas_call | solution.py:107
  173.6 0.0 copy-done.1
  173.6 0.7 concatenate.12
  174.3 0.0 copy-start.3
  174.3 0.0 copy-start.4
  174.3 85.4 %shard_map.113 = (bf16[128,2048]{1,0:T(8,128)(2,1)}, f32[8,8,128]{2,1,0:T(8,128)}, f32[36,16,128]{2,1,0:T(8,128)}, bf16[36,128,128]{2,1,0:T(8,128)(2,1)}) custom-call(bf16[8,896,256]{2,1,0:T(8,128)(2,1)} %get-tuple-element.19.pg, bf16[1,896,128]{2,1,0:T(8,128)(2,1)} %bitcast.30, bf16[1024,896]{1,0:T(8,128)(2,1)} %get-tuple-element.21.choose, ...), custom_call_target="tpu_custom_call" | custom-call | flops 3758096384 | bytes 157286400 | tf_op jit(solution)/shard_map/pallas_call | solution.py:772
  259.8 0.0 copy-done.3
  259.8 0.9 fusion.4
  260.7 0.0 copy-done.4
  260.7 0.6 divide_convert_fusion
  261.3 1.9 copy.22
  263.1 0.0 copy-start.2
  263.1 2.5 copy.23
  265.6 0.0 copy-done.2
  265.6 0.7 copy.24
  (7 shorter events, 0.1 us)
Async XLA Ops:
  0.6 4.7 %copy-start = (bf16[1,3,12,128,128]{4,3,2,1,0:T(8,128)(2,1)S(1)}, bf16[1,3,12,128,128]{4,3,2,1,0:T(8,128)(2,1)}, u32[]{:S(2)}) copy-start(bf16[1,3,12,128,128]{4,3,2,1,0:T(8,128)(2,1)} %param.12) | copy-start | bytes 3538948
  147.3 26.2 %copy-start.1 = (f32[1,3,12,16,128]{4,3,2,1,0:T(8,128)S(1)}, f32[1,3,12,16,128]{4,3,2,1,0:T(8,128)}, u32[]{:S(2)}) copy-start(f32[1,3,12,16,128]{4,3,2,1,0:T(8,128)} %param.14) | copy-start | bytes 884740
  174.3 85.5 %copy-start.3 = (s32[128,6]{0,1:T(8,128)S(1)}, s32[128,6]{0,1:T(8,128)}, u32[]{:S(2)}) copy-start(s32[128,6]{0,1:T(8,128)} %param.10) | copy-start | bytes 9220
  174.3 86.3 %copy-start.4 = (bf16[128,6]{0,1:T(8,128)(2,1)S(1)}, bf16[128,6]{0,1:T(8,128)(2,1)}, u32[]{:S(2)}) copy-start(bf16[128,6]{0,1:T(8,128)(2,1)} %param.11) | copy-start | bytes 4612
  263.1 2.5 copy-start.2
